TPU v7x, 32 devices: a whole 2x2x4 slice. The times are simulated.
32 devices in a mesh: blk: 8 (over y, x, core), req: 4 (over z).
Axes of the slice: x: 2, y: 2, z: 4, core: 2. Of those that a mesh axis runs over, the one named last changes fastest.
Arguments:
- verified_queries: bfloat16 [4, 16, 5, 1024], P('req', 'blk'), may hold values from -96 to 96
- new_keys: bfloat16 [4, 16, 5, 256], P('req', 'blk'), may hold values from -6 to 6
- verified_value_rows: bfloat16 [4, 16, 5, 256], P('req', 'blk'), may hold values from -6 to 6
- prior_round_keys: bfloat16 [4, 16, 5, 256], P('req', 'blk'), may hold values from -6 to 6
- prior_round_values: bfloat16 [4, 16, 5, 256], P('req', 'blk'), may hold values from -6 to 6
- accepted: int32 [4, 16], P('req', 'blk'), may hold values from 0 to 5
- group_id: int32 [4, 16], P('req'), may hold values from 0 to 15
- cache_len: int32 [4, 16], P('req'), may hold values from 0 to 8192, as said below
- slot_owner: int32 [4, 64], P('req'), may hold values from 0 to 15, as said below
- piece_cache_keys: bfloat16 [4, 64, 256, 256], P('req', 'blk'), may hold values from -6 to 6
- piece_cache_values: bfloat16 [4, 64, 256, 256], P('req', 'blk'), may hold values from -6 to 6
- shared_prompt_keys: bfloat16 [16, 256, 256], P('req', 'blk'), may hold values from -6 to 6
- shared_prompt_values: bfloat16 [16, 256, 256], P('req', 'blk'), may hold values from -6 to 6
- prompt_mask: int32 [16, 8], P('req', 'blk'), may hold values 0 or 1
Outputs:
- attended: bfloat16 [4, 16, 5, 1024], P('req', 'blk')
Inputs may be any that keep to these rules, and one draw needn't show every extreme that they name: `slot_owner`: A request's cache is the concatenation, in piece order, of the pieces that name it. In every batch one request owns exactly 32 pieces and no request owns more. `cache_len`: A request's length is at most 256 times the number of pieces it owns and more than 256 times one fewer; in every batch one request holds exactly 8192 rows.
All inputs are finite; a program needn't handle non-finite values. No bound on the sum of `prompt_mask` on one device may be relied on, other than what follows from the above.
Results may differ from a plain program's by a relative error of at most 0.003.
Values may be sent and summed in bfloat16 or wider, within the bound.
No kernel may reach another device: no remote copies, remote signals or barrier semaphores. Data moves between devices by JAX's collectives and lax.ppermute only.
A program may use at most 64 MiB of HBM per device.

v0:
```python
import jax
import jax.numpy as jnp
from jax import lax
from jax.sharding import PartitionSpec as P

QUERY_HEADS = 16
KEY_HEADS = 4
HEAD_SIZE = 64
VERIFIED_COUNT = 5


LOWEST = -1e30


def block_weights(scores, live_rows):
    masked = jnp.where(live_rows, scores, LOWEST)
    ceiling = jnp.max(masked, axis=-1)
    weights = jnp.where(live_rows, jnp.exp(masked - ceiling[..., None]), 0.0).astype(jnp.bfloat16)
    return (ceiling, weights, jnp.sum(weights.astype(jnp.float32), axis=-1))


def per_device(
    verified_queries,
    new_keys,
    verified_value_rows,
    prior_round_keys,
    prior_round_values,
    accepted,
    group_id,
    cache_len,
    slot_owner,
    piece_cache_keys,
    piece_cache_values,
    shared_prompt_keys,
    shared_prompt_values,
    prompt_mask,
):
    position_here = lax.axis_index("blk")
    request_rows = verified_queries.shape[1]
    rows_of_batch = group_id.shape[1]
    local_pieces = piece_cache_keys.shape[1]
    rows_of_piece = piece_cache_keys.shape[2]
    heads_per_key = QUERY_HEADS // KEY_HEADS
    score_scale = HEAD_SIZE ** (-0.5)
    row_lanes = QUERY_HEADS * VERIFIED_COUNT
    highest = lax.Precision.HIGHEST
    every_query = lax.all_gather(verified_queries, "blk", axis=1, tiled=True)[0].reshape(
        rows_of_batch, VERIFIED_COUNT, KEY_HEADS, heads_per_key, HEAD_SIZE
    )
    owners = slot_owner[0]
    requests_all = jnp.arange(rows_of_batch, dtype=jnp.int32)
    owner_table = (owners[:, None] == requests_all[None, :]).astype(jnp.int32)
    before = jnp.cumsum(owner_table, axis=0) - owner_table
    ranking = jnp.sum(before * owner_table, axis=1)
    filling = jnp.clip(cache_len[0][owners] - ranking * rows_of_piece, 0, rows_of_piece)
    my_owner = lax.dynamic_slice_in_dim(owners, position_here * local_pieces, local_pieces)
    my_fill = lax.dynamic_slice_in_dim(filling, position_here * local_pieces, local_pieces)
    slot_query = every_query[my_owner]
    keys_of_slot = piece_cache_keys[0].reshape(local_pieces, rows_of_piece, KEY_HEADS, HEAD_SIZE)
    values_of_slot = piece_cache_values[0].reshape(
        local_pieces, rows_of_piece, KEY_HEADS, HEAD_SIZE
    )
    scores = (
        jnp.einsum(
            "snkgd,sjkd->skgnj", slot_query, keys_of_slot, preferred_element_type=jnp.float32
        )
        * score_scale
    )
    live_piece = jnp.arange(rows_of_piece, dtype=jnp.int32)[None, :] < my_fill[:, None]
    live_rows = jnp.broadcast_to(live_piece[:, None, None, None, :], scores.shape)
    slot_top, slot_weights, slot_mass = block_weights(scores, live_rows)
    slot_part = jnp.einsum(
        "skgnj,sjkd->skgnd", slot_weights, values_of_slot, preferred_element_type=jnp.float32
    )
    collected_keys, collected_values, gathered_live = (
        lax.all_gather(shared_prompt_keys, "req", axis=0, tiled=True),
        lax.all_gather(shared_prompt_values, "req", axis=0, tiled=True),
        lax.all_gather(prompt_mask[:, 0].astype(jnp.bfloat16), "req", axis=0, tiled=True),
    )
    prompt_groups = group_id[0]
    keys_of_block = collected_keys[prompt_groups].reshape(rows_of_batch, -1, KEY_HEADS, HEAD_SIZE)
    values_of_block = collected_values[prompt_groups].reshape(
        rows_of_batch, -1, KEY_HEADS, HEAD_SIZE
    )
    block_live = gathered_live[prompt_groups] > 0.5
    scores = (
        jnp.einsum(
            "rnkgd,rjkd->rkgnj", every_query, keys_of_block, preferred_element_type=jnp.float32
        )
        * score_scale
    )
    live_rows = jnp.broadcast_to(block_live[:, None, None, None, None], scores.shape)
    prompt_top, prompt_weights, prompt_mass = block_weights(scores, live_rows)
    prompt_part = jnp.einsum(
        "rkgnj,rjkd->rkgnd", prompt_weights, values_of_block, preferred_element_type=jnp.float32
    )
    choose = my_owner[:, None] == requests_all[None, :]
    picked = choose.astype(jnp.float32)
    slot_flat = slot_top.reshape(local_pieces, row_lanes)
    prompt_flat = prompt_top.reshape(rows_of_batch, row_lanes)
    slot_best = jnp.max(jnp.where(choose[:, :, None], slot_flat[:, None, :], LOWEST), axis=0)
    device_top = jnp.maximum(slot_best, prompt_flat)
    overall_top = lax.pmax(device_top, "blk")
    slot_lift = jnp.exp(slot_flat - overall_top[my_owner])
    slot_terms = (
        slot_lift[..., None] * slot_part.reshape(local_pieces, row_lanes, HEAD_SIZE)
    ).reshape(local_pieces, row_lanes * HEAD_SIZE)
    prompt_lift = jnp.exp(prompt_flat - overall_top)
    numerator = jnp.dot(picked.T, slot_terms, precision=highest) + (
        prompt_lift[..., None] * prompt_part.reshape(rows_of_batch, row_lanes, HEAD_SIZE)
    ).reshape(rows_of_batch, row_lanes * HEAD_SIZE)
    denominator = jnp.dot(
        picked.T, slot_lift * slot_mass.reshape(local_pieces, row_lanes), precision=highest
    ) + prompt_lift * prompt_mass.reshape(rows_of_batch, row_lanes)
    numerator, denominator = (numerator, denominator)
    got_numerator, got_denominator = (
        lax.psum_scatter(numerator, "blk", scatter_dimension=0, tiled=True),
        lax.psum_scatter(denominator, "blk", scatter_dimension=0, tiled=True),
    )
    got_top = lax.dynamic_slice_in_dim(overall_top, position_here * request_rows, request_rows)
    request_query = verified_queries[0].reshape(
        request_rows, VERIFIED_COUNT, KEY_HEADS, heads_per_key, HEAD_SIZE
    )
    request_keys = jnp.concatenate([prior_round_keys[0], new_keys[0]], axis=1).reshape(
        request_rows, 2 * VERIFIED_COUNT, KEY_HEADS, HEAD_SIZE
    )
    request_values = jnp.concatenate(
        [prior_round_values[0], verified_value_rows[0]], axis=1
    ).reshape(request_rows, 2 * VERIFIED_COUNT, KEY_HEADS, HEAD_SIZE)
    scores = (
        jnp.einsum(
            "rnkgd,rjkd->rkgnj", request_query, request_keys, preferred_element_type=jnp.float32
        )
        * score_scale
    )
    column = jnp.arange(2 * VERIFIED_COUNT, dtype=jnp.int32)
    position = jnp.arange(VERIFIED_COUNT, dtype=jnp.int32)
    live_prev = (column[None, :] < VERIFIED_COUNT) & (column[None, :] < accepted[0][:, None])
    live_new = (column[None, :] >= VERIFIED_COUNT) & (
        column[None, :] - VERIFIED_COUNT <= position[:, None]
    )
    live_rows = live_prev[:, None, None, None, :] | live_new[None, None, None, :, :]
    own_top, own_weights, own_mass = block_weights(scores, live_rows)
    own_part = jnp.einsum(
        "rkgnj,rjkd->rkgnd", own_weights, request_values, preferred_element_type=jnp.float32
    )
    own_flat = own_top.reshape(request_rows, row_lanes)
    best_top = jnp.maximum(got_top, own_flat)
    far_lift = jnp.exp(got_top - best_top)
    near_lift = jnp.exp(own_flat - best_top)
    overall_mass = far_lift * got_denominator + near_lift * own_mass.reshape(
        request_rows, row_lanes
    )
    overall_part = far_lift[..., None] * got_numerator.reshape(
        request_rows, row_lanes, HEAD_SIZE
    ) + near_lift[..., None] * own_part.reshape(request_rows, row_lanes, HEAD_SIZE)
    attention_output = (overall_part / overall_mass[..., None]).reshape(
        request_rows, KEY_HEADS, heads_per_key, VERIFIED_COUNT, HEAD_SIZE
    )
    return (
        attention_output.transpose(0, 3, 1, 2, 4)
        .reshape(1, request_rows, VERIFIED_COUNT, QUERY_HEADS * HEAD_SIZE)
        .astype(jnp.bfloat16)
    )


def solution(mesh):
    placed = (
        P("req", "blk", None, None),
        P("req", "blk", None, None),
        P("req", "blk", None, None),
        P("req", "blk", None, None),
        P("req", "blk", None, None),
        P("req", "blk"),
        P("req", None),
        P("req", None),
        P("req", None),
        P("req", "blk", None, None),
        P("req", "blk", None, None),
        P("req", "blk", None),
        P("req", "blk", None),
        P("req", "blk"),
    )
    return jax.shard_map(
        per_device,
        mesh=mesh,
        in_specs=placed,
        out_specs=P("req", "blk", None, None),
        check_vma=False,
    )
```

profile of v0, /device:TPU:0, one launch (start us, length us, event | category | flops | bytes accessed | tf_op | source)
XLA Modules:
  0.0 155.7 jit_solution(5203253228424417421)
XLA Ops:
  6.5 0.7 copy-done.18
  7.9 0.7 copy-done.25
  8.5 0.6 copy-done.28
  10.7 13.4 %all-reduce = bf16[16]{0:T(256)(128)(2,1)S(1)} all-reduce(bf16[16]{0:T(256)(128)(2,1)S(1)} %dynamic-update-slice), channel_id=2, replica_groups=mesh['blk'=8,'req'=4] {'req'}, use_global_device_ids=true, to_apply=%add | all-reduce | flops 16 | bytes 64 | tf_op jit(solution)/shard_map/all_gather | solution.py:78
  24.3 0.7 gather_fusion.2
  25.4 0.8 gather_fusion
  26.3 9.3 %all_gather.12 = bf16[1,16,5,1024]{3,2,0,1:T(8,128)(2,1)S(1)} all-gather(bf16[1,2,5,1024]{3,2,0,1:T(8,128)(2,1)S(1)} %copy.55), channel_id=1, replica_groups=mesh['blk'=8,'req'=4] {'blk'}, dimensions={1}, use_global_device_ids=true | all-gather | bytes 184320 | tf_op jit(solution)/shard_map/all_gather | solution.py:47
  36.6 14.4 %all_gather.14 = bf16[16,32,256]{2,1,0:T(8,128)(2,1)S(1)} all-gather(bf16[4,32,256]{2,1,0:T(8,128)(2,1)S(1)} %copy-done.8), channel_id=1, replica_groups=mesh['blk'=8,'req'=4] {'req'}, dimensions={0}, use_global_device_ids=true | all-gather | bytes 327680 | tf_op jit(solution)/shard_map/all_gather | solution.py:76
  51.8 0.7 gather_fusion.1
  52.5 1.5 fusion.40
  55.5 12.2 %pmax.7 = f32[16,80]{1,0:T(8,128)S(1)} all-reduce(f32[16,80]{1,0:T(8,128)S(1)} %max.18), channel_id=1, replica_groups=mesh['blk'=8,'req'=4] {'blk'}, use_global_device_ids=true, to_apply=%region_5.6 | all-reduce | flops 1280 | bytes 10240 | tf_op jit(solution)/shard_map/pmax | solution.py:103
  67.7 0.6 subtract_exponential_fusion
  68.3 1.1 gather_fusion.4
  69.5 14.4 %all_gather.15 = bf16[16,32,256]{2,1,0:T(8,128)(2,1)S(1)} all-gather(bf16[4,32,256]{2,1,0:T(8,128)(2,1)S(1)} %copy-done.9), channel_id=1, replica_groups=mesh['blk'=8,'req'=4] {'req'}, dimensions={0}, use_global_device_ids=true | all-gather | bytes 327680 | tf_op jit(solution)/shard_map/all_gather | solution.py:77
  84.4 1.1 reshape.310
  86.1 1.7 %fusion.10 = f32[16,4,4,5,64]{4,3,2,1,0:T(8,128)S(1)} fusion(bf16[16,32,4,64,1]{3,2,1,0,4:T(4,128)(2,1)} %bitcast.77, f32[16,4,4,5,32]{4,3,2,1,0:T(8,128)S(1)} %copy-done.1, f32[16,4,4,5]{3,2,1,0:T(4,128)} %copy-done.4, pred[16]{0:T(512)(128)(4,1)S(1)} %copy-done.22), kind=kOutput, calls=%fused_computation.26 | convolution fusion | flops 5365760 | bytes 758800 | tf_op jit(solution)/shard_map/rkgnj,rjkd->rkgnd/dot_general | solution.py:94
  89.8 1.5 copy.66
  91.3 0.7 copy-done.12
  92.5 0.8 reshape.309
  93.3 2.1 %convolution_add_fusion = f32[16,5120]{1,0:T(8,128)} fusion(f32[16,5120]{1,0:T(8,128)S(1)} %mul.110, f32[16,5120]{1,0:T(8,128)S(1)} %reshape.311, f32[8,5120]{1,0:T(8,128)S(1)} %mul.107, f32[8,5120]{1,0:T(8,128)} %reshape.309, s32[8]{0:T(128)S(1)} %copy-done.20), kind=kOutput, calls=%fused_computation.6 | convolution fusion | flops 8069248 | bytes 1310752 | tf_op jit(solution)/shard_map/dot_general | solution.py:109
  95.4 0.7 copy-done.7
  96.7 0.8 convert_reduce_fusion
  98.0 0.7 copy-done.14
  98.8 0.7 copy-done.15
  99.5 0.7 copy-done.16
  100.3 0.7 copy-done.17
  101.1 0.6 copy-done.26
  103.1 12.1 %all-reduce.2 = f32[16,80]{1,0:T(8,128)S(1)} all-reduce(f32[16,80]{1,0:T(8,128)S(1)} %convolution_add_fusion.1), channel_id=4, replica_groups=mesh['blk'=8,'req'=4] {'blk'}, use_global_device_ids=true, to_apply=%region_10.11.clone | all-reduce | flops 1280 | bytes 10240
  115.2 0.6 copy-done.27
  117.4 29.5 %all-reduce.5.cloned.1.call-done = f32[16,5120]{1,0:T(8,128)} async-done(((f32[16,5120]{1,0:T(8,128)}), f32[16,5120]{1,0:T(8,128)}) %all-reduce.5.cloned.1.call-update) | async-done | bytes 327696
  146.9 0.9 constant_dynamic-slice_fusion
  148.2 0.7 convert_element_type.56
  (118 shorter events, 13.1 us)
Async XLA Ops:
  6.5 18.8 %copy-start = (s32[1,16]{1,0:T(1,128)S(1)}, s32[1,16]{1,0:T(1,128)}, u32[]{:S(2)}) copy-start(s32[1,16]{1,0:T(1,128)} %param.21) | copy-start | bytes 196
  6.5 140.3 %all-reduce.5.cloned.1.call-start = ((), (), s32[]{:S(2)}) async-start(), calls=%async_computation | async-start | bytes 655360
  6.5 0.7 copy-start.18
  7.2 0.7 copy-start.24
  7.9 16.3 %copy-start.19 = (s32[8]{0:T(128)}, s32[8]{0:T(128)S(1)}, u32[]{:S(2)}) copy-start(s32[8]{0:T(128)S(1)} %fusion.33) | copy-start | bytes 100
  7.9 0.7 copy-start.25
  8.5 0.7 copy-start.28
  24.3 0.7 copy-start.6
  24.9 27.6 %copy-start.21 = (pred[16]{0:T(512)(128)(4,1)}, pred[16]{0:T(512)(128)(4,1)S(1)}, u32[]{:S(2)}) copy-start(pred[16]{0:T(512)(128)(4,1)S(1)} %broadcast_compare_fusion) | copy-start | bytes 52
  26.3 28.4 %copy-start.11 = (pred[8,256]{1,0:T(8,128)(4,1)}, pred[8,256]{1,0:T(8,128)(4,1)S(1)}, u32[]{:S(2)}) copy-start(pred[8,256]{1,0:T(8,128)(4,1)S(1)} %iota_compare_fusion.1) | copy-start | bytes 6148
  35.7 0.8 copy-start.8
  52.5 1.6 %copy-start.3 = (bf16[1,8,256,256]{3,2,1,0:T(8,128)(2,1)S(1)}, bf16[1,8,256,256]{3,2,1,0:T(8,128)(2,1)}, u32[]{:S(2)}) copy-start(bf16[1,8,256,256]{3,2,1,0:T(8,128)(2,1)} %param.23) | copy-start | bytes 3145732
  54.0 0.7 copy-start.4
  54.7 14.8 %copy-start.9 = (bf16[4,32,256]{2,1,0:T(8,128)(2,1)S(1)}, bf16[4,32,256]{2,1,0:T(8,128)(2,1)}, u32[]{:S(2)}) copy-start(bf16[4,32,256]{2,1,0:T(8,128)(2,1)} %param.26) | copy-start | bytes 196612
  55.2 30.3 %copy-start.1 = (f32[16,4,4,5,32]{4,3,2,1,0:T(8,128)S(1)}, f32[16,4,4,5,32]{4,3,2,1,0:T(8,128)}, u32[]{:S(2)}) copy-start(f32[16,4,4,5,32]{4,3,2,1,0:T(8,128)} %get-tuple-element.9) | copy-start | bytes 491524
  85.5 0.6 copy-start.22
  87.8 0.7 copy-start.13
  88.7 0.7 copy-start.10
  91.3 0.7 copy-start.12
  92.0 1.3 copy-start.20
  92.5 3.7 %copy-start.2 = (f32[16,4,4,5,32]{4,3,2,1,0:T(8,128)S(1)}, f32[16,4,4,5,32]{4,3,2,1,0:T(8,128)}, u32[]{:S(2)}) copy-start(f32[16,4,4,5,32]{4,3,2,1,0:T(8,128)} %get-tuple-element.9) | copy-start | bytes 491524
  95.3 0.7 copy-start.7
  95.3 0.9 copy-start.5
  96.1 0.6 copy-start.23
  98.0 0.7 copy-start.14
  98.7 0.7 copy-start.15
  99.5 0.7 copy-start.16
  100.3 0.7 copy-start.17
  101.1 0.7 copy-start.26
  115.1 0.7 copy-start.27
Sparse Core Ops, SparseCore 0:
  95.5 51.3 all-reduce.4
where the time goes:
time: 156 us
  blocking collectives  75.9 us (49%)
  waiting for transfers between devices  29.5 us (19%)
  local copies, waits for them, and re-layouts  25.3 us (16%)
  between operations  15.1 us (10%)
  matrix products  7 us (4%)
  other arithmetic  2.93 us (2%)
    unnamed x2, waiting for transfers between devices  29.5 us
    unnamed x66, local copies, waits for them, and re-layouts  15 us
    all_gather x1, blocking collectives, per_device(): lax.all_gather(shared_prompt_keys, 'req', axis=0, tiled=True)  14.4 us
    all_gather x1, blocking collectives, per_device(): lax.all_gather(shared_prompt_values, 'req', axis=0, tiled=True)  14.4 us
    all_gather x1, blocking collectives, per_device(): lax.all_gather(prompt_mask[:, 0].astype(jnp.bfloat16), 'req', axis=0, til...  13.4 us
    pmax x1, blocking collectives, per_device(): overall_top = lax.pmax(device_top, 'blk')  12.2 us
    unnamed x1, blocking collectives  12.1 us
    all_gather x1, blocking collectives, per_device(): lax.all_gather(verified_queries, 'blk', axis=1, tiled=True)[0]  9.31 us
  transfers between devices with their start and end apart: 1, of which 1 were waited for; matrix products, arithmetic and copies ran while one was open for 3% of the time, Pallas kernels for 0%

commit v1 on v0

v1 whole, which is shorter than its diff:
```python
import functools

import jax
import jax.numpy as jnp
from jax import lax
from jax.experimental import pallas as pl
from jax.experimental.pallas import tpu as pltpu
from jax.sharding import PartitionSpec as P

QUERY_HEADS = 16
KEY_HEADS = 4
HEAD_SIZE = 64
GROUP = QUERY_HEADS // KEY_HEADS
POSITIONS = 8
ROWS = GROUP * POSITIONS
WIDTH = KEY_HEADS * HEAD_SIZE
MESSAGE = WIDTH + 128

LOWEST = float(jnp.bfloat16(-1e30))
DEAD_MARK = 64.0

F32 = jnp.float32
BF16 = jnp.bfloat16
VMEM_LIMIT = 48 * 1024 * 1024


def head_of_lane(shape):
    return lax.broadcasted_iota(jnp.int32, shape, len(shape) - 1) // HEAD_SIZE


def swap_halves(x):
    pieces = [pltpu.roll(x[:, i : i + 128], HEAD_SIZE, 1) for i in range(0, x.shape[1], 128)]
    return jnp.concatenate(pieces, axis=1)


def spread_queries(q):
    lanes = head_of_lane(q.shape)
    zero = jnp.zeros_like(q)
    return jnp.concatenate([jnp.where(lanes == c, q, zero) for c in range(KEY_HEADS)], axis=0)


def fold_heads(x):
    lanes = head_of_lane((ROWS, WIDTH))
    out = jnp.broadcast_to(x[:ROWS], (ROWS, WIDTH))
    for c in range(1, KEY_HEADS):
        out = jnp.where(lanes == c, x[c * ROWS : (c + 1) * ROWS], out)
    return out


def score(q, keys):
    return lax.dot_general(
        spread_queries(q), keys, (((1,), (1,)), ((), ())), preferred_element_type=F32
    )


def weigh(weights, values):
    ones = jnp.ones((values.shape[0], 128), BF16)
    mass = jnp.dot(weights, ones, preferred_element_type=F32)
    part = jnp.dot(weights, values, preferred_element_type=F32)
    return jnp.concatenate([mass, mass], axis=1), part


def attend(q, keys, values, live):
    masked = jnp.where(live, score(q, keys), LOWEST)
    top = jnp.max(masked, axis=1, keepdims=True)
    weights = jnp.exp(masked - top).astype(BF16)
    mass, part = weigh(weights, values)
    return fold_heads(top), fold_heads(mass), fold_heads(part)


def attend_two(q, keys, values, live):
    masked = jnp.where(live, score(q, keys), LOWEST)
    first = lax.broadcasted_iota(jnp.int32, masked.shape, 1) < masked.shape[1] // 2
    top_a = jnp.max(jnp.where(first, masked, LOWEST), axis=1, keepdims=True)
    top_b = jnp.max(jnp.where(first, LOWEST, masked), axis=1, keepdims=True)
    weights = jnp.exp(masked - jnp.where(first, top_a, top_b))
    both = jnp.concatenate(
        [jnp.where(first, weights, 0.0), jnp.where(first, 0.0, weights)], axis=0
    ).astype(BF16)
    mass, part = weigh(both, values)
    rows = masked.shape[0]
    return (
        (fold_heads(top_a), fold_heads(mass[:rows]), fold_heads(part[:rows])),
        (fold_heads(top_b), fold_heads(mass[rows:]), fold_heads(part[rows:])),
    )


def merge(*blocks):
    top = functools.reduce(jnp.maximum, [b[0] for b in blocks])
    lifts = [jnp.exp(b[0] - top) for b in blocks]
    mass = functools.reduce(jnp.add, [a * b[1] for a, b in zip(lifts, blocks)])
    part = functools.reduce(jnp.add, [a * b[2] for a, b in zip(lifts, blocks)])
    return top, mass, part


def pack_message(top, mass, part):
    rounded = top.astype(BF16).astype(F32)
    lift = jnp.exp(top - rounded)
    top, mass, part = rounded, mass * lift, part * lift
    lane = lax.broadcasted_iota(jnp.int32, (ROWS, 128), 1)
    first = (lane % 64) < 32
    narrow = lambda x: jnp.where(first, x[:, :128], x[:, 128:])
    top, mass = narrow(top), narrow(mass)
    high = mass.astype(BF16).astype(F32)
    place = lane % 32
    packed = jnp.where(
        place == 0, top, jnp.where(place == 1, high, jnp.where(place == 2, mass - high, 0.0))
    )
    return part, packed


def open_message(message):
    row = lax.broadcasted_iota(jnp.int32, (128, WIDTH), 0)
    head = lax.broadcasted_iota(jnp.int32, (128, WIDTH), 1) // HEAD_SIZE
    owner = ((row // 32) % 2) * 2 + row // 64
    place = row % 32
    pick_top = jnp.where((owner == head) & (place == 0), 1.0, 0.0).astype(BF16)
    pick_mass = jnp.where((owner == head) & ((place == 1) | (place == 2)), 1.0, 0.0).astype(BF16)
    packed = message[:, WIDTH:].astype(BF16)
    top = jnp.dot(packed, pick_top, preferred_element_type=F32)
    mass = jnp.dot(packed, pick_mass, preferred_element_type=F32)
    return top, mass, message[:, :WIDTH]


def start_copies(pairs, sems):
    copies = [
        pltpu.make_async_copy(source, target, sems.at[i]) for i, (source, target) in enumerate(pairs)
    ]
    for copy in copies:
        copy.start()
    return copies


def prompts_out_kernel(mask_hbm, keys_hbm, values_hbm, out_ref, mask_ref, sems):
    held, rows = keys_hbm.shape[0], keys_hbm.shape[1]
    copies = start_copies(
        [
            (mask_hbm, mask_ref),
            (keys_hbm, out_ref.at[:, pl.ds(0, rows)]),
            (values_hbm, out_ref.at[:, pl.ds(rows, rows)]),
        ],
        sems,
    )
    for copy in copies:
        copy.wait()
    at = lax.broadcasted_iota(jnp.int32, (16, 128), 0) + lax.broadcasted_iota(
        jnp.int32, (16, 128), 1
    )
    for i in range(held):
        dead = mask_ref[0, i] != 1
        keys = out_ref[i, :16, :128].astype(F32)
        out_ref[i, :16, :128] = jnp.where((at == 0) & dead, DEAD_MARK, keys).astype(BF16)


def queries_out_kernel(own_ref, sibling_ref, out_ref, pad_ref):
    count, each = own_ref.shape[1], own_ref.shape[2]
    low = lax.broadcasted_iota(jnp.int32, (POSITIONS, 128), 1) < HEAD_SIZE
    pad_ref[...] = jnp.zeros_like(pad_ref)
    for i in range(2 * each):
        source = own_ref if i < each else sibling_ref
        for n in range(count):
            pad_ref[i, n : n + 1] = source[0, n].astype(F32)[i % each : i % each + 1]
    for i in range(2 * each):
        q = pad_ref[i] * HEAD_SIZE**-0.5
        swapped = swap_halves(q)
        rows = []
        for g in range(GROUP):
            columns = []
            for c in range(0, KEY_HEADS, 2):
                halves = []
                for half in range(2):
                    tile = (GROUP * (c + half) + g) // 2
                    array = q if g % 2 == half else swapped
                    halves.append(array[:, tile * 128 : tile * 128 + 128])
                columns.append(jnp.where(low, halves[0], halves[1]))
            rows.append(jnp.concatenate(columns, axis=1))
        out_ref[i] = jnp.concatenate(rows, axis=0).astype(BF16)


def place_of(request, each, chip, core, kept):
    device = lax.div(request, each)
    distance = lax.shift_right_logical(device, 1) ^ chip
    return ((device & 1) ^ core) * kept + distance * each + lax.rem(request, each)


def own_kernel(chips, each, shifts, held, *refs):
    owner_hbm, length_hbm, accepted_hbm, group_hbm = refs[:4]
    pk_hbm, nk_hbm, pv_hbm, nv_hbm, keys_hbm, values_hbm = refs[4:10]
    query_ref, own_out, table_out, keys_out, values_out = refs[10:15]
    owner_ref, length_ref, accepted_ref, group_ref, owner_row, near, rows_ref = refs[15:22]
    small_sems, near_sems, key_sems, value_sems = refs[22:]
    pieces, rows = keys_out.shape[0], keys_out.shape[1]
    kept = chips * each
    small = start_copies(
        [
            (owner_hbm, owner_ref),
            (length_hbm, length_ref),
            (accepted_hbm, accepted_ref),
            (group_hbm, group_ref),
            (owner_hbm, owner_row),
        ],
        small_sems,
    )
    small += start_copies(
        [(x.at[0], near.at[j]) for j, x in enumerate((pk_hbm, nk_hbm, pv_hbm, nv_hbm))], near_sems
    )
    large = start_copies([(keys_hbm.at[0, i], keys_out.at[i]) for i in range(pieces)], key_sems)
    large += start_copies([(values_hbm.at[0, i], values_out.at[i]) for i in range(pieces)], value_sems)
    me = lax.axis_index("blk")
    z = lax.axis_index("req")
    chip, core = lax.shift_right_logical(me, 1), me & 1
    rows_ref[...] = jnp.zeros_like(rows_ref)
    for copy in small:
        copy.wait()

    count = near.shape[1]
    for n in range(count):
        for j in range(4):
            pair = near[j, n].astype(F32)
            for k in range(each):
                at = (j % 2) * POSITIONS + n
                rows_ref[j // 2, k, at : at + 1] = pair[k : k + 1]
    for k in range(each):
        shape = (KEY_HEADS * ROWS, 2 * POSITIONS)
        column = lax.broadcasted_iota(jnp.int32, shape, 1)
        position = lax.broadcasted_iota(jnp.int32, shape, 0) % POSITIONS
        taken = accepted_ref[0, k]
        live = ((column < POSITIONS) & (column < taken)) | (
            (column >= POSITIONS)
            & (column < POSITIONS + count)
            & (column - POSITIONS <= position)
        )
        got = attend(query_ref[k], rows_ref[0, k].astype(BF16), rows_ref[1, k].astype(BF16), live)
        for j in range(3):
            own_out[j, k] = got[j]

    owners = owner_row[...]
    slot = lax.broadcasted_iota(jnp.int32, owners.shape, 1)
    for i in range(pieces):
        index = me * pieces + i
        owner = owner_ref[0, index]
        same = jnp.where((owners == owner) & (slot < index), 1.0, 0.0)
        rank = jnp.sum(same, axis=1, keepdims=True).astype(jnp.int32)
        place = place_of(owner, each, chip, core, kept)
        table_out[i : i + 1] = jnp.full((1, 128), place, jnp.int32)
        table_out[pieces + i : pieces + i + 1] = jnp.broadcast_to(
            length_ref[0, owner] - rank * rows, (1, 128)
        )
    for i in range(kept):
        request = ((chip ^ (i // each)) * 2 + core) * each + i % each
        group = group_ref[0, request]
        shift = lax.rem(z - lax.div(group, held) + shifts, shifts)
        at = shift * held + lax.rem(group, held)
        table_out[2 * pieces + i : 2 * pieces + i + 1] = jnp.full((1, 128), at, jnp.int32)
    for copy in large:
        copy.wait()


def pieces_kernel(chips, each, *refs):
    table_ref, own_ref = refs[:2]
    query_refs = refs[2 : 2 + chips]
    keys, values, mine_out, sibling_out, queries, acc = refs[2 + chips :]
    pieces, rows = keys.shape[0], keys.shape[1]
    kept = chips * each
    for s in range(chips):
        for side in range(2):
            queries[side * kept + s * each : side * kept + (s + 1) * each] = query_refs[s][
                side * each : (side + 1) * each
            ]
    lane = lax.broadcasted_iota(jnp.int32, (1, rows), 1)
    places = [jnp.max(table_ref[i : i + 1]) for i in range(pieces)]
    got = []
    for i in range(pieces):
        filled = table_ref[pieces + i : pieces + i + 1]
        live = lane < jnp.concatenate([filled] * (rows // 128), axis=1)
        got.append(attend(queries[places[i]], keys[i], values[i], live))
    acc[0] = jnp.full_like(acc[0], LOWEST)
    acc[1] = jnp.zeros_like(acc[1])
    acc[2] = jnp.zeros_like(acc[2])
    for k in range(each):
        acc[0, k] = own_ref[0, k]
    for i in range(pieces):
        acc[0, places[i]] = jnp.maximum(acc[0, places[i]], got[i][0])
    for k in range(each):
        lift = jnp.exp(own_ref[0, k] - acc[0, k])
        acc[1, k] = own_ref[1, k] * lift
        acc[2, k] = own_ref[2, k] * lift
    for i in range(pieces):
        lift = jnp.exp(got[i][0] - acc[0, places[i]])
        acc[1, places[i]] += lift * got[i][1]
        acc[2, places[i]] += lift * got[i][2]
    mine_out[...] = acc[:, :kept]
    sibling_out[...] = acc[:, kept:]


def join_kernel(mine_ref, sibling_ref, out_ref):
    for i in range(mine_ref.shape[1]):
        joined = merge([mine_ref[j, i] for j in range(3)], [sibling_ref[j, i] for j in range(3)])
        for j in range(3):
            out_ref[j, i] = joined[j]


def prompts_kernel(chips, each, shifts, first_row, *refs):
    table_ref = refs[0]
    query_refs = refs[1 : 1 + chips]
    joined_ref = refs[1 + chips]
    block_refs = refs[2 + chips : 2 + chips + 2 * shifts]
    out_refs = refs[2 + chips + 2 * shifts :]
    held, rows = block_refs[0].shape[0], block_refs[0].shape[1] // 2
    lane = lax.broadcasted_iota(jnp.int32, (1, 2 * rows), 1)
    got = []
    for i in range(chips * each):
        at = jnp.max(table_ref[first_row + i : first_row + i + 1])
        shift, slot = lax.div(at, held), lax.rem(at, held)

        def block(side):
            out = block_refs[side * shifts][slot]
            for s in range(1, shifts):
                out = jnp.where(shift == s, block_refs[side * shifts + s][slot], out)
            return out

        mine, other = block(0), block(1)
        marks = jnp.where(lane < rows, mine[:1, :1].astype(F32), other[:1, :1].astype(F32))
        got.append(
            attend_two(
                query_refs[i // each][i % each],
                jnp.concatenate([mine[:rows], other[:rows]], axis=0),
                jnp.concatenate([mine[rows:], other[rows:]], axis=0),
                marks < 0.5 * DEAD_MARK,
            )
        )
    for i in range(chips * each):
        merged = merge([joined_ref[j, i] for j in range(3)], *got[i])
        part, packed = pack_message(*merged)
        out_refs[i // each][i % each, :, :WIDTH] = part
        out_refs[i // each][i % each, :, WIDTH:] = packed


def combine_kernel(chips, *refs):
    message_refs, out_ref = refs[:chips], refs[chips]
    count, each = out_ref.shape[1], out_ref.shape[2]
    low = lax.broadcasted_iota(jnp.int32, (POSITIONS, 128), 1) < HEAD_SIZE
    rows = []
    for k in range(each):
        parts = [open_message(ref[k]) for ref in message_refs]
        _, mass, part = merge(*parts)
        out = part / mass
        swapped = swap_halves(out)
        columns = []
        for head in range(0, QUERY_HEADS, 2):
            c, g = head // GROUP, head % GROUP
            tile = slice((c // 2) * 128, (c // 2) * 128 + 128)
            first, second = (out, swapped) if c % 2 == 0 else (swapped, out)
            columns.append(
                jnp.where(
                    low,
                    first[g * POSITIONS : (g + 1) * POSITIONS, tile],
                    second[(g + 1) * POSITIONS : (g + 2) * POSITIONS, tile],
                )
            )
        rows.append(jnp.concatenate(columns, axis=1))
    for n in range(count):
        out_ref[0, n] = jnp.concatenate([row[n : n + 1] for row in rows], axis=0).astype(BF16)


HBM = pl.BlockSpec(memory_space=pltpu.HBM)
VMEM = pl.BlockSpec(memory_space=pltpu.VMEM)


def in_hbm(x):
    return pltpu.with_memory_space_constraint(x, pltpu.HBM)


def call(kernel, name, out_shape, in_specs, scratch=(), cost=0):
    many = isinstance(out_shape, (list, tuple))
    return pl.pallas_call(
        kernel,
        name=name,
        out_shape=out_shape,
        in_specs=in_specs,
        out_specs=[VMEM] * len(out_shape) if many else VMEM,
        scratch_shapes=list(scratch),
        cost_estimate=pl.CostEstimate(flops=0, bytes_accessed=cost, transcendentals=0),
        compiler_params=pltpu.CompilerParams(vmem_limit_bytes=VMEM_LIMIT),
    )


def per_device(
    devices,
    shifts,
    verified_queries,
    new_keys,
    verified_value_rows,
    prior_round_keys,
    prior_round_values,
    accepted,
    group_id,
    cache_len,
    slot_owner,
    piece_cache_keys,
    piece_cache_values,
    shared_prompt_keys,
    shared_prompt_values,
    prompt_mask,
):
    shape = jax.ShapeDtypeStruct
    each = verified_queries.shape[1]
    chips = devices // 2
    pieces, piece_rows = piece_cache_keys.shape[1:3]
    held, block_rows = shared_prompt_keys.shape[:2]
    kept = chips * each

    def other_core(x):
        return lax.ppermute(x, "blk", [(i, i ^ 1) for i in range(devices)])

    def other_chip(x, s):
        return lax.ppermute(x, "blk", [(i, i ^ (2 * s)) for i in range(devices)])

    def along_req(x, s):
        return lax.ppermute(x, "req", [(i, (i + s) % shifts) for i in range(shifts)])

    verified_queries, prior_round_keys, new_keys, prior_round_values, verified_value_rows = (
        jnp.transpose(x, (0, 2, 1, 3))
        for x in (
            verified_queries, prior_round_keys, new_keys, prior_round_values, verified_value_rows,
        )
    )
    sibling_queries = other_core(verified_queries)
    own_blocks = call(
        prompts_out_kernel,
        "prompts_out",
        shape((held, 2 * block_rows, WIDTH), BF16),
        [HBM] * 3,
        [pltpu.SMEM((1, held), jnp.int32), pltpu.SemaphoreType.DMA((3,))],
    )(in_hbm(prompt_mask.T), in_hbm(shared_prompt_keys), in_hbm(shared_prompt_values))
    blocks = [own_blocks] + [along_req(own_blocks, s) for s in range(1, shifts)]

    sibling_queries, own_blocks = lax.optimization_barrier((sibling_queries, own_blocks))
    chip_queries = call(
        queries_out_kernel,
        "queries_out",
        shape((2 * each, ROWS, WIDTH), BF16),
        [VMEM, VMEM],
        [pltpu.VMEM((2 * each, POSITIONS, QUERY_HEADS * HEAD_SIZE), F32)],
    )(verified_queries, sibling_queries)
    queries = [chip_queries] + [other_chip(chip_queries, s) for s in range(1, chips)]

    near = (prior_round_keys, new_keys, prior_round_values, verified_value_rows)
    count = verified_queries.shape[1]
    piece_shape = (pieces, piece_rows, WIDTH)
    own, table, keys, values = call(
        functools.partial(own_kernel, chips, each, shifts, held),
        "own",
        [
            shape((3, each, ROWS, WIDTH), F32),
            shape((2 * pieces + kept, 128), jnp.int32),
            shape(piece_shape, BF16),
            shape(piece_shape, BF16),
        ],
        [HBM] * 10 + [VMEM],
        [
            pltpu.SMEM(slot_owner.shape, jnp.int32),
            pltpu.SMEM(cache_len.shape, jnp.int32),
            pltpu.SMEM(accepted.shape, jnp.int32),
            pltpu.SMEM(group_id.shape, jnp.int32),
            pltpu.VMEM(slot_owner.shape, jnp.int32),
            pltpu.VMEM((4, count, each, WIDTH), BF16),
            pltpu.VMEM((2, each, 2 * POSITIONS, WIDTH), F32),
            pltpu.SemaphoreType.DMA((5,)),
            pltpu.SemaphoreType.DMA((4,)),
            pltpu.SemaphoreType.DMA((pieces,)),
            pltpu.SemaphoreType.DMA((pieces,)),
        ],
        8 * 1024 * 1024,
    )(
        *(in_hbm(x) for x in (slot_owner, cache_len, accepted, group_id) + near),
        in_hbm(piece_cache_keys),
        in_hbm(piece_cache_values),
        chip_queries,
    )

    wide = (kept, ROWS, WIDTH)
    mine, to_sibling = call(
        functools.partial(pieces_kernel, chips, each),
        "pieces",
        [shape((3,) + wide, F32)] * 2,
        [VMEM] * (chips + 4),
        [
            pltpu.VMEM((2 * kept, ROWS, WIDTH), BF16),
            pltpu.VMEM((3, 2 * kept, ROWS, WIDTH), F32),
        ],
    )(table, own, *queries, keys, values)
    to_sibling, *blocks = lax.optimization_barrier((to_sibling, *blocks))
    joined = call(join_kernel, "join", shape((3,) + wide, F32), [VMEM, VMEM])(
        mine, other_core(to_sibling)
    )
    sibling_blocks = [other_core(x) for x in blocks]

    messages = call(
        functools.partial(prompts_kernel, chips, each, shifts, 2 * pieces),
        "prompts",
        [shape((each, ROWS, MESSAGE), F32)] * chips,
        [VMEM] * (2 + chips + 2 * shifts),
    )(table, *queries, joined, *blocks, *sibling_blocks)
    arrived = [messages[0]] + [other_chip(messages[s], s) for s in range(1, chips)]

    out = call(
        functools.partial(combine_kernel, chips),
        "combine",
        shape(verified_queries.shape, BF16),
        [VMEM] * chips,
    )(*arrived)
    return jnp.transpose(out, (0, 2, 1, 3))


def solution(mesh):
    placed = (
        P("req", "blk", None, None),
        P("req", "blk", None, None),
        P("req", "blk", None, None),
        P("req", "blk", None, None),
        P("req", "blk", None, None),
        P("req", "blk"),
        P("req", None),
        P("req", None),
        P("req", None),
        P("req", "blk", None, None),
        P("req", "blk", None, None),
        P("req", "blk", None),
        P("req", "blk", None),
        P("req", "blk"),
    )
    return jax.shard_map(
        functools.partial(per_device, mesh.shape["blk"], mesh.shape["req"]),
        mesh=mesh,
        in_specs=placed,
        out_specs=P("req", "blk", None, None),
        check_vma=False,
    )
```

time: 156 us -> 32.5 us (0.21)
  blocking collectives: 75.9 us -> 0 us
  local copies, waits for them, and re-layouts: 25.3 us -> 0.01 us
  waiting for transfers between devices: 29.5 us -> 8.12 us
  starting transfers between devices: 0.01 us -> 15.6 us
  between operations: 15.1 us -> 0.09 us
  Pallas kernels: 0 us -> 8.57 us
  matrix products: 7 us -> 0 us
  other arithmetic: 2.93 us -> 0 us
    all_gather x4 -> x0, blocking collectives: 51.5 us -> none  [the longest x1 14.4 us: per_device(): lax.all_gather(shared_prompt_keys, 'req', axis=0, tiled=True)]
    unnamed x2 -> x0, waiting for transfers between devices: 29.5 us -> none
    ppermute x0 -> x15, starting transfers between devices: none -> 15.6 us  [the longest x6 8.45 us: other_chip(): return lax.ppermute(x, 'blk', [(i, i ^ 2 * s) for i in range(devices)])]
    unnamed x66 -> x2, local copies, waits for them, and re-layouts: 15 us -> 0.01 us
    pmax x1 -> x0, blocking collectives: 12.2 us -> none  [per_device(): overall_top = lax.pmax(device_top, 'blk')]
    unnamed x1 -> x0, blocking collectives: 12.1 us -> none
    pallas_call x0 -> x7, Pallas kernels: none -> 8.57 us  [the longest x1 2.57 us: per_device(): call(functools.partial(prompts_kernel, chips, each, shifts, 2 * pieces),...]
    ppermute x0 -> x15, waiting for transfers between devices: none -> 8.12 us  [the longest x6 6.21 us: other_chip(): return lax.ppermute(x, 'blk', [(i, i ^ 2 * s) for i in range(devices)])]
  transfers between devices with their start and end apart: 1 -> 15, of which waited for: 1 -> 9; matrix products, arithmetic and copies ran while one was open for 3% -> 0% of each run, Pallas kernels for 0% -> 15%
where the time goes in v1:
time: 32.5 us; the launch traced here: 32.4 us
  starting transfers between devices  15.6 us (48%)
  Pallas kernels  8.57 us (26%)
  waiting for transfers between devices  8.12 us (25%)
    ppermute x6, starting transfers between devices, other_chip(): return lax.ppermute(x, 'blk', [(i, i ^ 2 * s) for i in range(devices)])  8.45 us
    ppermute x6, waiting for transfers between devices, other_chip(): return lax.ppermute(x, 'blk', [(i, i ^ 2 * s) for i in range(devices)])  6.21 us
    ppermute x3, starting transfers between devices, along_req(): lax.ppermute(x, 'req', [(i, (i + s) % shifts) for i in range(shifts)])  5.51 us
    pallas_call x1, Pallas kernels, per_device(): call(functools.partial(prompts_kernel, chips, each, shifts, 2 * pieces),...  2.57 us
    pallas_call x1, Pallas kernels, per_device(): call(functools.partial(own_kernel, chips, each, shifts, held), 'own', [sh...  2.24 us
    ppermute x6, waiting for transfers between devices, other_core(): return lax.ppermute(x, 'blk', [(i, i ^ 1) for i in range(devices)])  1.91 us
    ppermute x6, starting transfers between devices, other_core(): return lax.ppermute(x, 'blk', [(i, i ^ 1) for i in range(devices)])  1.61 us
    pallas_call x1, Pallas kernels, per_device(): call(functools.partial(pieces_kernel, chips, each), 'pieces', [shape((3,)...  1.59 us
  transfers between devices with their start and end apart: 15, of which 9 were waited for; matrix products, arithmetic and copies ran while one was open for 0% of the time, Pallas kernels for 15%

profile of v1, /device:TPU:0, one launch (start us, length us, event | category | flops | bytes accessed | tf_op | source)
XLA Modules:
  0.0 32.4 jit_solution(16281394195537468573)
XLA Ops:
  0.0 0.5 %collective-permute-start = (bf16[1,5,2,1024]{3,2,1,0:T(2,128)(2,1)}, bf16[1,5,2,1024]{3,2,1,0:T(2,128)(2,1)S(1)}, u32[]{:S(2)}, u32[]{:S(2)}) collective-permute-start(bf16[1,5,2,1024]{3,2,1,0:T(2,128)(2,1)} %bitcast.7), channel_id=1, source_target_pairs={{0,4},{4,0},{8,12},{12,8},{16,20},{20,16},{24,28},{28,24},{1,5},{5... | collective-permute-start | bytes 61448 | tf_op jit(solution)/shard_map/ppermute | solution.py:414
  0.5 0.9 %prompts_out.1.refs_6_ = bf16[4,64,256]{2,1,0:T(8,128)(2,1)S(1)} custom-call(s32[1,4]{1,0:T(1,128)} %bitcast.13, bf16[4,32,256]{2,1,0:T(8,128)(2,1)} %keys_hbm.1, bf16[4,32,256]{2,1,0:T(8,128)(2,1)} %values_hbm.1), custom_call_target="tpu_custom_call" | custom-call | tf_op jit(solution)/shard_map/prompts_out/pallas_call | solution.py:429
  1.4 0.1 collective-permute-done.sibling_ref
  1.5 0.1 queries_out.1.refs_10_.refs_2_.refs_1_
  1.6 2.9 %collective-permute-start.1 = (bf16[4,32,256]{2,1,0:T(8,128)(2,1)S(1)}, bf16[4,32,256]{2,1,0:T(8,128)(2,1)S(1)}, u32[]{:S(2)}, u32[]{:S(2)}) collective-permute-start(bf16[4,32,256]{2,1,0:T(8,128)(2,1)S(1)} %queries_out.1.refs_10_.refs_2_.refs_1_), channel_id=1, source_target_pairs={{0,8},{4,12},{8,0},{12,4},{16,24},{20,28},{24,16},{28,20},{1,9},{5... | collective-permute-start | bytes 196616 | tf_op jit(solution)/shard_map/ppermute | solution.py:417
  4.5 1.6 %collective-permute-start.4 = (bf16[4,64,256]{2,1,0:T(8,128)(2,1)S(1)}, bf16[4,64,256]{2,1,0:T(8,128)(2,1)S(1)}, u32[]{:S(2)}, u32[]{:S(2)}) collective-permute-start(bf16[4,64,256]{2,1,0:T(8,128)(2,1)S(1)} %prompts_out.1.refs_6_), channel_id=1, source_target_pairs={{0,1},{1,2},{2,3},{3,0},{4,5},{5,6},{6,7},{7,4},{8,9},{9,10},{10,1... | collective-permute-start | bytes 393224 | tf_op jit(solution)/shard_map/ppermute | solution.py:420
  6.1 2.6 %collective-permute-start.5 = (bf16[4,64,256]{2,1,0:T(8,128)(2,1)S(1)}, bf16[4,64,256]{2,1,0:T(8,128)(2,1)S(1)}, u32[]{:S(2)}, u32[]{:S(2)}) collective-permute-start(bf16[4,64,256]{2,1,0:T(8,128)(2,1)S(1)} %prompts_out.1.refs_6_), channel_id=1, source_target_pairs={{0,2},{1,3},{2,0},{3,1},{4,6},{5,7},{6,4},{7,5},{8,10},{9,11},{10,... | collective-permute-start | bytes 393224 | tf_op jit(solution)/shard_map/ppermute | solution.py:420
  8.7 1.3 %collective-permute-start.6 = (bf16[4,64,256]{2,1,0:T(8,128)(2,1)S(1)}, bf16[4,64,256]{2,1,0:T(8,128)(2,1)S(1)}, u32[]{:S(2)}, u32[]{:S(2)}) collective-permute-start(bf16[4,64,256]{2,1,0:T(8,128)(2,1)S(1)} %prompts_out.1.refs_6_), channel_id=1, source_target_pairs={{0,3},{1,0},{2,1},{3,2},{4,7},{5,4},{6,5},{7,6},{8,11},{9,8},{10,9... | collective-permute-start | bytes 393224 | tf_op jit(solution)/shard_map/ppermute | solution.py:420
  10.0 1.5 %collective-permute-start.2 = (bf16[4,32,256]{2,1,0:T(8,128)(2,1)S(1)}, bf16[4,32,256]{2,1,0:T(8,128)(2,1)S(1)}, u32[]{:S(2)}, u32[]{:S(2)}) collective-permute-start(bf16[4,32,256]{2,1,0:T(8,128)(2,1)S(1)} %queries_out.1.refs_10_.refs_2_.refs_1_), channel_id=1, source_target_pairs={{0,16},{4,20},{8,24},{12,28},{16,0},{20,4},{24,8},{28,12},{1,17},{... | collective-permute-start | bytes 196616 | tf_op jit(solution)/shard_map/ppermute | solution.py:417
  11.6 0.5 %collective-permute-start.3 = (bf16[4,32,256]{2,1,0:T(8,128)(2,1)S(1)}, bf16[4,32,256]{2,1,0:T(8,128)(2,1)S(1)}, u32[]{:S(2)}, u32[]{:S(2)}) collective-permute-start(bf16[4,32,256]{2,1,0:T(8,128)(2,1)S(1)} %queries_out.1.refs_10_.refs_2_.refs_1_), channel_id=1, source_target_pairs={{0,24},{4,28},{8,16},{12,20},{16,8},{20,12},{24,0},{28,4},{1,25},{... | collective-permute-start | bytes 196616 | tf_op jit(solution)/shard_map/ppermute | solution.py:417
  12.0 2.2 %own.1 = (f32[3,2,32,256]{3,2,1,0:T(8,128)S(1)}, s32[24,128]{1,0:T(8,128)S(1)}, bf16[8,256,256]{2,1,0:T(8,128)(2,1)S(1)}, bf16[8,256,256]{2,1,0:T(8,128)(2,1)S(1)}) custom-call(s32[1,64]{1,0:T(1,128)} %refs_0_.1, s32[1,16]{1,0:T(1,128)} %refs_1_.1, s32[1,2]{1,0:T(1,128)} %refs_2_.1, s32[1,16]{1,0:T(1,128)} %refs_3_.1, bf16[1,5,2,256]{3,2,1,0:T(2,128)(2,1)} %bitcast.9, ...), custom_call_target="tpu_custom_call" | custom-call | bytes 8388608 | tf_op jit(solution)/shard_map/own/pallas_call | solution.py:451
  14.3 0.7 %collective-permute-done.2.refs_4_.refs_3_ = bf16[4,32,256]{2,1,0:T(8,128)(2,1)S(1)} collective-permute-done((bf16[4,32,256]{2,1,0:T(8,128)(2,1)S(1)}, bf16[4,32,256]{2,1,0:T(8,128)(2,1)S(1)}, u32[]{:S(2)}, u32[]{:S(2)}) %collective-permute-start.2) | collective-permute-done | bytes 65568 | tf_op jit(solution)/shard_map/ppermute | solution.py:417
  15.0 1.7 %collective-permute-done.3.refs_5_.refs_4_ = bf16[4,32,256]{2,1,0:T(8,128)(2,1)S(1)} collective-permute-done((bf16[4,32,256]{2,1,0:T(8,128)(2,1)S(1)}, bf16[4,32,256]{2,1,0:T(8,128)(2,1)S(1)}, u32[]{:S(2)}, u32[]{:S(2)}) %collective-permute-start.3) | collective-permute-done | bytes 65568 | tf_op jit(solution)/shard_map/ppermute | solution.py:417
  16.7 1.6 %pieces.1 = (f32[3,8,32,256]{3,2,1,0:T(8,128)S(1)}, f32[3,8,32,256]{3,2,1,0:T(8,128)S(1)}) custom-call(s32[24,128]{1,0:T(8,128)S(1)} %get-tuple-element.22.refs_0_, f32[3,2,32,256]{3,2,1,0:T(8,128)S(1)} %get-tuple-element.23.refs_1_, bf16[4,32,256]{2,1,0:T(8,128)(2,1)S(1)} %queries_out.1.refs_10_.refs_2_.refs_1_, ...), custom_call_target="tpu_custom_call" | custom-call | tf_op jit(solution)/shard_map/pieces/pallas_call | solution.py:483
  18.4 0.1 collective-permute-start.7
  18.4 0.5 %collective-permute-start.10 = (bf16[4,64,256]{2,1,0:T(8,128)(2,1)S(1)}, bf16[4,64,256]{2,1,0:T(8,128)(2,1)S(1)}, u32[]{:S(2)}, u32[]{:S(2)}) collective-permute-start(bf16[4,64,256]{2,1,0:T(8,128)(2,1)S(1)} %collective-permute-done.5.refs_8_), channel_id=1, source_target_pairs={{0,4},{4,0},{8,12},{12,8},{16,20},{20,16},{24,28},{28,24},{1,5},{5... | collective-permute-start | bytes 393224 | tf_op jit(solution)/shard_map/ppermute | solution.py:414
  18.9 0.1 collective-permute-start.11
  19.0 0.4 %collective-permute-start.8 = (bf16[4,64,256]{2,1,0:T(8,128)(2,1)S(1)}, bf16[4,64,256]{2,1,0:T(8,128)(2,1)S(1)}, u32[]{:S(2)}, u32[]{:S(2)}) collective-permute-start(bf16[4,64,256]{2,1,0:T(8,128)(2,1)S(1)} %prompts_out.1.refs_6_), channel_id=1, source_target_pairs={{0,4},{4,0},{8,12},{12,8},{16,20},{20,16},{24,28},{28,24},{1,5},{5... | collective-permute-start | bytes 393224 | tf_op jit(solution)/shard_map/ppermute | solution.py:414
  19.4 0.1 collective-permute-start.9
  19.5 1.2 %collective-permute-done.7.sibling_ref = f32[3,8,32,256]{3,2,1,0:T(8,128)S(1)} collective-permute-done((f32[3,8,32,256]{3,2,1,0:T(8,128)S(1)}, f32[3,8,32,256]{3,2,1,0:T(8,128)S(1)}, u32[]{:S(2)}, u32[]{:S(2)}) %collective-permute-start.7) | collective-permute-done | bytes 786464 | tf_op jit(solution)/shard_map/ppermute | solution.py:414
  20.7 0.2 join.1.refs_5_
  20.9 0.0 collective-permute-done.10.refs_12_
  20.9 0.2 collective-permute-done.11.refs_13_
  21.1 0.2 collective-permute-done.8.refs_10_
  21.3 0.2 collective-permute-done.9.refs_11_
  21.5 2.6 %prompts.1 = (f32[2,32,384]{2,1,0:T(8,128)S(1)}, f32[2,32,384]{2,1,0:T(8,128)S(1)}, f32[2,32,384]{2,1,0:T(8,128)S(1)}, f32[2,32,384]{2,1,0:T(8,128)S(1)}) custom-call(s32[24,128]{1,0:T(8,128)S(1)} %get-tuple-element.22.refs_0_, bf16[4,32,256]{2,1,0:T(8,128)(2,1)S(1)} %queries_out.1.refs_10_.refs_2_.refs_1_, ...), custom_call_target="tpu_custom_call" | custom-call | tf_op jit(solution)/shard_map/prompts/pallas_call | solution.py:499
  24.0 0.6 %collective-permute-start.12 = (f32[2,32,384]{2,1,0:T(8,128)S(1)}, f32[2,32,384]{2,1,0:T(8,128)S(1)}, u32[]{:S(2)}, u32[]{:S(2)}) collective-permute-start(f32[2,32,384]{2,1,0:T(8,128)S(1)} %get-tuple-element.34), channel_id=1, source_target_pairs={{0,8},{4,12},{8,0},{12,4},{16,24},{20,28},{24,16},{28,20},{1,9},{5... | collective-permute-start | bytes 294920 | tf_op jit(solution)/shard_map/ppermute | solution.py:417
  24.6 0.5 %collective-permute-start.13 = (f32[2,32,384]{2,1,0:T(8,128)S(1)}, f32[2,32,384]{2,1,0:T(8,128)S(1)}, u32[]{:S(2)}, u32[]{:S(2)}) collective-permute-start(f32[2,32,384]{2,1,0:T(8,128)S(1)} %get-tuple-element.35), channel_id=1, source_target_pairs={{0,16},{4,20},{8,24},{12,28},{16,0},{20,4},{24,8},{28,12},{1,17},{... | collective-permute-start | bytes 294920 | tf_op jit(solution)/shard_map/ppermute | solution.py:417
  25.1 2.5 %collective-permute-start.14 = (f32[2,32,384]{2,1,0:T(8,128)S(1)}, f32[2,32,384]{2,1,0:T(8,128)S(1)}, u32[]{:S(2)}, u32[]{:S(2)}) collective-permute-start(f32[2,32,384]{2,1,0:T(8,128)S(1)} %get-tuple-element.36), channel_id=1, source_target_pairs={{0,24},{4,28},{8,16},{12,20},{16,8},{20,12},{24,0},{28,4},{1,25},{... | collective-permute-start | bytes 294920 | tf_op jit(solution)/shard_map/ppermute | solution.py:417
  27.6 2.1 %collective-permute-done.12.refs_1_ = f32[2,32,384]{2,1,0:T(8,128)S(1)} collective-permute-done((f32[2,32,384]{2,1,0:T(8,128)S(1)}, f32[2,32,384]{2,1,0:T(8,128)S(1)}, u32[]{:S(2)}, u32[]{:S(2)}) %collective-permute-start.12) | collective-permute-done | bytes 98336 | tf_op jit(solution)/shard_map/ppermute | solution.py:417
  29.7 1.7 %collective-permute-done.13.refs_2_ = f32[2,32,384]{2,1,0:T(8,128)S(1)} collective-permute-done((f32[2,32,384]{2,1,0:T(8,128)S(1)}, f32[2,32,384]{2,1,0:T(8,128)S(1)}, u32[]{:S(2)}, u32[]{:S(2)}) %collective-permute-start.13) | collective-permute-done | bytes 98336 | tf_op jit(solution)/shard_map/ppermute | solution.py:417
  31.4 1.0 %combine.1 = bf16[1,5,2,1024]{3,2,1,0:T(2,128)(2,1)} custom-call(f32[2,32,384]{2,1,0:T(8,128)S(1)} %get-tuple-element.33.refs_0_, f32[2,32,384]{2,1,0:T(8,128)S(1)} %collective-permute-done.12.refs_1_, f32[2,32,384]{2,1,0:T(8,128)S(1)} %collective-permute-done.13.refs_2_, f32[2,32,384]{2,1,0:T(8,128)S(1)} %collective-permute-done.14.refs_3_), custom_call_target="tpu_custom_call" | custom-call | tf_op jit(solution)/shard_map/combine/pallas_call | solution.py:507
  (7 shorter events, 0.0 us)
Async XLA Ops:
  0.0 1.5 %collective-permute-start = (bf16[1,5,2,1024]{3,2,1,0:T(2,128)(2,1)}, bf16[1,5,2,1024]{3,2,1,0:T(2,128)(2,1)S(1)}, u32[]{:S(2)}, u32[]{:S(2)}) collective-permute-start(bf16[1,5,2,1024]{3,2,1,0:T(2,128)(2,1)} %bitcast.7), channel_id=1, source_target_pairs={{0,4},{4,0},{8,12},{12,8},{16,20},{20,16},{24,28},{28,24},{1,5},{5... | collective-permute-start | bytes 61448 | tf_op jit(solution)/shard_map/ppermute | solution.py:414
  0.5 1.1 %copy-start = (bf16[1,2,5,1024]{3,1,2,0:T(2,128)(2,1)S(1)}, bf16[1,2,5,1024]{3,1,2,0:T(2,128)(2,1)}, u32[]{:S(2)}) copy-start(bf16[1,2,5,1024]{3,1,2,0:T(2,128)(2,1)} %param.14) | copy-start | bytes 61444
  1.6 9.9 %collective-permute-start.1 = (bf16[4,32,256]{2,1,0:T(8,128)(2,1)S(1)}, bf16[4,32,256]{2,1,0:T(8,128)(2,1)S(1)}, u32[]{:S(2)}, u32[]{:S(2)}) collective-permute-start(bf16[4,32,256]{2,1,0:T(8,128)(2,1)S(1)} %queries_out.1.refs_10_.refs_2_.refs_1_), channel_id=1, source_target_pairs={{0,8},{4,12},{8,0},{12,4},{16,24},{20,28},{24,16},{28,20},{1,9},{5... | collective-permute-start | bytes 196616 | tf_op jit(solution)/shard_map/ppermute | solution.py:417
  4.5 13.8 %collective-permute-start.4 = (bf16[4,64,256]{2,1,0:T(8,128)(2,1)S(1)}, bf16[4,64,256]{2,1,0:T(8,128)(2,1)S(1)}, u32[]{:S(2)}, u32[]{:S(2)}) collective-permute-start(bf16[4,64,256]{2,1,0:T(8,128)(2,1)S(1)} %prompts_out.1.refs_6_), channel_id=1, source_target_pairs={{0,1},{1,2},{2,3},{3,0},{4,5},{5,6},{6,7},{7,4},{8,9},{9,10},{10,1... | collective-permute-start | bytes 393224 | tf_op jit(solution)/shard_map/ppermute | solution.py:420
  6.1 12.2 %collective-permute-start.5 = (bf16[4,64,256]{2,1,0:T(8,128)(2,1)S(1)}, bf16[4,64,256]{2,1,0:T(8,128)(2,1)S(1)}, u32[]{:S(2)}, u32[]{:S(2)}) collective-permute-start(bf16[4,64,256]{2,1,0:T(8,128)(2,1)S(1)} %prompts_out.1.refs_6_), channel_id=1, source_target_pairs={{0,2},{1,3},{2,0},{3,1},{4,6},{5,7},{6,4},{7,5},{8,10},{9,11},{10,... | collective-permute-start | bytes 393224 | tf_op jit(solution)/shard_map/ppermute | solution.py:420
  8.7 9.7 %collective-permute-start.6 = (bf16[4,64,256]{2,1,0:T(8,128)(2,1)S(1)}, bf16[4,64,256]{2,1,0:T(8,128)(2,1)S(1)}, u32[]{:S(2)}, u32[]{:S(2)}) collective-permute-start(bf16[4,64,256]{2,1,0:T(8,128)(2,1)S(1)} %prompts_out.1.refs_6_), channel_id=1, source_target_pairs={{0,3},{1,0},{2,1},{3,2},{4,7},{5,4},{6,5},{7,6},{8,11},{9,8},{10,9... | collective-permute-start | bytes 393224 | tf_op jit(solution)/shard_map/ppermute | solution.py:420
  10.0 5.0 %collective-permute-start.2 = (bf16[4,32,256]{2,1,0:T(8,128)(2,1)S(1)}, bf16[4,32,256]{2,1,0:T(8,128)(2,1)S(1)}, u32[]{:S(2)}, u32[]{:S(2)}) collective-permute-start(bf16[4,32,256]{2,1,0:T(8,128)(2,1)S(1)} %queries_out.1.refs_10_.refs_2_.refs_1_), channel_id=1, source_target_pairs={{0,16},{4,20},{8,24},{12,28},{16,0},{20,4},{24,8},{28,12},{1,17},{... | collective-permute-start | bytes 196616 | tf_op jit(solution)/shard_map/ppermute | solution.py:417
  11.6 5.2 %collective-permute-start.3 = (bf16[4,32,256]{2,1,0:T(8,128)(2,1)S(1)}, bf16[4,32,256]{2,1,0:T(8,128)(2,1)S(1)}, u32[]{:S(2)}, u32[]{:S(2)}) collective-permute-start(bf16[4,32,256]{2,1,0:T(8,128)(2,1)S(1)} %queries_out.1.refs_10_.refs_2_.refs_1_), channel_id=1, source_target_pairs={{0,24},{4,28},{8,16},{12,20},{16,8},{20,12},{24,0},{28,4},{1,25},{... | collective-permute-start | bytes 196616 | tf_op jit(solution)/shard_map/ppermute | solution.py:417
  18.4 2.4 %collective-permute-start.7 = (f32[3,8,32,256]{3,2,1,0:T(8,128)S(1)}, f32[3,8,32,256]{3,2,1,0:T(8,128)S(1)}, u32[]{:S(2)}, u32[]{:S(2)}) collective-permute-start(f32[3,8,32,256]{3,2,1,0:T(8,128)S(1)} %get-tuple-element.28), channel_id=1, source_target_pairs={{0,4},{4,0},{8,12},{12,8},{16,20},{20,16},{24,28},{28,24},{1,5},{5... | collective-permute-start | bytes 2359304 | tf_op jit(solution)/shard_map/ppermute | solution.py:414
  18.4 2.5 %collective-permute-start.10 = (bf16[4,64,256]{2,1,0:T(8,128)(2,1)S(1)}, bf16[4,64,256]{2,1,0:T(8,128)(2,1)S(1)}, u32[]{:S(2)}, u32[]{:S(2)}) collective-permute-start(bf16[4,64,256]{2,1,0:T(8,128)(2,1)S(1)} %collective-permute-done.5.refs_8_), channel_id=1, source_target_pairs={{0,4},{4,0},{8,12},{12,8},{16,20},{20,16},{24,28},{28,24},{1,5},{5... | collective-permute-start | bytes 393224 | tf_op jit(solution)/shard_map/ppermute | solution.py:414
  18.9 2.1 %collective-permute-start.11 = (bf16[4,64,256]{2,1,0:T(8,128)(2,1)S(1)}, bf16[4,64,256]{2,1,0:T(8,128)(2,1)S(1)}, u32[]{:S(2)}, u32[]{:S(2)}) collective-permute-start(bf16[4,64,256]{2,1,0:T(8,128)(2,1)S(1)} %collective-permute-done.6.refs_9_), channel_id=1, source_target_pairs={{0,4},{4,0},{8,12},{12,8},{16,20},{20,16},{24,28},{28,24},{1,5},{5... | collective-permute-start | bytes 393224 | tf_op jit(solution)/shard_map/ppermute | solution.py:414
  19.0 2.3 %collective-permute-start.8 = (bf16[4,64,256]{2,1,0:T(8,128)(2,1)S(1)}, bf16[4,64,256]{2,1,0:T(8,128)(2,1)S(1)}, u32[]{:S(2)}, u32[]{:S(2)}) collective-permute-start(bf16[4,64,256]{2,1,0:T(8,128)(2,1)S(1)} %prompts_out.1.refs_6_), channel_id=1, source_target_pairs={{0,4},{4,0},{8,12},{12,8},{16,20},{20,16},{24,28},{28,24},{1,5},{5... | collective-permute-start | bytes 393224 | tf_op jit(solution)/shard_map/ppermute | solution.py:414
  19.4 2.0 %collective-permute-start.9 = (bf16[4,64,256]{2,1,0:T(8,128)(2,1)S(1)}, bf16[4,64,256]{2,1,0:T(8,128)(2,1)S(1)}, u32[]{:S(2)}, u32[]{:S(2)}) collective-permute-start(bf16[4,64,256]{2,1,0:T(8,128)(2,1)S(1)} %collective-permute-done.4.refs_7_), channel_id=1, source_target_pairs={{0,4},{4,0},{8,12},{12,8},{16,20},{20,16},{24,28},{28,24},{1,5},{5... | collective-permute-start | bytes 393224 | tf_op jit(solution)/shard_map/ppermute | solution.py:414
  24.0 5.6 %collective-permute-start.12 = (f32[2,32,384]{2,1,0:T(8,128)S(1)}, f32[2,32,384]{2,1,0:T(8,128)S(1)}, u32[]{:S(2)}, u32[]{:S(2)}) collective-permute-start(f32[2,32,384]{2,1,0:T(8,128)S(1)} %get-tuple-element.34), channel_id=1, source_target_pairs={{0,8},{4,12},{8,0},{12,4},{16,24},{20,28},{24,16},{28,20},{1,9},{5... | collective-permute-start | bytes 294920 | tf_op jit(solution)/shard_map/ppermute | solution.py:417
  24.6 6.7 %collective-permute-start.13 = (f32[2,32,384]{2,1,0:T(8,128)S(1)}, f32[2,32,384]{2,1,0:T(8,128)S(1)}, u32[]{:S(2)}, u32[]{:S(2)}) collective-permute-start(f32[2,32,384]{2,1,0:T(8,128)S(1)} %get-tuple-element.35), channel_id=1, source_target_pairs={{0,16},{4,20},{8,24},{12,28},{16,0},{20,4},{24,8},{28,12},{1,17},{... | collective-permute-start | bytes 294920 | tf_op jit(solution)/shard_map/ppermute | solution.py:417
  25.1 6.2 %collective-permute-start.14 = (f32[2,32,384]{2,1,0:T(8,128)S(1)}, f32[2,32,384]{2,1,0:T(8,128)S(1)}, u32[]{:S(2)}, u32[]{:S(2)}) collective-permute-start(f32[2,32,384]{2,1,0:T(8,128)S(1)} %get-tuple-element.36), channel_id=1, source_target_pairs={{0,24},{4,28},{8,16},{12,20},{16,8},{20,12},{24,0},{28,4},{1,25},{... | collective-permute-start | bytes 294920 | tf_op jit(solution)/shard_map/ppermute | solution.py:417

commit v2 on v1

v2 whole, which is shorter than its diff:
```python
import functools

import jax
import jax.numpy as jnp
from jax import lax
from jax.experimental import pallas as pl
from jax.experimental.pallas import tpu as pltpu
from jax.sharding import PartitionSpec as P

QUERY_HEADS = 16
KEY_HEADS = 4
HEAD_SIZE = 64
GROUP = QUERY_HEADS // KEY_HEADS
POSITIONS = 8
ROWS = GROUP * POSITIONS
WIDTH = KEY_HEADS * HEAD_SIZE
MESSAGE = 3 * POSITIONS

LOWEST = float(jnp.bfloat16(-1e30))
DEAD_MARK = 64.0

F32 = jnp.float32
BF16 = jnp.bfloat16
VMEM_LIMIT = 48 * 1024 * 1024


def head_of_lane(shape):
    return lax.broadcasted_iota(jnp.int32, shape, len(shape) - 1) // HEAD_SIZE


def swap_halves(x):
    pieces = [pltpu.roll(x[:, i : i + 128], HEAD_SIZE, 1) for i in range(0, x.shape[1], 128)]
    return jnp.concatenate(pieces, axis=1)


def spread_queries(q):
    lanes = head_of_lane(q.shape)
    zero = jnp.zeros_like(q)
    return jnp.concatenate([jnp.where(lanes == c, q, zero) for c in range(KEY_HEADS)], axis=0)


def fold_heads(x):
    lanes = head_of_lane((ROWS, WIDTH))
    out = jnp.broadcast_to(x[:ROWS], (ROWS, WIDTH))
    for c in range(1, KEY_HEADS):
        out = jnp.where(lanes == c, x[c * ROWS : (c + 1) * ROWS], out)
    return out


def score(q, keys):
    return lax.dot_general(
        spread_queries(q), keys, (((1,), (1,)), ((), ())), preferred_element_type=F32
    )


def weigh(weights, values):
    ones = jnp.ones((values.shape[0], 128), BF16)
    mass = jnp.dot(weights, ones, preferred_element_type=F32)
    part = jnp.dot(weights, values, preferred_element_type=F32)
    return jnp.concatenate([mass, mass], axis=1), part


def attend(q, keys, values, live):
    masked = jnp.where(live, score(q, keys), LOWEST)
    top = jnp.max(masked, axis=1, keepdims=True)
    weights = jnp.exp(masked - top).astype(BF16)
    mass, part = weigh(weights, values)
    return fold_heads(top), fold_heads(mass), fold_heads(part)


def attend_two(q, keys, values, live):
    masked = jnp.where(live, score(q, keys), LOWEST)
    first = lax.broadcasted_iota(jnp.int32, masked.shape, 1) < masked.shape[1] // 2
    top_a = jnp.max(jnp.where(first, masked, LOWEST), axis=1, keepdims=True)
    top_b = jnp.max(jnp.where(first, LOWEST, masked), axis=1, keepdims=True)
    weights = jnp.exp(masked - jnp.where(first, top_a, top_b))
    both = jnp.concatenate(
        [jnp.where(first, weights, 0.0), jnp.where(first, 0.0, weights)], axis=0
    ).astype(BF16)
    mass, part = weigh(both, values)
    rows = masked.shape[0]
    return (
        (fold_heads(top_a), fold_heads(mass[:rows]), fold_heads(part[:rows])),
        (fold_heads(top_b), fold_heads(mass[rows:]), fold_heads(part[rows:])),
    )


def merge(*blocks):
    top = functools.reduce(jnp.maximum, [b[0] for b in blocks])
    lifts = [jnp.exp(b[0] - top) for b in blocks]
    mass = functools.reduce(jnp.add, [a * b[1] for a, b in zip(lifts, blocks)])
    part = functools.reduce(jnp.add, [a * b[2] for a, b in zip(lifts, blocks)])
    return top, mass, part


def spot(shape):
    lane = lax.broadcasted_iota(jnp.int32, shape, 1) % HEAD_SIZE
    return lane == lax.broadcasted_iota(jnp.int32, shape, 0) % ROWS


def pack_message(top, mass, part):
    rounded = top.astype(BF16).astype(F32)
    lift = jnp.exp(top - rounded)
    mass, part = mass * lift, part * lift
    high = mass.astype(BF16).astype(F32)
    at = spot((ROWS, WIDTH))
    row_of = lambda x: jnp.sum(jnp.where(at, x, 0.0), axis=0, keepdims=True)
    sub = lax.broadcasted_iota(jnp.int32, (POSITIONS, WIDTH), 0)
    tile = lambda i: part[i * POSITIONS : (i + 1) * POSITIONS]
    return jnp.concatenate(
        [
            jnp.where(sub < 5, tile(0), pltpu.roll(tile(3), 5, 0)),
            jnp.where(sub < 5, tile(1), jnp.where(sub < 7, pltpu.roll(tile(3), 2, 0), row_of(rounded))),
            jnp.where(sub < 5, tile(2), jnp.where(sub < 6, row_of(high), row_of(mass - high))),
        ],
        axis=0,
    )


def open_messages(messages):
    at = spot((ROWS, WIDTH))
    rows = []
    for x in messages:
        for r in (15, 21, 22):
            rows.append(jnp.where(at, x[r : r + 1], 0.0).astype(BF16))
    same_head = lax.broadcasted_iota(jnp.int32, (WIDTH, WIDTH), 0) // HEAD_SIZE == (
        lax.broadcasted_iota(jnp.int32, (WIDTH, WIDTH), 1) // HEAD_SIZE
    )
    ones = jnp.where(same_head, 1.0, 0.0).astype(BF16)
    spread = jnp.dot(jnp.concatenate(rows, axis=0), ones, preferred_element_type=F32)
    sub = lax.broadcasted_iota(jnp.int32, (POSITIONS, WIDTH), 0)
    out = []
    for i, x in enumerate(messages):
        get = lambda j: spread[(3 * i + j) * ROWS : (3 * i + j + 1) * ROWS]
        last = jnp.where(sub < 3, pltpu.roll(x[0:8], 3, 0), pltpu.roll(x[8:16], 6, 0))
        out.append((get(0), get(1) + get(2), jnp.concatenate([x, last], axis=0)))
    return out


def start_copies(pairs, sems):
    copies = [
        pltpu.make_async_copy(source, target, sems.at[i]) for i, (source, target) in enumerate(pairs)
    ]
    for copy in copies:
        copy.start()
    return copies


def format_queries(q):
    low = lax.broadcasted_iota(jnp.int32, (POSITIONS, 128), 1) < HEAD_SIZE
    swapped = swap_halves(q)
    rows = []
    for g in range(GROUP):
        columns = []
        for c in range(0, KEY_HEADS, 2):
            halves = []
            for half in range(2):
                tile = (GROUP * (c + half) + g) // 2
                array = q if g % 2 == half else swapped
                halves.append(array[:, tile * 128 : tile * 128 + 128])
            columns.append(jnp.where(low, halves[0], halves[1]))
        rows.append(jnp.concatenate(columns, axis=1))
    return jnp.concatenate(rows, axis=0)


def across_cores(j, chips):
    if j == 0 or j == chips - 1:
        return j
    return j + 1 if j % 2 else j - 1


def place_of(request, each, chip, core, kept):
    device = lax.div(request, each)
    distance = lax.shift_right_logical(device, 1) ^ chip
    return ((device & 1) ^ core) * kept + distance * each + lax.rem(request, each)


def parcel_kernel(mask_hbm, keys_hbm, values_hbm, query_hbm, parcel, mask_ref, query, pad, sems):
    held, rows = keys_hbm.shape[:2]
    pairs = [(mask_hbm, mask_ref), (query_hbm, query)]
    for i in range(held):
        at = 2 * i * rows
        pairs.append((keys_hbm.at[i], parcel.at[pl.ds(at, rows)]))
        pairs.append((values_hbm.at[i], parcel.at[pl.ds(at + rows, rows)]))
    copies = start_copies(pairs, sems)
    pad[...] = jnp.zeros_like(pad)
    for copy in copies:
        copy.wait()
    at = lax.broadcasted_iota(jnp.int32, (16, 128), 0) + lax.broadcasted_iota(
        jnp.int32, (16, 128), 1
    )
    for i in range(held):
        spot_rows = slice(2 * i * rows, 2 * i * rows + 16)
        keys = parcel[spot_rows, :128].astype(F32)
        dead = mask_ref[0, i] != 1
        parcel[spot_rows, :128] = jnp.where((at == 0) & dead, DEAD_MARK, keys).astype(BF16)
    count, each = query.shape[1:3]
    for n in range(count):
        pair = query[0, n].astype(F32) * HEAD_SIZE**-0.5
        for k in range(each):
            pad[k, n : n + 1] = pair[k : k + 1]
    end = 2 * held * rows
    for k in range(each):
        parcel[end + k * ROWS : end + (k + 1) * ROWS] = format_queries(pad[k]).astype(BF16)


def own_kernel(chips, each, shifts, held, *refs):
    owner_hbm, length_hbm, accepted_hbm, group_hbm = refs[:4]
    near_hbm, (keys_hbm, values_hbm) = refs[4:8], refs[8:10]
    query_ref, own_out, table_out, keys_out, values_out = refs[10:15]
    owner_ref, length_ref, accepted_ref, group_ref = refs[15:19]
    owner_row, near, rows_ref, small_sems, piece_sems = refs[19:]
    pieces, rows = keys_out.shape[:2]
    kept = chips * each
    small = start_copies(
        [
            (owner_hbm, owner_ref),
            (length_hbm, length_ref),
            (accepted_hbm, accepted_ref),
            (group_hbm, group_ref),
            (owner_hbm, owner_row),
        ]
        + [(x.at[0], near.at[j]) for j, x in enumerate(near_hbm)],
        small_sems,
    )
    large = start_copies(
        [(keys_hbm.at[0, i], keys_out.at[i]) for i in range(pieces)]
        + [(values_hbm.at[0, i], values_out.at[i]) for i in range(pieces)],
        piece_sems,
    )
    me = lax.axis_index("blk")
    z = lax.axis_index("req")
    chip, core = lax.shift_right_logical(me, 1), me & 1
    rows_ref[...] = jnp.zeros_like(rows_ref)
    for copy in small:
        copy.wait()
    count = near.shape[1]
    for n in range(count):
        for j in range(4):
            pair = near[j, n].astype(F32)
            for k in range(each):
                to = (j % 2) * POSITIONS + n
                rows_ref[j // 2, k, to : to + 1] = pair[k : k + 1]

    shape = (KEY_HEADS * ROWS, 2 * POSITIONS)
    column = lax.broadcasted_iota(jnp.int32, shape, 1)
    position = lax.broadcasted_iota(jnp.int32, shape, 0) % POSITIONS
    for k in range(each):
        live = ((column < POSITIONS) & (column < accepted_ref[0, k])) | (
            (column >= POSITIONS)
            & (column < POSITIONS + count)
            & (column - POSITIONS <= position)
        )
        got = attend(query_ref[k], rows_ref[0, k].astype(BF16), rows_ref[1, k].astype(BF16), live)
        for j in range(3):
            own_out[j, k] = got[j]

    owners = owner_row[...]
    slot = lax.broadcasted_iota(jnp.int32, owners.shape, 1)
    for i in range(pieces):
        index = me * pieces + i
        owner = owner_ref[0, index]
        same = jnp.where((owners == owner) & (slot < index), 1.0, 0.0)
        rank = jnp.sum(same, axis=1, keepdims=True).astype(jnp.int32)
        place = place_of(owner, each, chip, core, kept)
        table_out[i : i + 1] = jnp.full((1, 128), place, jnp.int32)
        table_out[pieces + i : pieces + i + 1] = jnp.broadcast_to(
            length_ref[0, owner] - rank * rows, (1, 128)
        )
    for i in range(kept):
        request = ((chip ^ (i // each)) * 2 + core) * each + i % each
        group = group_ref[0, request]
        shift = z ^ lax.div(group, held)
        fetched = (shift & ~1) - 1 + ((shift ^ core) & 1)
        array = jnp.where(shift == 0, 0, jnp.where(shift == 1, shifts - 1, fetched))
        to = 2 * pieces + i
        table_out[to : to + 1] = jnp.full((1, 128), array * held + lax.rem(group, held), jnp.int32)
    for copy in large:
        copy.wait()


def pair_kernel(own_ref, sibling_ref, both_ref, own_blocks_ref, queries_ref):
    held, size = own_blocks_ref.shape[:2]
    half = queries_ref.shape[0] // 2
    for side, ref in enumerate((own_ref, sibling_ref)):
        for i in range(held):
            block = ref[i * size : (i + 1) * size]
            both_ref[side * held + i] = block
            if side == 0:
                own_blocks_ref[i] = block
        for k in range(half):
            at = held * size + k * ROWS
            queries_ref[side * half + k] = ref[at : at + ROWS]


def pieces_kernel(chips, each, *refs):
    table_ref = refs[0]
    query_refs = refs[1 : 1 + chips]
    keys, values, mine_out = refs[1 + chips : 4 + chips]
    sibling_outs = refs[4 + chips : 6 + chips]
    queries_out, queries, acc = refs[6 + chips :]
    pieces, rows = keys.shape[0], keys.shape[1]
    kept = chips * each
    core = lax.axis_index("blk") & 1
    for j in range(chips):
        distance = jnp.where(core == 0, j, across_cores(j, chips))
        handed = j > 0 and j < chips - 1 and j % 2 == 0
        for side in range(2):
            start = (1 - side if handed else side) * each
            queries[pl.ds(side * kept + distance * each, each)] = query_refs[j][
                start : start + each
            ]
    queries_out[...] = queries[:kept]
    lane = lax.broadcasted_iota(jnp.int32, (1, rows), 1)
    places = [jnp.max(table_ref[i : i + 1]) for i in range(pieces)]
    got = []
    for i in range(pieces):
        filled = table_ref[pieces + i : pieces + i + 1]
        live = lane < jnp.concatenate([filled] * (rows // 128), axis=1)
        got.append(attend(queries[places[i]], keys[i], values[i], live))
    acc[0] = jnp.full_like(acc[0], LOWEST)
    acc[1] = jnp.zeros_like(acc[1])
    acc[2] = jnp.zeros_like(acc[2])
    for i in range(pieces):
        acc[0, places[i]] = jnp.maximum(acc[0, places[i]], got[i][0])
    for i in range(pieces):
        lift = jnp.exp(got[i][0] - acc[0, places[i]])
        acc[1, places[i]] += lift * got[i][1]
        acc[2, places[i]] += lift * got[i][2]
    mine_out[...] = acc[:, :kept]
    for i in range(kept):
        half, at = divmod(i, kept // 2)
        sibling_outs[half][at] = pack_message(*[acc[j, kept + i] for j in range(3)])


def join_kernel(mine_ref, own_ref, first_ref, second_ref, out_ref):
    half, each = first_ref.shape[0], own_ref.shape[1]
    opened = open_messages([first_ref[i] for i in range(half)] + [second_ref[i] for i in range(half)])
    for i in range(2 * half):
        blocks = [[mine_ref[j, i] for j in range(3)], opened[i]]
        if i < each:
            blocks.append([own_ref[j, i] for j in range(3)])
        joined = merge(*blocks)
        for j in range(3):
            out_ref[j, i] = joined[j]


def prompts_kernel(chips, each, shifts, first_row, *refs):
    table_ref, query_ref, joined_ref = refs[:3]
    array_refs, near_refs, out_refs = refs[3 : 2 + shifts], refs[2 + shifts : 4 + shifts], refs[4 + shifts :]
    held, rows = near_refs[0].shape[0], near_refs[0].shape[1] // 2
    lane = lax.broadcasted_iota(jnp.int32, (1, 2 * rows), 1)
    got = []
    for i in range(chips * each):
        at = jnp.max(table_ref[first_row + i : first_row + i + 1])
        array, slot = lax.div(at, held), lax.rem(at, held)

        def block(side):
            out = near_refs[side][slot]
            for j, ref in enumerate(array_refs):
                out = jnp.where(array == j, ref[side * held + slot], out)
            return out

        mine, other = block(0), block(1)
        marks = jnp.where(lane < rows, mine[:1, :1].astype(F32), other[:1, :1].astype(F32))
        got.append(
            attend(
                query_ref[i],
                jnp.concatenate([mine[:rows], other[:rows]], axis=0),
                jnp.concatenate([mine[rows:], other[rows:]], axis=0),
                marks < 0.5 * DEAD_MARK,
            )
        )
    for i in range(chips * each):
        merged = merge([joined_ref[j, i] for j in range(3)], got[i])
        out_refs[i // each][i % each] = pack_message(*merged)


def combine_kernel(chips, *refs):
    message_refs, out_ref = refs[:chips], refs[chips]
    count, each = out_ref.shape[1], out_ref.shape[2]
    low = lax.broadcasted_iota(jnp.int32, (POSITIONS, 128), 1) < HEAD_SIZE
    rows = []
    opened = open_messages([ref[k] for k in range(each) for ref in message_refs])
    for k in range(each):
        _, mass, part = merge(*opened[k * chips : (k + 1) * chips])
        out = part / mass
        swapped = swap_halves(out)
        columns = []
        for head in range(0, QUERY_HEADS, 2):
            c, g = head // GROUP, head % GROUP
            tile = slice((c // 2) * 128, (c // 2) * 128 + 128)
            first, second = (out, swapped) if c % 2 == 0 else (swapped, out)
            columns.append(
                jnp.where(
                    low,
                    first[g * POSITIONS : (g + 1) * POSITIONS, tile],
                    second[(g + 1) * POSITIONS : (g + 2) * POSITIONS, tile],
                )
            )
        rows.append(jnp.concatenate(columns, axis=1))
    for n in range(count):
        out_ref[0, n] = jnp.concatenate([row[n : n + 1] for row in rows], axis=0).astype(BF16)


ANY = pl.BlockSpec(memory_space=pl.ANY)
HBM = pl.BlockSpec(memory_space=pltpu.HBM)
VMEM = pl.BlockSpec(memory_space=pltpu.VMEM)


def in_hbm(x):
    return pltpu.with_memory_space_constraint(x, pltpu.HBM)


def call(kernel, name, out_shape, in_specs, scratch=(), cost=0):
    many = isinstance(out_shape, (list, tuple))
    return pl.pallas_call(
        kernel,
        name=name,
        out_shape=out_shape,
        in_specs=in_specs,
        out_specs=[VMEM] * len(out_shape) if many else VMEM,
        scratch_shapes=list(scratch),
        cost_estimate=pl.CostEstimate(flops=0, bytes_accessed=cost, transcendentals=0),
        compiler_params=pltpu.CompilerParams(vmem_limit_bytes=VMEM_LIMIT),
    )


def per_device(
    devices,
    shifts,
    verified_queries,
    new_keys,
    verified_value_rows,
    prior_round_keys,
    prior_round_values,
    accepted,
    group_id,
    cache_len,
    slot_owner,
    piece_cache_keys,
    piece_cache_values,
    shared_prompt_keys,
    shared_prompt_values,
    prompt_mask,
):
    shape = jax.ShapeDtypeStruct
    each = verified_queries.shape[1]
    chips = devices // 2
    pieces, piece_rows = piece_cache_keys.shape[1:3]
    held, block_rows = shared_prompt_keys.shape[:2]
    kept = chips * each

    def other_core(x):
        return lax.ppermute(x, "blk", [(i, i ^ 1) for i in range(devices)])

    def other_chip(x, s):
        return lax.ppermute(x, "blk", [(i, i ^ (2 * s)) for i in range(devices)])

    def along_req(x, even, odd):
        pairs = []
        for i in range(devices * shifts):
            d, z = divmod(i, shifts)
            pairs.append((i, d * shifts + (z ^ (odd if d % 2 else even))))
        return lax.ppermute(x, ("blk", "req"), pairs)

    verified_queries, prior_round_keys, new_keys, prior_round_values, verified_value_rows = (
        jnp.transpose(x, (0, 2, 1, 3))
        for x in (
            verified_queries, prior_round_keys, new_keys, prior_round_values, verified_value_rows,
        )
    )
    near = (prior_round_keys, new_keys, prior_round_values, verified_value_rows)
    count = verified_queries.shape[1]
    block_size = 2 * block_rows
    piece_shape = (pieces, piece_rows, WIDTH)
    parcel = call(
        parcel_kernel,
        "parcel",
        shape((held * block_size + each * ROWS, WIDTH), BF16),
        [HBM] * 4,
        [
            pltpu.SMEM((1, held), jnp.int32),
            pltpu.VMEM(verified_queries.shape, BF16),
            pltpu.VMEM((each, POSITIONS, QUERY_HEADS * HEAD_SIZE), F32),
            pltpu.SemaphoreType.DMA((2 + 2 * held,)),
        ],
    )(
        *(
            in_hbm(x)
            for x in (prompt_mask.T, shared_prompt_keys, shared_prompt_values, verified_queries)
        )
    )
    both_blocks, own_blocks, chip_queries = call(
        pair_kernel,
        "pair",
        [
            shape((2 * held, block_size, WIDTH), BF16),
            shape((held, block_size, WIDTH), BF16),
            shape((2 * each, ROWS, WIDTH), BF16),
        ],
        [VMEM] * 2,
    )(parcel, other_core(parcel))
    far_blocks = [along_req(both_blocks, s, s + 1) for s in range(2, shifts, 2)]
    near_blocks = along_req(own_blocks, 1, 1)

    own, table, keys, values = call(
        functools.partial(own_kernel, chips, each, shifts, held),
        "own",
        [
            shape((3, each, ROWS, WIDTH), F32),
            shape((2 * pieces + kept, 128), jnp.int32),
            shape(piece_shape, BF16),
            shape(piece_shape, BF16),
        ],
        [HBM] * 10 + [VMEM],
        [
            pltpu.SMEM(slot_owner.shape, jnp.int32),
            pltpu.SMEM(cache_len.shape, jnp.int32),
            pltpu.SMEM(accepted.shape, jnp.int32),
            pltpu.SMEM(group_id.shape, jnp.int32),
            pltpu.VMEM(slot_owner.shape, jnp.int32),
            pltpu.VMEM((4, count, each, WIDTH), BF16),
            pltpu.VMEM((2, each, 2 * POSITIONS, WIDTH), F32),
            pltpu.SemaphoreType.DMA((9,)),
            pltpu.SemaphoreType.DMA((2 * pieces,)),
        ],
        8 * 1024 * 1024,
    )(
        *(
            in_hbm(x)
            for x in (slot_owner, cache_len, accepted, group_id)
            + near
            + (piece_cache_keys, piece_cache_values)
        ),
        chip_queries,
    )

    queries = [chip_queries]
    for s in range(1, chips - 1, 2):
        fetched = lax.ppermute(
            chip_queries,
            "blk",
            [(i, i ^ (2 * (across_cores(s, chips) if i % 2 else s))) for i in range(devices)],
        )
        fetched = lax.optimization_barrier((fetched, table))[0]
        queries += [fetched, other_core(fetched)]
    if chips > 1:
        queries.append(other_chip(chip_queries, chips - 1))

    wide = (kept, ROWS, WIDTH)
    mine, *to_sibling, kept_queries = call(
        functools.partial(pieces_kernel, chips, each),
        "pieces",
        [shape((3,) + wide, F32)]
        + [shape((kept // 2, MESSAGE, WIDTH), F32)] * 2
        + [shape(wide, BF16)],
        [VMEM] * (chips + 3),
        [
            pltpu.VMEM((2 * kept, ROWS, WIDTH), BF16),
            pltpu.VMEM((3, 2 * kept, ROWS, WIDTH), F32),
        ],
    )(table, *queries, keys, values)
    near_blocks, *to_sibling = lax.optimization_barrier((near_blocks, *to_sibling))
    from_sibling = [other_core(x) for x in to_sibling]
    joined = call(join_kernel, "join", shape((3,) + wide, F32), [VMEM] * 4)(
        mine, own, *from_sibling
    )
    block_arrays = [both_blocks]
    for x in far_blocks:
        x = lax.optimization_barrier((x, joined))[0]
        block_arrays += [x, other_core(x)]
    block_arrays += [near_blocks, other_core(near_blocks)]

    messages = call(
        functools.partial(prompts_kernel, chips, each, shifts, 2 * pieces),
        "prompts",
        [shape((each, MESSAGE, WIDTH), F32)] * chips,
        [VMEM] * (4 + shifts),
    )(table, kept_queries, joined, *block_arrays)
    arrived = [messages[0]] + [other_chip(messages[s], s) for s in range(1, chips)]

    out = call(
        functools.partial(combine_kernel, chips),
        "combine",
        shape(verified_queries.shape, BF16),
        [VMEM] * chips,
    )(*arrived)
    return jnp.transpose(out, (0, 2, 1, 3))


def solution(mesh):
    placed = (
        P("req", "blk", None, None),
        P("req", "blk", None, None),
        P("req", "blk", None, None),
        P("req", "blk", None, None),
        P("req", "blk", None, None),
        P("req", "blk"),
        P("req", None),
        P("req", None),
        P("req", None),
        P("req", "blk", None, None),
        P("req", "blk", None, None),
        P("req", "blk", None),
        P("req", "blk", None),
        P("req", "blk"),
    )
    return jax.shard_map(
        functools.partial(per_device, mesh.shape["blk"], mesh.shape["req"]),
        mesh=mesh,
        in_specs=placed,
        out_specs=P("req", "blk", None, None),
        check_vma=False,
    )
```

time: 32.5 us -> 32.2 us (level)
  starting transfers between devices: 15.6 us -> 13.8 us
  waiting for transfers between devices: 8.12 us -> 9.59 us
    ppermute x6 -> x4, starting transfers between devices: 8.45 us -> 5.04 us  [other_chip(): return lax.ppermute(x, 'blk', [(i, i ^ 2 * s) for i in range(devices)])]
    ppermute x3, starting transfers between devices: 5.51 us -> 7.08 us  [the longest x2 5.59 us: along_req(): return lax.ppermute(x, ('blk', 'req'), pairs)]
    ppermute x6, waiting for transfers between devices: 1.91 us -> 3.19 us  [other_core(): return lax.ppermute(x, 'blk', [(i, i ^ 1) for i in range(devices)])]
    ppermute x3, waiting for transfers between devices: 0.01 us -> 0.6 us  [the longest x2 0.6 us: along_req(): return lax.ppermute(x, ('blk', 'req'), pairs)]
    pallas_call x1, Pallas kernels: 2.57 us -> 2.11 us  [per_device(): call(functools.partial(prompts_kernel, chips, each, shifts, 2 * pieces),...]
    ppermute x6 -> x4, waiting for transfers between devices: 6.21 us -> 5.8 us  [other_chip(): return lax.ppermute(x, 'blk', [(i, i ^ 2 * s) for i in range(devices)])]
  transfers between devices with their start and end apart: 15 -> 13, of which waited for: 9 -> 9; matrix products, arithmetic and copies ran while one was open for 0% -> 0% of each run, Pallas kernels for 15% -> 13%
where the time goes in v2:
time: 32.2 us; the launch traced here: 32 us
  starting transfers between devices  13.8 us (43%)
  waiting for transfers between devices  9.59 us (30%)
  Pallas kernels  8.49 us (26%)
    ppermute x4, waiting for transfers between devices, other_chip(): return lax.ppermute(x, 'blk', [(i, i ^ 2 * s) for i in range(devices)])  5.8 us
    ppermute x2, starting transfers between devices, along_req(): return lax.ppermute(x, ('blk', 'req'), pairs)  5.59 us
    ppermute x4, starting transfers between devices, other_chip(): return lax.ppermute(x, 'blk', [(i, i ^ 2 * s) for i in range(devices)])  5.04 us
    ppermute x6, waiting for transfers between devices, other_core(): return lax.ppermute(x, 'blk', [(i, i ^ 1) for i in range(devices)])  3.19 us
    pallas_call x1, Pallas kernels, per_device(): call(functools.partial(own_kernel, chips, each, shifts, held), 'own', [sh...  2.29 us
    pallas_call x1, Pallas kernels, per_device(): call(functools.partial(prompts_kernel, chips, each, shifts, 2 * pieces),...  2.11 us
    pallas_call x1, Pallas kernels, per_device(): call(functools.partial(pieces_kernel, chips, each), 'pieces', [shape((3,)...  1.71 us
    ppermute x6, starting transfers between devices, other_core(): return lax.ppermute(x, 'blk', [(i, i ^ 1) for i in range(devices)])  1.67 us
  transfers between devices with their start and end apart: 13, of which 9 were waited for; matrix products, arithmetic and copies ran while one was open for 0% of the time, Pallas kernels for 13%

profile of v2, /device:TPU:0, one launch (start us, length us, event | category | flops | bytes accessed | tf_op | source)
XLA Modules:
  0.0 32.0 jit_solution(14646787453074181059)
XLA Ops:
  0.0 1.0 %parcel.1.own_ref = bf16[320,256]{1,0:T(8,128)(2,1)S(1)} custom-call(s32[1,4]{1,0:T(1,128)} %bitcast.12, bf16[4,32,256]{2,1,0:T(8,128)(2,1)} %keys_hbm.1, bf16[4,32,256]{2,1,0:T(8,128)(2,1)} %values_hbm.1, bf16[1,5,2,1024]{3,2,1,0:T(2,128)(2,1)} %bitcast.7), custom_call_target="tpu_custom_call" | custom-call | tf_op jit(solution)/shard_map/parcel/pallas_call | solution.py:477
  1.0 0.5 %collective-permute-start = (bf16[320,256]{1,0:T(8,128)(2,1)S(1)}, bf16[320,256]{1,0:T(8,128)(2,1)S(1)}, u32[]{:S(2)}, u32[]{:S(2)}) collective-permute-start(bf16[320,256]{1,0:T(8,128)(2,1)S(1)} %parcel.1.own_ref), channel_id=1, source_target_pairs={{0,4},{4,0},{8,12},{12,8},{16,20},{20,16},{24,28},{28,24},{1,5},{5... | collective-permute-start | bytes 491528 | tf_op jit(solution)/shard_map/ppermute | solution.py:455
  1.6 1.0 %collective-permute-done.sibling_ref = bf16[320,256]{1,0:T(8,128)(2,1)S(1)} collective-permute-done((bf16[320,256]{1,0:T(8,128)(2,1)S(1)}, bf16[320,256]{1,0:T(8,128)(2,1)S(1)}, u32[]{:S(2)}, u32[]{:S(2)}) %collective-permute-start) | collective-permute-done | bytes 163872 | tf_op jit(solution)/shard_map/ppermute | solution.py:455
  2.6 4.0 %collective-permute-start.7 = (bf16[8,64,256]{2,1,0:T(8,128)(2,1)S(1)}, bf16[8,64,256]{2,1,0:T(8,128)(2,1)S(1)}, u32[]{:S(2)}, u32[]{:S(2)}) collective-permute-start(bf16[8,64,256]{2,1,0:T(8,128)(2,1)S(1)} %get-tuple-element.38.refs_3_), channel_id=1, source_target_pairs={{0,2},{1,3},{2,0},{3,1},{4,7},{5,6},{6,5},{7,4},{8,10},{9,11},{10,... | collective-permute-start | bytes 786440 | tf_op jit(solution)/shard_map/ppermute | solution.py:465
  6.6 1.5 %collective-permute-start.1 = (bf16[4,32,256]{2,1,0:T(8,128)(2,1)S(1)}, bf16[4,32,256]{2,1,0:T(8,128)(2,1)S(1)}, u32[]{:S(2)}, u32[]{:S(2)}) collective-permute-start(bf16[4,32,256]{2,1,0:T(8,128)(2,1)S(1)} %get-tuple-element.25.refs_10_.refs_1_), channel_id=1, source_target_pairs={{0,8},{4,20},{8,0},{12,28},{16,24},{20,4},{24,16},{28,12},{1,9},{5... | collective-permute-start | bytes 196616 | tf_op jit(solution)/shard_map/ppermute | solution.py:541
  8.1 1.6 %collective-permute-start.4 = (bf16[4,64,256]{2,1,0:T(8,128)(2,1)S(1)}, bf16[4,64,256]{2,1,0:T(8,128)(2,1)S(1)}, u32[]{:S(2)}, u32[]{:S(2)}) collective-permute-start(bf16[4,64,256]{2,1,0:T(8,128)(2,1)S(1)} %get-tuple-element.33), channel_id=1, source_target_pairs={{0,1},{1,0},{2,3},{3,2},{4,5},{5,4},{6,7},{7,6},{8,9},{9,8},{10,11... | collective-permute-start | bytes 393224 | tf_op jit(solution)/shard_map/ppermute | solution.py:465
  9.7 1.5 %collective-permute-start.3 = (bf16[4,32,256]{2,1,0:T(8,128)(2,1)S(1)}, bf16[4,32,256]{2,1,0:T(8,128)(2,1)S(1)}, u32[]{:S(2)}, u32[]{:S(2)}) collective-permute-start(bf16[4,32,256]{2,1,0:T(8,128)(2,1)S(1)} %get-tuple-element.25.refs_10_.refs_1_), channel_id=1, source_target_pairs={{0,24},{4,28},{8,16},{12,20},{16,8},{20,12},{24,0},{28,4},{1,25},{... | collective-permute-start | bytes 196616 | tf_op jit(solution)/shard_map/ppermute | solution.py:458
  11.2 2.3 %own.1 = (f32[3,2,32,256]{3,2,1,0:T(8,128)S(1)}, s32[24,128]{1,0:T(8,128)S(1)}, bf16[8,256,256]{2,1,0:T(8,128)(2,1)S(1)}, bf16[8,256,256]{2,1,0:T(8,128)(2,1)S(1)}) custom-call(s32[1,64]{1,0:T(1,128)} %refs_0_.1, s32[1,16]{1,0:T(1,128)} %refs_1_.1, s32[1,2]{1,0:T(1,128)} %refs_2_.1, s32[1,16]{1,0:T(1,128)} %refs_3_.1, bf16[1,5,2,256]{3,2,1,0:T(2,128)(2,1)} %bitcast.8, ...), custom_call_target="tpu_custom_call" | custom-call | bytes 8388608 | tf_op jit(solution)/shard_map/own/pallas_call | solution.py:507
  13.5 0.0 collective-permute-done.1.refs_2_
  13.5 0.1 collective-permute-start.2
  13.6 1.3 %collective-permute-done.3.refs_4_ = bf16[4,32,256]{2,1,0:T(8,128)(2,1)S(1)} collective-permute-done((bf16[4,32,256]{2,1,0:T(8,128)(2,1)S(1)}, bf16[4,32,256]{2,1,0:T(8,128)(2,1)S(1)}, u32[]{:S(2)}, u32[]{:S(2)}) %collective-permute-start.3) | collective-permute-done | bytes 65568 | tf_op jit(solution)/shard_map/ppermute | solution.py:458
  14.9 0.0 collective-permute-done.2.refs_3_
  14.9 1.7 %pieces.1 = (f32[3,8,32,256]{3,2,1,0:T(8,128)S(1)}, f32[4,24,256]{2,1,0:T(8,128)S(1)}, f32[4,24,256]{2,1,0:T(8,128)S(1)}, bf16[8,32,256]{2,1,0:T(8,128)(2,1)S(1)}) custom-call(s32[24,128]{1,0:T(8,128)S(1)} %get-tuple-element.26.refs_0_, bf16[4,32,256]{2,1,0:T(8,128)(2,1)S(1)} %get-tuple-element.25.refs_10_.refs_1_, ...), custom_call_target="tpu_custom_call" | custom-call | tf_op jit(solution)/shard_map/pieces/pallas_call | solution.py:552
  16.6 0.0 collective-permute-done.4.refs_6_
  16.6 0.2 collective-permute-start.5
  16.8 0.4 %collective-permute-start.6 = (f32[4,24,256]{2,1,0:T(8,128)S(1)}, f32[4,24,256]{2,1,0:T(8,128)S(1)}, u32[]{:S(2)}, u32[]{:S(2)}) collective-permute-start(f32[4,24,256]{2,1,0:T(8,128)S(1)} %get-tuple-element.37), channel_id=1, source_target_pairs={{0,4},{4,0},{8,12},{12,8},{16,20},{20,16},{24,28},{28,24},{1,5},{5... | collective-permute-start | bytes 294920 | tf_op jit(solution)/shard_map/ppermute | solution.py:455
  17.2 0.8 %collective-permute-done.5.first_ref = f32[4,24,256]{2,1,0:T(8,128)S(1)} collective-permute-done((f32[4,24,256]{2,1,0:T(8,128)S(1)}, f32[4,24,256]{2,1,0:T(8,128)S(1)}, u32[]{:S(2)}, u32[]{:S(2)}) %collective-permute-start.5) | collective-permute-done | bytes 98336 | tf_op jit(solution)/shard_map/ppermute | solution.py:455
  18.0 0.2 collective-permute-done.6.second_ref
  18.1 0.3 join.1.refs_2_
  18.4 0.6 %collective-permute-done.7.refs_4_ = bf16[8,64,256]{2,1,0:T(8,128)(2,1)S(1)} collective-permute-done((bf16[8,64,256]{2,1,0:T(8,128)(2,1)S(1)}, bf16[8,64,256]{2,1,0:T(8,128)(2,1)S(1)}, u32[]{:S(2)}, u32[]{:S(2)}) %collective-permute-start.7) | collective-permute-done | bytes 262176 | tf_op jit(solution)/shard_map/ppermute | solution.py:465
  19.0 0.0 collective-permute-start.8
  19.0 0.5 %collective-permute-start.9 = (bf16[4,64,256]{2,1,0:T(8,128)(2,1)S(1)}, bf16[4,64,256]{2,1,0:T(8,128)(2,1)S(1)}, u32[]{:S(2)}, u32[]{:S(2)}) collective-permute-start(bf16[4,64,256]{2,1,0:T(8,128)(2,1)S(1)} %collective-permute-done.4.refs_6_), channel_id=1, source_target_pairs={{0,4},{4,0},{8,12},{12,8},{16,20},{20,16},{24,28},{28,24},{1,5},{5... | collective-permute-start | bytes 393224 | tf_op jit(solution)/shard_map/ppermute | solution.py:455
  19.5 1.2 %collective-permute-done.9.refs_7_ = bf16[4,64,256]{2,1,0:T(8,128)(2,1)S(1)} collective-permute-done((bf16[4,64,256]{2,1,0:T(8,128)(2,1)S(1)}, bf16[4,64,256]{2,1,0:T(8,128)(2,1)S(1)}, u32[]{:S(2)}, u32[]{:S(2)}) %collective-permute-start.9) | collective-permute-done | bytes 131104 | tf_op jit(solution)/shard_map/ppermute | solution.py:455
  20.8 0.0 collective-permute-done.8.refs_5_
  20.8 2.1 %prompts.1 = (f32[2,24,256]{2,1,0:T(8,128)S(1)}, f32[2,24,256]{2,1,0:T(8,128)S(1)}, f32[2,24,256]{2,1,0:T(8,128)S(1)}, f32[2,24,256]{2,1,0:T(8,128)S(1)}) custom-call(s32[24,128]{1,0:T(8,128)S(1)} %get-tuple-element.26.refs_0_, bf16[8,32,256]{2,1,0:T(8,128)(2,1)S(1)} %get-tuple-element.30.refs_1_, f32[3,8,32,256]{3,2,1,0:T(8,128)S(1)} %join.1.refs_2_, ...), custom_call_target="tpu_custom_call" | custom-call | tf_op jit(solution)/shard_map/prompts/pallas_call | solution.py:575
  22.9 1.6 %collective-permute-start.10 = (f32[2,24,256]{2,1,0:T(8,128)S(1)}, f32[2,24,256]{2,1,0:T(8,128)S(1)}, u32[]{:S(2)}, u32[]{:S(2)}) collective-permute-start(f32[2,24,256]{2,1,0:T(8,128)S(1)} %get-tuple-element.42), channel_id=1, source_target_pairs={{0,8},{4,12},{8,0},{12,4},{16,24},{20,28},{24,16},{28,20},{1,9},{5... | collective-permute-start | bytes 147464 | tf_op jit(solution)/shard_map/ppermute | solution.py:458
  24.4 1.5 %collective-permute-start.11 = (f32[2,24,256]{2,1,0:T(8,128)S(1)}, f32[2,24,256]{2,1,0:T(8,128)S(1)}, u32[]{:S(2)}, u32[]{:S(2)}) collective-permute-start(f32[2,24,256]{2,1,0:T(8,128)S(1)} %get-tuple-element.43), channel_id=1, source_target_pairs={{0,16},{4,20},{8,24},{12,28},{16,0},{20,4},{24,8},{28,12},{1,17},{... | collective-permute-start | bytes 147464 | tf_op jit(solution)/shard_map/ppermute | solution.py:458
  26.0 0.5 %collective-permute-start.12 = (f32[2,24,256]{2,1,0:T(8,128)S(1)}, f32[2,24,256]{2,1,0:T(8,128)S(1)}, u32[]{:S(2)}, u32[]{:S(2)}) collective-permute-start(f32[2,24,256]{2,1,0:T(8,128)S(1)} %get-tuple-element.44), channel_id=1, source_target_pairs={{0,24},{4,28},{8,16},{12,20},{16,8},{20,12},{24,0},{28,4},{1,25},{... | collective-permute-start | bytes 147464 | tf_op jit(solution)/shard_map/ppermute | solution.py:458
  26.4 0.6 %collective-permute-done.10.refs_1_ = f32[2,24,256]{2,1,0:T(8,128)S(1)} collective-permute-done((f32[2,24,256]{2,1,0:T(8,128)S(1)}, f32[2,24,256]{2,1,0:T(8,128)S(1)}, u32[]{:S(2)}, u32[]{:S(2)}) %collective-permute-start.10) | collective-permute-done | bytes 49184 | tf_op jit(solution)/shard_map/ppermute | solution.py:458
  27.0 1.5 %collective-permute-done.11.refs_2_ = f32[2,24,256]{2,1,0:T(8,128)S(1)} collective-permute-done((f32[2,24,256]{2,1,0:T(8,128)S(1)}, f32[2,24,256]{2,1,0:T(8,128)S(1)}, u32[]{:S(2)}, u32[]{:S(2)}) %collective-permute-start.11) | collective-permute-done | bytes 49184 | tf_op jit(solution)/shard_map/ppermute | solution.py:458
  28.5 2.4 %collective-permute-done.12.refs_3_ = f32[2,24,256]{2,1,0:T(8,128)S(1)} collective-permute-done((f32[2,24,256]{2,1,0:T(8,128)S(1)}, f32[2,24,256]{2,1,0:T(8,128)S(1)}, u32[]{:S(2)}, u32[]{:S(2)}) %collective-permute-start.12) | collective-permute-done | bytes 49184 | tf_op jit(solution)/shard_map/ppermute | solution.py:458
  30.9 1.0 %combine.1 = bf16[1,5,2,1024]{3,2,1,0:T(2,128)(2,1)} custom-call(f32[2,24,256]{2,1,0:T(8,128)S(1)} %get-tuple-element.41.refs_0_, f32[2,24,256]{2,1,0:T(8,128)S(1)} %collective-permute-done.10.refs_1_, f32[2,24,256]{2,1,0:T(8,128)S(1)} %collective-permute-done.11.refs_2_, f32[2,24,256]{2,1,0:T(8,128)S(1)} %collective-permute-done.12.refs_3_), custom_call_target="tpu_custom_call" | custom-call | tf_op jit(solution)/shard_map/combine/pallas_call | solution.py:583
  (1 shorter events, 0.0 us)
Async XLA Ops:
  1.0 1.5 %collective-permute-start = (bf16[320,256]{1,0:T(8,128)(2,1)S(1)}, bf16[320,256]{1,0:T(8,128)(2,1)S(1)}, u32[]{:S(2)}, u32[]{:S(2)}) collective-permute-start(bf16[320,256]{1,0:T(8,128)(2,1)S(1)} %parcel.1.own_ref), channel_id=1, source_target_pairs={{0,4},{4,0},{8,12},{12,8},{16,20},{20,16},{24,28},{28,24},{1,5},{5... | collective-permute-start | bytes 491528 | tf_op jit(solution)/shard_map/ppermute | solution.py:455
  2.6 16.4 %collective-permute-start.7 = (bf16[8,64,256]{2,1,0:T(8,128)(2,1)S(1)}, bf16[8,64,256]{2,1,0:T(8,128)(2,1)S(1)}, u32[]{:S(2)}, u32[]{:S(2)}) collective-permute-start(bf16[8,64,256]{2,1,0:T(8,128)(2,1)S(1)} %get-tuple-element.38.refs_3_), channel_id=1, source_target_pairs={{0,2},{1,3},{2,0},{3,1},{4,7},{5,6},{6,5},{7,4},{8,10},{9,11},{10,... | collective-permute-start | bytes 786440 | tf_op jit(solution)/shard_map/ppermute | solution.py:465
  6.6 6.9 %collective-permute-start.1 = (bf16[4,32,256]{2,1,0:T(8,128)(2,1)S(1)}, bf16[4,32,256]{2,1,0:T(8,128)(2,1)S(1)}, u32[]{:S(2)}, u32[]{:S(2)}) collective-permute-start(bf16[4,32,256]{2,1,0:T(8,128)(2,1)S(1)} %get-tuple-element.25.refs_10_.refs_1_), channel_id=1, source_target_pairs={{0,8},{4,20},{8,0},{12,28},{16,24},{20,4},{24,16},{28,12},{1,9},{5... | collective-permute-start | bytes 196616 | tf_op jit(solution)/shard_map/ppermute | solution.py:541
  8.1 8.5 %collective-permute-start.4 = (bf16[4,64,256]{2,1,0:T(8,128)(2,1)S(1)}, bf16[4,64,256]{2,1,0:T(8,128)(2,1)S(1)}, u32[]{:S(2)}, u32[]{:S(2)}) collective-permute-start(bf16[4,64,256]{2,1,0:T(8,128)(2,1)S(1)} %get-tuple-element.33), channel_id=1, source_target_pairs={{0,1},{1,0},{2,3},{3,2},{4,5},{5,4},{6,7},{7,6},{8,9},{9,8},{10,11... | collective-permute-start | bytes 393224 | tf_op jit(solution)/shard_map/ppermute | solution.py:465
  9.7 5.2 %collective-permute-start.3 = (bf16[4,32,256]{2,1,0:T(8,128)(2,1)S(1)}, bf16[4,32,256]{2,1,0:T(8,128)(2,1)S(1)}, u32[]{:S(2)}, u32[]{:S(2)}) collective-permute-start(bf16[4,32,256]{2,1,0:T(8,128)(2,1)S(1)} %get-tuple-element.25.refs_10_.refs_1_), channel_id=1, source_target_pairs={{0,24},{4,28},{8,16},{12,20},{16,8},{20,12},{24,0},{28,4},{1,25},{... | collective-permute-start | bytes 196616 | tf_op jit(solution)/shard_map/ppermute | solution.py:458
  13.5 1.4 %collective-permute-start.2 = (bf16[4,32,256]{2,1,0:T(8,128)(2,1)S(1)}, bf16[4,32,256]{2,1,0:T(8,128)(2,1)S(1)}, u32[]{:S(2)}, u32[]{:S(2)}) collective-permute-start(bf16[4,32,256]{2,1,0:T(8,128)(2,1)S(1)} %collective-permute-done.1.refs_2_), channel_id=1, source_target_pairs={{0,4},{4,0},{8,12},{12,8},{16,20},{20,16},{24,28},{28,24},{1,5},{5... | collective-permute-start | bytes 196616 | tf_op jit(solution)/shard_map/ppermute | solution.py:455
  16.6 1.4 %collective-permute-start.5 = (f32[4,24,256]{2,1,0:T(8,128)S(1)}, f32[4,24,256]{2,1,0:T(8,128)S(1)}, u32[]{:S(2)}, u32[]{:S(2)}) collective-permute-start(f32[4,24,256]{2,1,0:T(8,128)S(1)} %get-tuple-element.36), channel_id=1, source_target_pairs={{0,4},{4,0},{8,12},{12,8},{16,20},{20,16},{24,28},{28,24},{1,5},{5... | collective-permute-start | bytes 294920 | tf_op jit(solution)/shard_map/ppermute | solution.py:455
  16.8 1.4 %collective-permute-start.6 = (f32[4,24,256]{2,1,0:T(8,128)S(1)}, f32[4,24,256]{2,1,0:T(8,128)S(1)}, u32[]{:S(2)}, u32[]{:S(2)}) collective-permute-start(f32[4,24,256]{2,1,0:T(8,128)S(1)} %get-tuple-element.37), channel_id=1, source_target_pairs={{0,4},{4,0},{8,12},{12,8},{16,20},{20,16},{24,28},{28,24},{1,5},{5... | collective-permute-start | bytes 294920 | tf_op jit(solution)/shard_map/ppermute | solution.py:455
  19.0 1.7 %collective-permute-start.8 = (bf16[8,64,256]{2,1,0:T(8,128)(2,1)S(1)}, bf16[8,64,256]{2,1,0:T(8,128)(2,1)S(1)}, u32[]{:S(2)}, u32[]{:S(2)}) collective-permute-start(bf16[8,64,256]{2,1,0:T(8,128)(2,1)S(1)} %collective-permute-done.7.refs_4_), channel_id=1, source_target_pairs={{0,4},{4,0},{8,12},{12,8},{16,20},{20,16},{24,28},{28,24},{1,5},{5... | collective-permute-start | bytes 786440 | tf_op jit(solution)/shard_map/ppermute | solution.py:455
  19.0 1.7 %collective-permute-start.9 = (bf16[4,64,256]{2,1,0:T(8,128)(2,1)S(1)}, bf16[4,64,256]{2,1,0:T(8,128)(2,1)S(1)}, u32[]{:S(2)}, u32[]{:S(2)}) collective-permute-start(bf16[4,64,256]{2,1,0:T(8,128)(2,1)S(1)} %collective-permute-done.4.refs_6_), channel_id=1, source_target_pairs={{0,4},{4,0},{8,12},{12,8},{16,20},{20,16},{24,28},{28,24},{1,5},{5... | collective-permute-start | bytes 393224 | tf_op jit(solution)/shard_map/ppermute | solution.py:455
  22.9 4.2 %collective-permute-start.10 = (f32[2,24,256]{2,1,0:T(8,128)S(1)}, f32[2,24,256]{2,1,0:T(8,128)S(1)}, u32[]{:S(2)}, u32[]{:S(2)}) collective-permute-start(f32[2,24,256]{2,1,0:T(8,128)S(1)} %get-tuple-element.42), channel_id=1, source_target_pairs={{0,8},{4,12},{8,0},{12,4},{16,24},{20,28},{24,16},{28,20},{1,9},{5... | collective-permute-start | bytes 147464 | tf_op jit(solution)/shard_map/ppermute | solution.py:458
  24.4 4.1 %collective-permute-start.11 = (f32[2,24,256]{2,1,0:T(8,128)S(1)}, f32[2,24,256]{2,1,0:T(8,128)S(1)}, u32[]{:S(2)}, u32[]{:S(2)}) collective-permute-start(f32[2,24,256]{2,1,0:T(8,128)S(1)} %get-tuple-element.43), channel_id=1, source_target_pairs={{0,16},{4,20},{8,24},{12,28},{16,0},{20,4},{24,8},{28,12},{1,17},{... | collective-permute-start | bytes 147464 | tf_op jit(solution)/shard_map/ppermute | solution.py:458
  26.0 5.0 %collective-permute-start.12 = (f32[2,24,256]{2,1,0:T(8,128)S(1)}, f32[2,24,256]{2,1,0:T(8,128)S(1)}, u32[]{:S(2)}, u32[]{:S(2)}) collective-permute-start(f32[2,24,256]{2,1,0:T(8,128)S(1)} %get-tuple-element.44), channel_id=1, source_target_pairs={{0,24},{4,28},{8,16},{12,20},{16,8},{20,12},{24,0},{28,4},{1,25},{... | collective-permute-start | bytes 147464 | tf_op jit(solution)/shard_map/ppermute | solution.py:458

commit v3 on v2

--- a/solution.py
+++ b/solution.py
@@ -68,23 +68,6 @@
     return fold_heads(top), fold_heads(mass), fold_heads(part)
 
 
-def attend_two(q, keys, values, live):
-    masked = jnp.where(live, score(q, keys), LOWEST)
-    first = lax.broadcasted_iota(jnp.int32, masked.shape, 1) < masked.shape[1] // 2
-    top_a = jnp.max(jnp.where(first, masked, LOWEST), axis=1, keepdims=True)
-    top_b = jnp.max(jnp.where(first, LOWEST, masked), axis=1, keepdims=True)
-    weights = jnp.exp(masked - jnp.where(first, top_a, top_b))
-    both = jnp.concatenate(
-        [jnp.where(first, weights, 0.0), jnp.where(first, 0.0, weights)], axis=0
-    ).astype(BF16)
-    mass, part = weigh(both, values)
-    rows = masked.shape[0]
-    return (
-        (fold_heads(top_a), fold_heads(mass[:rows]), fold_heads(part[:rows])),
-        (fold_heads(top_b), fold_heads(mass[rows:]), fold_heads(part[rows:])),
-    )
-
-
 def merge(*blocks):
     top = functools.reduce(jnp.maximum, [b[0] for b in blocks])
     lifts = [jnp.exp(b[0] - top) for b in blocks]
@@ -96,6 +79,26 @@
 def spot(shape):
     lane = lax.broadcasted_iota(jnp.int32, shape, 1) % HEAD_SIZE
     return lane == lax.broadcasted_iota(jnp.int32, shape, 0) % ROWS
+
+
+def pack_rows(x, spare=(None, None, None)):
+    sub = lax.broadcasted_iota(jnp.int32, (POSITIONS, WIDTH), 0)
+    tile = lambda i: x[i * POSITIONS : (i + 1) * POSITIONS]
+    a, b, c = (jnp.zeros((1, WIDTH), x.dtype) if row is None else row for row in spare)
+    return jnp.concatenate(
+        [
+            jnp.where(sub < 5, tile(0), pltpu.roll(tile(3), 5, 0)),
+            jnp.where(sub < 5, tile(1), jnp.where(sub < 7, pltpu.roll(tile(3), 2, 0), a)),
+            jnp.where(sub < 5, tile(2), jnp.where(sub < 6, b, c)),
+        ],
+        axis=0,
+    )
+
+
+def unpack_rows(x):
+    sub = lax.broadcasted_iota(jnp.int32, (POSITIONS, WIDTH), 0)
+    last = jnp.where(sub < 3, pltpu.roll(x[0:8], 3, 0), pltpu.roll(x[8:16], 6, 0))
+    return jnp.concatenate([x, last], axis=0)
 
 
 def pack_message(top, mass, part):
@@ -105,16 +108,7 @@
     high = mass.astype(BF16).astype(F32)
     at = spot((ROWS, WIDTH))
     row_of = lambda x: jnp.sum(jnp.where(at, x, 0.0), axis=0, keepdims=True)
-    sub = lax.broadcasted_iota(jnp.int32, (POSITIONS, WIDTH), 0)
-    tile = lambda i: part[i * POSITIONS : (i + 1) * POSITIONS]
-    return jnp.concatenate(
-        [
-            jnp.where(sub < 5, tile(0), pltpu.roll(tile(3), 5, 0)),
-            jnp.where(sub < 5, tile(1), jnp.where(sub < 7, pltpu.roll(tile(3), 2, 0), row_of(rounded))),
-            jnp.where(sub < 5, tile(2), jnp.where(sub < 6, row_of(high), row_of(mass - high))),
-        ],
-        axis=0,
-    )
+    return pack_rows(part, (row_of(rounded), row_of(high), row_of(mass - high)))
 
 
 def open_messages(messages):
@@ -128,12 +122,10 @@
     )
     ones = jnp.where(same_head, 1.0, 0.0).astype(BF16)
     spread = jnp.dot(jnp.concatenate(rows, axis=0), ones, preferred_element_type=F32)
-    sub = lax.broadcasted_iota(jnp.int32, (POSITIONS, WIDTH), 0)
     out = []
     for i, x in enumerate(messages):
         get = lambda j: spread[(3 * i + j) * ROWS : (3 * i + j + 1) * ROWS]
-        last = jnp.where(sub < 3, pltpu.roll(x[0:8], 3, 0), pltpu.roll(x[8:16], 6, 0))
-        out.append((get(0), get(1) + get(2), jnp.concatenate([x, last], axis=0)))
+        out.append((get(0), get(1) + get(2), unpack_rows(x)))
     return out
 
 
@@ -175,13 +167,16 @@
     return ((device & 1) ^ core) * kept + distance * each + lax.rem(request, each)
 
 
-def parcel_kernel(mask_hbm, keys_hbm, values_hbm, query_hbm, parcel, mask_ref, query, pad, sems):
+def parcel_kernel(
+    mask_hbm, keys_hbm, values_hbm, query_hbm, blocks_ref, queries_ref, mask_ref, query, pad, sems
+):
     held, rows = keys_hbm.shape[:2]
-    pairs = [(mask_hbm, mask_ref), (query_hbm, query)]
-    for i in range(held):
-        at = 2 * i * rows
-        pairs.append((keys_hbm.at[i], parcel.at[pl.ds(at, rows)]))
-        pairs.append((values_hbm.at[i], parcel.at[pl.ds(at + rows, rows)]))
+    pairs = [
+        (mask_hbm, mask_ref),
+        (query_hbm, query),
+        (keys_hbm, blocks_ref.at[:, pl.ds(0, rows)]),
+        (values_hbm, blocks_ref.at[:, pl.ds(rows, rows)]),
+    ]
     copies = start_copies(pairs, sems)
     pad[...] = jnp.zeros_like(pad)
     for copy in copies:
@@ -190,18 +185,27 @@
         jnp.int32, (16, 128), 1
     )
     for i in range(held):
-        spot_rows = slice(2 * i * rows, 2 * i * rows + 16)
-        keys = parcel[spot_rows, :128].astype(F32)
+        keys = blocks_ref[i, :16, :128].astype(F32)
         dead = mask_ref[0, i] != 1
-        parcel[spot_rows, :128] = jnp.where((at == 0) & dead, DEAD_MARK, keys).astype(BF16)
+        blocks_ref[i, :16, :128] = jnp.where((at == 0) & dead, DEAD_MARK, keys).astype(BF16)
     count, each = query.shape[1:3]
     for n in range(count):
         pair = query[0, n].astype(F32) * HEAD_SIZE**-0.5
         for k in range(each):
             pad[k, n : n + 1] = pair[k : k + 1]
-    end = 2 * held * rows
     for k in range(each):
-        parcel[end + k * ROWS : end + (k + 1) * ROWS] = format_queries(pad[k]).astype(BF16)
+        queries_ref[k] = pack_rows(format_queries(pad[k])).astype(BF16)
+
+
+def pair_kernel(own_ref, sibling_ref, out_ref):
+    half = own_ref.shape[0]
+    out_ref[:half] = own_ref[...]
+    out_ref[half:] = sibling_ref[...]
+
+
+def gather_kernel(*refs):
+    for i, ref in enumerate(refs[:-1]):
+        refs[-1][i] = ref[...]
 
 
 def own_kernel(chips, each, shifts, held, *refs):
@@ -251,7 +255,8 @@
             & (column < POSITIONS + count)
             & (column - POSITIONS <= position)
         )
-        got = attend(query_ref[k], rows_ref[0, k].astype(BF16), rows_ref[1, k].astype(BF16), live)
+        query = unpack_rows(query_ref[k].astype(F32)).astype(BF16)
+        got = attend(query, rows_ref[0, k].astype(BF16), rows_ref[1, k].astype(BF16), live)
         for j in range(3):
             own_out[j, k] = got[j]
 
@@ -271,26 +276,11 @@
         request = ((chip ^ (i // each)) * 2 + core) * each + i % each
         group = group_ref[0, request]
         shift = z ^ lax.div(group, held)
-        fetched = (shift & ~1) - 1 + ((shift ^ core) & 1)
-        array = jnp.where(shift == 0, 0, jnp.where(shift == 1, shifts - 1, fetched))
+        array = jnp.where(shift < 2, shift, (shift & ~1) + ((shift ^ core) & 1))
         to = 2 * pieces + i
         table_out[to : to + 1] = jnp.full((1, 128), array * held + lax.rem(group, held), jnp.int32)
     for copy in large:
         copy.wait()
-
-
-def pair_kernel(own_ref, sibling_ref, both_ref, own_blocks_ref, queries_ref):
-    held, size = own_blocks_ref.shape[:2]
-    half = queries_ref.shape[0] // 2
-    for side, ref in enumerate((own_ref, sibling_ref)):
-        for i in range(held):
-            block = ref[i * size : (i + 1) * size]
-            both_ref[side * held + i] = block
-            if side == 0:
-                own_blocks_ref[i] = block
-        for k in range(half):
-            at = held * size + k * ROWS
-            queries_ref[side * half + k] = ref[at : at + ROWS]
 
 
 def pieces_kernel(chips, each, *refs):
@@ -307,9 +297,9 @@
         handed = j > 0 and j < chips - 1 and j % 2 == 0
         for side in range(2):
             start = (1 - side if handed else side) * each
-            queries[pl.ds(side * kept + distance * each, each)] = query_refs[j][
-                start : start + each
-            ]
+            for k in range(each):
+                query = unpack_rows(query_refs[j][start + k].astype(F32))
+                queries[side * kept + distance * each + k] = query.astype(BF16)
     queries_out[...] = queries[:kept]
     lane = lax.broadcasted_iota(jnp.int32, (1, rows), 1)
     places = [jnp.max(table_ref[i : i + 1]) for i in range(pieces)]
@@ -345,10 +335,19 @@
             out_ref[j, i] = joined[j]
 
 
-def prompts_kernel(chips, each, shifts, first_row, *refs):
+def prompts_kernel(chips, each, first_row, *refs):
     table_ref, query_ref, joined_ref = refs[:3]
-    array_refs, near_refs, out_refs = refs[3 : 2 + shifts], refs[2 + shifts : 4 + shifts], refs[4 + shifts :]
-    held, rows = near_refs[0].shape[0], near_refs[0].shape[1] // 2
+    own_ref, sibling_ref, fetched_ref, swapped_ref = refs[3:7]
+    out_refs = refs[7:]
+    held, rows = own_ref.shape[0], own_ref.shape[1] // 2
+    far = fetched_ref.shape[0] - 1
+    pairs = [
+        (lambda i: own_ref[i], lambda i: sibling_ref[i]),
+        (lambda i: fetched_ref[far, i], lambda i: swapped_ref[far, i]),
+    ]
+    for p in range(0, far, 2):
+        for ref in (fetched_ref, swapped_ref):
+            pairs.append(tuple(lambda i, ref=ref, at=p + side: ref[at, i] for side in range(2)))
     lane = lax.broadcasted_iota(jnp.int32, (1, 2 * rows), 1)
     got = []
     for i in range(chips * each):
@@ -356,9 +355,9 @@
         array, slot = lax.div(at, held), lax.rem(at, held)
 
         def block(side):
-            out = near_refs[side][slot]
-            for j, ref in enumerate(array_refs):
-                out = jnp.where(array == j, ref[side * held + slot], out)
+            out = pairs[0][side](slot)
+            for j in range(1, len(pairs)):
+                out = jnp.where(array == j, pairs[j][side](slot), out)
             return out
 
         mine, other = block(0), block(1)
@@ -403,7 +402,6 @@
         out_ref[0, n] = jnp.concatenate([row[n : n + 1] for row in rows], axis=0).astype(BF16)
 
 
-ANY = pl.BlockSpec(memory_space=pl.ANY)
 HBM = pl.BlockSpec(memory_space=pltpu.HBM)
 VMEM = pl.BlockSpec(memory_space=pltpu.VMEM)
 
@@ -474,16 +472,19 @@
     count = verified_queries.shape[1]
     block_size = 2 * block_rows
     piece_shape = (pieces, piece_rows, WIDTH)
-    parcel = call(
+    own_blocks, own_queries = call(
         parcel_kernel,
         "parcel",
-        shape((held * block_size + each * ROWS, WIDTH), BF16),
+        [
+            shape((held, block_size, WIDTH), BF16),
+            shape((each, MESSAGE, WIDTH), BF16),
+        ],
         [HBM] * 4,
         [
             pltpu.SMEM((1, held), jnp.int32),
             pltpu.VMEM(verified_queries.shape, BF16),
             pltpu.VMEM((each, POSITIONS, QUERY_HEADS * HEAD_SIZE), F32),
-            pltpu.SemaphoreType.DMA((2 + 2 * held,)),
+            pltpu.SemaphoreType.DMA((4,)),
         ],
     )(
         *(
@@ -491,18 +492,16 @@
             for x in (prompt_mask.T, shared_prompt_keys, shared_prompt_values, verified_queries)
         )
     )
-    both_blocks, own_blocks, chip_queries = call(
-        pair_kernel,
-        "pair",
-        [
-            shape((2 * held, block_size, WIDTH), BF16),
-            shape((held, block_size, WIDTH), BF16),
-            shape((2 * each, ROWS, WIDTH), BF16),
-        ],
-        [VMEM] * 2,
-    )(parcel, other_core(parcel))
-    far_blocks = [along_req(both_blocks, s, s + 1) for s in range(2, shifts, 2)]
-    near_blocks = along_req(own_blocks, 1, 1)
+    sibling_blocks, sibling_queries, later_blocks = lax.optimization_barrier(
+        (other_core(own_blocks), other_core(own_queries), own_blocks)
+    )
+    fetched = []
+    for s in range(2, shifts, 2):
+        fetched += [along_req(x, s, s + 1) for x in (own_blocks, sibling_blocks)]
+    fetched.append(along_req(later_blocks, 1, 1))
+    chip_queries = call(
+        pair_kernel, "pair", shape((2 * each, MESSAGE, WIDTH), BF16), [VMEM] * 2
+    )(own_queries, sibling_queries)
 
     own, table, keys, values = call(
         functools.partial(own_kernel, chips, each, shifts, held),
@@ -538,13 +537,13 @@
 
     queries = [chip_queries]
     for s in range(1, chips - 1, 2):
-        fetched = lax.ppermute(
+        taken = lax.ppermute(
             chip_queries,
             "blk",
             [(i, i ^ (2 * (across_cores(s, chips) if i % 2 else s))) for i in range(devices)],
         )
-        fetched = lax.optimization_barrier((fetched, table))[0]
-        queries += [fetched, other_core(fetched)]
+        taken = lax.optimization_barrier((taken, table))[0]
+        queries += [taken, other_core(taken)]
     if chips > 1:
         queries.append(other_chip(chip_queries, chips - 1))
 
@@ -561,23 +560,24 @@
             pltpu.VMEM((3, 2 * kept, ROWS, WIDTH), F32),
         ],
     )(table, *queries, keys, values)
-    near_blocks, *to_sibling = lax.optimization_barrier((near_blocks, *to_sibling))
     from_sibling = [other_core(x) for x in to_sibling]
     joined = call(join_kernel, "join", shape((3,) + wide, F32), [VMEM] * 4)(
         mine, own, *from_sibling
     )
-    block_arrays = [both_blocks]
-    for x in far_blocks:
-        x = lax.optimization_barrier((x, joined))[0]
-        block_arrays += [x, other_core(x)]
-    block_arrays += [near_blocks, other_core(near_blocks)]
+    fetched = lax.optimization_barrier((kept_queries, *fetched))[1:]
+    gathered = call(
+        gather_kernel,
+        "gather",
+        shape((len(fetched), held, block_size, WIDTH), BF16),
+        [VMEM] * len(fetched),
+    )(*fetched)
 
     messages = call(
-        functools.partial(prompts_kernel, chips, each, shifts, 2 * pieces),
+        functools.partial(prompts_kernel, chips, each, 2 * pieces),
         "prompts",
         [shape((each, MESSAGE, WIDTH), F32)] * chips,
-        [VMEM] * (4 + shifts),
-    )(table, kept_queries, joined, *block_arrays)
+        [VMEM] * 7,
+    )(table, kept_queries, joined, own_blocks, sibling_blocks, gathered, other_core(gathered))
     arrived = [messages[0]] + [other_chip(messages[s], s) for s in range(1, chips)]
 
     out = call(

time: 32.2 us -> 31.8 us (0.988)
  waiting for transfers between devices: 9.59 us -> 8.68 us
  starting transfers between devices: 13.8 us -> 14.3 us
    ppermute x6, waiting for transfers between devices: 3.19 us -> 1.52 us  [other_core(): return lax.ppermute(x, 'blk', [(i, i ^ 1) for i in range(devices)])]
    ppermute x2 -> x3, waiting for transfers between devices: 0.6 us -> 1.52 us  [along_req(): return lax.ppermute(x, ('blk', 'req'), pairs)]
    ppermute x2 -> x3, starting transfers between devices: 5.59 us -> 6.46 us  [along_req(): return lax.ppermute(x, ('blk', 'req'), pairs)]
    ppermute x6, starting transfers between devices: 1.67 us -> 1.31 us  [other_core(): return lax.ppermute(x, 'blk', [(i, i ^ 1) for i in range(devices)])]
    pallas_call x3 -> x4, Pallas kernels: 3.18 us -> 3.14 us  [the longest x1 2.09 us: per_device(): call(functools.partial(prompts_kernel, chips, each, 2 * pieces), 'prompts...]
  transfers between devices with their start and end apart: 13 -> 14, of which waited for: 9 -> 8; matrix products, arithmetic and copies ran while one was open for 0% -> 0% of each run, Pallas kernels for 13% -> 14%
where the time goes in v3:
time: 31.8 us; the launch traced here: 31.6 us
  starting transfers between devices  14.3 us (45%)
  waiting for transfers between devices  8.68 us (27%)
  Pallas kernels  8.49 us (27%)
    ppermute x3, starting transfers between devices, along_req(): return lax.ppermute(x, ('blk', 'req'), pairs)  6.46 us
    ppermute x4, waiting for transfers between devices, other_chip(): return lax.ppermute(x, 'blk', [(i, i ^ 2 * s) for i in range(devices)])  5.63 us
    ppermute x4, starting transfers between devices, other_chip(): return lax.ppermute(x, 'blk', [(i, i ^ 2 * s) for i in range(devices)])  5.04 us
    pallas_call x1, Pallas kernels, per_device(): call(functools.partial(own_kernel, chips, each, shifts, held), 'own', [sh...  2.28 us
    pallas_call x1, Pallas kernels, per_device(): call(functools.partial(prompts_kernel, chips, each, 2 * pieces), 'prompts...  2.09 us
    pallas_call x1, Pallas kernels, per_device(): call(functools.partial(pieces_kernel, chips, each), 'pieces', [shape((3,)...  1.75 us
    ppermute x6, waiting for transfers between devices, other_core(): return lax.ppermute(x, 'blk', [(i, i ^ 1) for i in range(devices)])  1.52 us
    ppermute x3, waiting for transfers between devices, along_req(): return lax.ppermute(x, ('blk', 'req'), pairs)  1.52 us
  transfers between devices with their start and end apart: 14, of which 8 were waited for; matrix products, arithmetic and copies ran while one was open for 0% of the time, Pallas kernels for 14%

profile of v3, /device:TPU:0, one launch (start us, length us, event | category | flops | bytes accessed | tf_op | source)
XLA Modules:
  0.0 31.6 jit_solution(6457185569788405045)
XLA Ops:
  0.0 1.0 %parcel.1 = (bf16[4,64,256]{2,1,0:T(8,128)(2,1)S(1)}, bf16[2,24,256]{2,1,0:T(8,128)(2,1)S(1)}) custom-call(s32[1,4]{1,0:T(1,128)} %bitcast.12, bf16[4,32,256]{2,1,0:T(8,128)(2,1)} %keys_hbm.1, bf16[4,32,256]{2,1,0:T(8,128)(2,1)} %values_hbm.1, bf16[1,5,2,1024]{3,2,1,0:T(2,128)(2,1)} %bitcast.7), custom_call_target="tpu_custom_call" | custom-call | tf_op jit(solution)/shard_map/parcel/pallas_call | solution.py:475
  1.0 0.5 %collective-permute-start = (bf16[4,64,256]{2,1,0:T(8,128)(2,1)S(1)}, bf16[4,64,256]{2,1,0:T(8,128)(2,1)S(1)}, u32[]{:S(2)}, u32[]{:S(2)}) collective-permute-start(bf16[4,64,256]{2,1,0:T(8,128)(2,1)S(1)} %get-tuple-element.39.refs_3_), channel_id=1, source_target_pairs={{0,4},{4,0},{8,12},{12,8},{16,20},{20,16},{24,28},{28,24},{1,5},{5... | collective-permute-start | bytes 393224 | tf_op jit(solution)/shard_map/ppermute | solution.py:453
  1.5 0.1 collective-permute-start.1
  1.6 4.0 %collective-permute-start.7 = (bf16[4,64,256]{2,1,0:T(8,128)(2,1)S(1)}, bf16[4,64,256]{2,1,0:T(8,128)(2,1)S(1)}, u32[]{:S(2)}, u32[]{:S(2)}) collective-permute-start(bf16[4,64,256]{2,1,0:T(8,128)(2,1)S(1)} %get-tuple-element.39.refs_3_), channel_id=1, source_target_pairs={{0,2},{1,3},{2,0},{3,1},{4,7},{5,6},{6,5},{7,4},{8,10},{9,11},{10,... | collective-permute-start | bytes 393224 | tf_op jit(solution)/shard_map/ppermute | solution.py:463
  5.6 0.0 collective-permute-done.1.sibling_ref
  5.6 0.0 collective-permute-done.refs_4_
  5.6 0.9 %collective-permute-start.8 = (bf16[4,64,256]{2,1,0:T(8,128)(2,1)S(1)}, bf16[4,64,256]{2,1,0:T(8,128)(2,1)S(1)}, u32[]{:S(2)}, u32[]{:S(2)}) collective-permute-start(bf16[4,64,256]{2,1,0:T(8,128)(2,1)S(1)} %collective-permute-done.refs_4_), channel_id=1, source_target_pairs={{0,2},{1,3},{2,0},{3,1},{4,7},{5,6},{6,5},{7,4},{8,10},{9,11},{10,... | collective-permute-start | bytes 393224 | tf_op jit(solution)/shard_map/ppermute | solution.py:463
  6.5 1.6 %collective-permute-start.9 = (bf16[4,64,256]{2,1,0:T(8,128)(2,1)S(1)}, bf16[4,64,256]{2,1,0:T(8,128)(2,1)S(1)}, u32[]{:S(2)}, u32[]{:S(2)}) collective-permute-start(bf16[4,64,256]{2,1,0:T(8,128)(2,1)S(1)} %get-tuple-element.39.refs_3_), channel_id=1, source_target_pairs={{0,1},{1,0},{2,3},{3,2},{4,5},{5,4},{6,7},{7,6},{8,9},{9,8},{10,11... | collective-permute-start | bytes 393224 | tf_op jit(solution)/shard_map/ppermute | solution.py:463
  8.1 1.5 %collective-permute-start.2 = (bf16[4,24,256]{2,1,0:T(8,128)(2,1)S(1)}, bf16[4,24,256]{2,1,0:T(8,128)(2,1)S(1)}, u32[]{:S(2)}, u32[]{:S(2)}) collective-permute-start(bf16[4,24,256]{2,1,0:T(8,128)(2,1)S(1)} %pair.1.refs_10_.refs_1_), channel_id=1, source_target_pairs={{0,8},{4,20},{8,0},{12,28},{16,24},{20,4},{24,16},{28,12},{1,9},{5... | collective-permute-start | bytes 147464 | tf_op jit(solution)/shard_map/ppermute | solution.py:540
  9.6 1.5 %collective-permute-start.4 = (bf16[4,24,256]{2,1,0:T(8,128)(2,1)S(1)}, bf16[4,24,256]{2,1,0:T(8,128)(2,1)S(1)}, u32[]{:S(2)}, u32[]{:S(2)}) collective-permute-start(bf16[4,24,256]{2,1,0:T(8,128)(2,1)S(1)} %pair.1.refs_10_.refs_1_), channel_id=1, source_target_pairs={{0,24},{4,28},{8,16},{12,20},{16,8},{20,12},{24,0},{28,4},{1,25},{... | collective-permute-start | bytes 147464 | tf_op jit(solution)/shard_map/ppermute | solution.py:456
  11.1 2.3 %own.1 = (f32[3,2,32,256]{3,2,1,0:T(8,128)S(1)}, s32[24,128]{1,0:T(8,128)S(1)}, bf16[8,256,256]{2,1,0:T(8,128)(2,1)S(1)}, bf16[8,256,256]{2,1,0:T(8,128)(2,1)S(1)}) custom-call(s32[1,64]{1,0:T(1,128)} %refs_0_.1, s32[1,16]{1,0:T(1,128)} %refs_1_.1, s32[1,2]{1,0:T(1,128)} %refs_2_.1, s32[1,16]{1,0:T(1,128)} %refs_3_.1, bf16[1,5,2,256]{3,2,1,0:T(2,128)(2,1)} %bitcast.8, ...), custom_call_target="tpu_custom_call" | custom-call | bytes 8388608 | tf_op jit(solution)/shard_map/own/pallas_call | solution.py:506
  13.4 0.0 collective-permute-done.2.refs_2_
  13.4 0.1 collective-permute-start.3
  13.5 1.1 %collective-permute-done.4.refs_4_ = bf16[4,24,256]{2,1,0:T(8,128)(2,1)S(1)} collective-permute-done((bf16[4,24,256]{2,1,0:T(8,128)(2,1)S(1)}, bf16[4,24,256]{2,1,0:T(8,128)(2,1)S(1)}, u32[]{:S(2)}, u32[]{:S(2)}) %collective-permute-start.4) | collective-permute-done | bytes 49184 | tf_op jit(solution)/shard_map/ppermute | solution.py:456
  14.6 0.1 collective-permute-done.3.refs_3_
  14.7 1.8 %pieces.1 = (f32[3,8,32,256]{3,2,1,0:T(8,128)S(1)}, f32[4,24,256]{2,1,0:T(8,128)S(1)}, f32[4,24,256]{2,1,0:T(8,128)S(1)}, bf16[8,32,256]{2,1,0:T(8,128)(2,1)S(1)}) custom-call(s32[24,128]{1,0:T(8,128)S(1)} %get-tuple-element.29.refs_0_, bf16[4,24,256]{2,1,0:T(8,128)(2,1)S(1)} %pair.1.refs_10_.refs_1_, ...), custom_call_target="tpu_custom_call" | custom-call | tf_op jit(solution)/shard_map/pieces/pallas_call | solution.py:551
  16.5 1.5 %collective-permute-done.8.refs_1_ = bf16[4,64,256]{2,1,0:T(8,128)(2,1)S(1)} collective-permute-done((bf16[4,64,256]{2,1,0:T(8,128)(2,1)S(1)}, bf16[4,64,256]{2,1,0:T(8,128)(2,1)S(1)}, u32[]{:S(2)}, u32[]{:S(2)}) %collective-permute-start.8) | collective-permute-done | bytes 131104 | tf_op jit(solution)/shard_map/ppermute | solution.py:463
  18.0 0.1 collective-permute-start.10
  18.1 0.5 %collective-permute-start.5 = (f32[4,24,256]{2,1,0:T(8,128)S(1)}, f32[4,24,256]{2,1,0:T(8,128)S(1)}, u32[]{:S(2)}, u32[]{:S(2)}) collective-permute-start(f32[4,24,256]{2,1,0:T(8,128)S(1)} %get-tuple-element.36), channel_id=1, source_target_pairs={{0,4},{4,0},{8,12},{12,8},{16,20},{20,16},{24,28},{28,24},{1,5},{5... | collective-permute-start | bytes 294920 | tf_op jit(solution)/shard_map/ppermute | solution.py:453
  18.6 0.1 collective-permute-start.6
  18.7 1.3 %collective-permute-done.5.first_ref = f32[4,24,256]{2,1,0:T(8,128)S(1)} collective-permute-done((f32[4,24,256]{2,1,0:T(8,128)S(1)}, f32[4,24,256]{2,1,0:T(8,128)S(1)}, u32[]{:S(2)}, u32[]{:S(2)}) %collective-permute-start.5) | collective-permute-done | bytes 98336 | tf_op jit(solution)/shard_map/ppermute | solution.py:453
  19.9 0.1 collective-permute-done.6.second_ref
  20.1 0.3 join.1.refs_2_
  20.4 0.0 collective-permute-done.10.refs_6_
  20.4 2.1 %prompts.1 = (f32[2,24,256]{2,1,0:T(8,128)S(1)}, f32[2,24,256]{2,1,0:T(8,128)S(1)}, f32[2,24,256]{2,1,0:T(8,128)S(1)}, f32[2,24,256]{2,1,0:T(8,128)S(1)}) custom-call(s32[24,128]{1,0:T(8,128)S(1)} %get-tuple-element.29.refs_0_, bf16[8,32,256]{2,1,0:T(8,128)(2,1)S(1)} %get-tuple-element.33.refs_1_, f32[3,8,32,256]{3,2,1,0:T(8,128)S(1)} %join.1.refs_2_, ...), custom_call_target="tpu_custom_call" | custom-call | tf_op jit(solution)/shard_map/prompts/pallas_call | solution.py:575
  22.5 1.6 %collective-permute-start.11 = (f32[2,24,256]{2,1,0:T(8,128)S(1)}, f32[2,24,256]{2,1,0:T(8,128)S(1)}, u32[]{:S(2)}, u32[]{:S(2)}) collective-permute-start(f32[2,24,256]{2,1,0:T(8,128)S(1)} %get-tuple-element.44), channel_id=1, source_target_pairs={{0,8},{4,12},{8,0},{12,4},{16,24},{20,28},{24,16},{28,20},{1,9},{5... | collective-permute-start | bytes 147464 | tf_op jit(solution)/shard_map/ppermute | solution.py:456
  24.1 1.5 %collective-permute-start.12 = (f32[2,24,256]{2,1,0:T(8,128)S(1)}, f32[2,24,256]{2,1,0:T(8,128)S(1)}, u32[]{:S(2)}, u32[]{:S(2)}) collective-permute-start(f32[2,24,256]{2,1,0:T(8,128)S(1)} %get-tuple-element.45), channel_id=1, source_target_pairs={{0,16},{4,20},{8,24},{12,28},{16,0},{20,4},{24,8},{28,12},{1,17},{... | collective-permute-start | bytes 147464 | tf_op jit(solution)/shard_map/ppermute | solution.py:456
  25.6 0.5 %collective-permute-start.13 = (f32[2,24,256]{2,1,0:T(8,128)S(1)}, f32[2,24,256]{2,1,0:T(8,128)S(1)}, u32[]{:S(2)}, u32[]{:S(2)}) collective-permute-start(f32[2,24,256]{2,1,0:T(8,128)S(1)} %get-tuple-element.46), channel_id=1, source_target_pairs={{0,24},{4,28},{8,16},{12,20},{16,8},{20,12},{24,0},{28,4},{1,25},{... | collective-permute-start | bytes 147464 | tf_op jit(solution)/shard_map/ppermute | solution.py:456
  26.1 0.6 %collective-permute-done.11.refs_1_ = f32[2,24,256]{2,1,0:T(8,128)S(1)} collective-permute-done((f32[2,24,256]{2,1,0:T(8,128)S(1)}, f32[2,24,256]{2,1,0:T(8,128)S(1)}, u32[]{:S(2)}, u32[]{:S(2)}) %collective-permute-start.11) | collective-permute-done | bytes 49184 | tf_op jit(solution)/shard_map/ppermute | solution.py:456
  26.7 1.5 %collective-permute-done.12.refs_2_ = f32[2,24,256]{2,1,0:T(8,128)S(1)} collective-permute-done((f32[2,24,256]{2,1,0:T(8,128)S(1)}, f32[2,24,256]{2,1,0:T(8,128)S(1)}, u32[]{:S(2)}, u32[]{:S(2)}) %collective-permute-start.12) | collective-permute-done | bytes 49184 | tf_op jit(solution)/shard_map/ppermute | solution.py:456
  28.2 2.4 %collective-permute-done.13.refs_3_ = f32[2,24,256]{2,1,0:T(8,128)S(1)} collective-permute-done((f32[2,24,256]{2,1,0:T(8,128)S(1)}, f32[2,24,256]{2,1,0:T(8,128)S(1)}, u32[]{:S(2)}, u32[]{:S(2)}) %collective-permute-start.13) | collective-permute-done | bytes 49184 | tf_op jit(solution)/shard_map/ppermute | solution.py:456
  30.6 1.0 %combine.1 = bf16[1,5,2,1024]{3,2,1,0:T(2,128)(2,1)} custom-call(f32[2,24,256]{2,1,0:T(8,128)S(1)} %get-tuple-element.43.refs_0_, f32[2,24,256]{2,1,0:T(8,128)S(1)} %collective-permute-done.11.refs_1_, f32[2,24,256]{2,1,0:T(8,128)S(1)} %collective-permute-done.12.refs_2_, f32[2,24,256]{2,1,0:T(8,128)S(1)} %collective-permute-done.13.refs_3_), custom_call_target="tpu_custom_call" | custom-call | tf_op jit(solution)/shard_map/combine/pallas_call | solution.py:583
  (4 shorter events, 0.0 us)
Async XLA Ops:
  1.0 4.6 %collective-permute-start = (bf16[4,64,256]{2,1,0:T(8,128)(2,1)S(1)}, bf16[4,64,256]{2,1,0:T(8,128)(2,1)S(1)}, u32[]{:S(2)}, u32[]{:S(2)}) collective-permute-start(bf16[4,64,256]{2,1,0:T(8,128)(2,1)S(1)} %get-tuple-element.39.refs_3_), channel_id=1, source_target_pairs={{0,4},{4,0},{8,12},{12,8},{16,20},{20,16},{24,28},{28,24},{1,5},{5... | collective-permute-start | bytes 393224 | tf_op jit(solution)/shard_map/ppermute | solution.py:453
  1.5 4.1 %collective-permute-start.1 = (bf16[2,24,256]{2,1,0:T(8,128)(2,1)S(1)}, bf16[2,24,256]{2,1,0:T(8,128)(2,1)S(1)}, u32[]{:S(2)}, u32[]{:S(2)}) collective-permute-start(bf16[2,24,256]{2,1,0:T(8,128)(2,1)S(1)} %get-tuple-element.26.own_ref), channel_id=1, source_target_pairs={{0,4},{4,0},{8,12},{12,8},{16,20},{20,16},{24,28},{28,24},{1,5},{5... | collective-permute-start | bytes 73736 | tf_op jit(solution)/shard_map/ppermute | solution.py:453
  1.6 14.8 %collective-permute-start.7 = (bf16[4,64,256]{2,1,0:T(8,128)(2,1)S(1)}, bf16[4,64,256]{2,1,0:T(8,128)(2,1)S(1)}, u32[]{:S(2)}, u32[]{:S(2)}) collective-permute-start(bf16[4,64,256]{2,1,0:T(8,128)(2,1)S(1)} %get-tuple-element.39.refs_3_), channel_id=1, source_target_pairs={{0,2},{1,3},{2,0},{3,1},{4,7},{5,6},{6,5},{7,4},{8,10},{9,11},{10,... | collective-permute-start | bytes 393224 | tf_op jit(solution)/shard_map/ppermute | solution.py:463
  5.6 12.3 %collective-permute-start.8 = (bf16[4,64,256]{2,1,0:T(8,128)(2,1)S(1)}, bf16[4,64,256]{2,1,0:T(8,128)(2,1)S(1)}, u32[]{:S(2)}, u32[]{:S(2)}) collective-permute-start(bf16[4,64,256]{2,1,0:T(8,128)(2,1)S(1)} %collective-permute-done.refs_4_), channel_id=1, source_target_pairs={{0,2},{1,3},{2,0},{3,1},{4,7},{5,6},{6,5},{7,4},{8,10},{9,11},{10,... | collective-permute-start | bytes 393224 | tf_op jit(solution)/shard_map/ppermute | solution.py:463
  6.5 11.5 %collective-permute-start.9 = (bf16[4,64,256]{2,1,0:T(8,128)(2,1)S(1)}, bf16[4,64,256]{2,1,0:T(8,128)(2,1)S(1)}, u32[]{:S(2)}, u32[]{:S(2)}) collective-permute-start(bf16[4,64,256]{2,1,0:T(8,128)(2,1)S(1)} %get-tuple-element.39.refs_3_), channel_id=1, source_target_pairs={{0,1},{1,0},{2,3},{3,2},{4,5},{5,4},{6,7},{7,6},{8,9},{9,8},{10,11... | collective-permute-start | bytes 393224 | tf_op jit(solution)/shard_map/ppermute | solution.py:463
  8.1 5.3 %collective-permute-start.2 = (bf16[4,24,256]{2,1,0:T(8,128)(2,1)S(1)}, bf16[4,24,256]{2,1,0:T(8,128)(2,1)S(1)}, u32[]{:S(2)}, u32[]{:S(2)}) collective-permute-start(bf16[4,24,256]{2,1,0:T(8,128)(2,1)S(1)} %pair.1.refs_10_.refs_1_), channel_id=1, source_target_pairs={{0,8},{4,20},{8,0},{12,28},{16,24},{20,4},{24,16},{28,12},{1,9},{5... | collective-permute-start | bytes 147464 | tf_op jit(solution)/shard_map/ppermute | solution.py:540
  9.6 5.0 %collective-permute-start.4 = (bf16[4,24,256]{2,1,0:T(8,128)(2,1)S(1)}, bf16[4,24,256]{2,1,0:T(8,128)(2,1)S(1)}, u32[]{:S(2)}, u32[]{:S(2)}) collective-permute-start(bf16[4,24,256]{2,1,0:T(8,128)(2,1)S(1)} %pair.1.refs_10_.refs_1_), channel_id=1, source_target_pairs={{0,24},{4,28},{8,16},{12,20},{16,8},{20,12},{24,0},{28,4},{1,25},{... | collective-permute-start | bytes 147464 | tf_op jit(solution)/shard_map/ppermute | solution.py:456
  13.4 1.3 %collective-permute-start.3 = (bf16[4,24,256]{2,1,0:T(8,128)(2,1)S(1)}, bf16[4,24,256]{2,1,0:T(8,128)(2,1)S(1)}, u32[]{:S(2)}, u32[]{:S(2)}) collective-permute-start(bf16[4,24,256]{2,1,0:T(8,128)(2,1)S(1)} %collective-permute-done.2.refs_2_), channel_id=1, source_target_pairs={{0,4},{4,0},{8,12},{12,8},{16,20},{20,16},{24,28},{28,24},{1,5},{5... | collective-permute-start | bytes 147464 | tf_op jit(solution)/shard_map/ppermute | solution.py:453
  18.0 2.4 %collective-permute-start.10 = (bf16[3,4,64,256]{3,2,1,0:T(8,128)(2,1)S(1)}, bf16[3,4,64,256]{3,2,1,0:T(8,128)(2,1)S(1)}, u32[]{:S(2)}, u32[]{:S(2)}) collective-permute-start(bf16[3,4,64,256]{3,2,1,0:T(8,128)(2,1)S(1)} %gather.1.refs_5_), channel_id=1, source_target_pairs={{0,4},{4,0},{8,12},{12,8},{16,20},{20,16},{24,28},{28,24},{1,5},{5... | collective-permute-start | bytes 1179656 | tf_op jit(solution)/shard_map/ppermute | solution.py:453
  18.1 1.9 %collective-permute-start.5 = (f32[4,24,256]{2,1,0:T(8,128)S(1)}, f32[4,24,256]{2,1,0:T(8,128)S(1)}, u32[]{:S(2)}, u32[]{:S(2)}) collective-permute-start(f32[4,24,256]{2,1,0:T(8,128)S(1)} %get-tuple-element.36), channel_id=1, source_target_pairs={{0,4},{4,0},{8,12},{12,8},{16,20},{20,16},{24,28},{28,24},{1,5},{5... | collective-permute-start | bytes 294920 | tf_op jit(solution)/shard_map/ppermute | solution.py:453
  18.6 1.5 %collective-permute-start.6 = (f32[4,24,256]{2,1,0:T(8,128)S(1)}, f32[4,24,256]{2,1,0:T(8,128)S(1)}, u32[]{:S(2)}, u32[]{:S(2)}) collective-permute-start(f32[4,24,256]{2,1,0:T(8,128)S(1)} %get-tuple-element.37), channel_id=1, source_target_pairs={{0,4},{4,0},{8,12},{12,8},{16,20},{20,16},{24,28},{28,24},{1,5},{5... | collective-permute-start | bytes 294920 | tf_op jit(solution)/shard_map/ppermute | solution.py:453
  22.5 4.2 %collective-permute-start.11 = (f32[2,24,256]{2,1,0:T(8,128)S(1)}, f32[2,24,256]{2,1,0:T(8,128)S(1)}, u32[]{:S(2)}, u32[]{:S(2)}) collective-permute-start(f32[2,24,256]{2,1,0:T(8,128)S(1)} %get-tuple-element.44), channel_id=1, source_target_pairs={{0,8},{4,12},{8,0},{12,4},{16,24},{20,28},{24,16},{28,20},{1,9},{5... | collective-permute-start | bytes 147464 | tf_op jit(solution)/shard_map/ppermute | solution.py:456
  24.1 4.1 %collective-permute-start.12 = (f32[2,24,256]{2,1,0:T(8,128)S(1)}, f32[2,24,256]{2,1,0:T(8,128)S(1)}, u32[]{:S(2)}, u32[]{:S(2)}) collective-permute-start(f32[2,24,256]{2,1,0:T(8,128)S(1)} %get-tuple-element.45), channel_id=1, source_target_pairs={{0,16},{4,20},{8,24},{12,28},{16,0},{20,4},{24,8},{28,12},{1,17},{... | collective-permute-start | bytes 147464 | tf_op jit(solution)/shard_map/ppermute | solution.py:456
  25.6 5.0 %collective-permute-start.13 = (f32[2,24,256]{2,1,0:T(8,128)S(1)}, f32[2,24,256]{2,1,0:T(8,128)S(1)}, u32[]{:S(2)}, u32[]{:S(2)}) collective-permute-start(f32[2,24,256]{2,1,0:T(8,128)S(1)} %get-tuple-element.46), channel_id=1, source_target_pairs={{0,24},{4,28},{8,16},{12,20},{16,8},{20,12},{24,0},{28,4},{1,25},{... | collective-permute-start | bytes 147464 | tf_op jit(solution)/shard_map/ppermute | solution.py:456

commit v4 on v3

--- a/solution.py
+++ b/solution.py
@@ -53,19 +53,18 @@
     )
 
 
-def weigh(weights, values):
-    ones = jnp.ones((values.shape[0], 128), BF16)
-    mass = jnp.dot(weights, ones, preferred_element_type=F32)
-    part = jnp.dot(weights, values, preferred_element_type=F32)
-    return jnp.concatenate([mass, mass], axis=1), part
-
-
-def attend(q, keys, values, live):
+def attend(q, keys, values, live, wide):
     masked = jnp.where(live, score(q, keys), LOWEST)
     top = jnp.max(masked, axis=1, keepdims=True)
     weights = jnp.exp(masked - top).astype(BF16)
-    mass, part = weigh(weights, values)
-    return fold_heads(top), fold_heads(mass), fold_heads(part)
+    if wide:
+        values = jnp.concatenate([values, jnp.ones((values.shape[0], 128), BF16)], axis=1)
+    part = jnp.dot(weights, values, preferred_element_type=F32)
+    if wide:
+        mass = jnp.concatenate([part[:, WIDTH:]] * 2, axis=1)
+    else:
+        mass = jnp.sum(weights.astype(F32), axis=1, keepdims=True)
+    return fold_heads(top), fold_heads(mass), fold_heads(part[:, :WIDTH])
 
 
 def merge(*blocks):
@@ -256,7 +255,7 @@
             & (column - POSITIONS <= position)
         )
         query = unpack_rows(query_ref[k].astype(F32)).astype(BF16)
-        got = attend(query, rows_ref[0, k].astype(BF16), rows_ref[1, k].astype(BF16), live)
+        got = attend(query, rows_ref[0, k].astype(BF16), rows_ref[1, k].astype(BF16), live, False)
         for j in range(3):
             own_out[j, k] = got[j]
 
@@ -307,7 +306,7 @@
     for i in range(pieces):
         filled = table_ref[pieces + i : pieces + i + 1]
         live = lane < jnp.concatenate([filled] * (rows // 128), axis=1)
-        got.append(attend(queries[places[i]], keys[i], values[i], live))
+        got.append(attend(queries[places[i]], keys[i], values[i], live, True))
     acc[0] = jnp.full_like(acc[0], LOWEST)
     acc[1] = jnp.zeros_like(acc[1])
     acc[2] = jnp.zeros_like(acc[2])
@@ -368,6 +367,7 @@
                 jnp.concatenate([mine[:rows], other[:rows]], axis=0),
                 jnp.concatenate([mine[rows:], other[rows:]], axis=0),
                 marks < 0.5 * DEAD_MARK,
+                False,
             )
         )
     for i in range(chips * each):
@@ -578,7 +578,7 @@
         [shape((each, MESSAGE, WIDTH), F32)] * chips,
         [VMEM] * 7,
     )(table, kept_queries, joined, own_blocks, sibling_blocks, gathered, other_core(gathered))
-    arrived = [messages[0]] + [other_chip(messages[s], s) for s in range(1, chips)]
+    arrived = [messages[0]] + [other_chip(messages[s], s) for s in range(chips - 1, 0, -1)]
 
     out = call(
         functools.partial(combine_kernel, chips),

time: 31.8 us -> 30 us (0.943)
  Pallas kernels: 8.49 us -> 7.42 us
  waiting for transfers between devices: 8.68 us -> 7.97 us
    ppermute x4, waiting for transfers between devices: 5.63 us -> 4.71 us  [other_chip(): return lax.ppermute(x, 'blk', [(i, i ^ 2 * s) for i in range(devices)])]
    pallas_call x1, Pallas kernels: 2.09 us -> 1.27 us  [per_device(): call(functools.partial(prompts_kernel, chips, each, 2 * pieces), 'prompts...]
where the time goes in v4:
time: 30 us; the launch traced here: 29.8 us
  starting transfers between devices  14.3 us (48%)
  waiting for transfers between devices  7.97 us (27%)
  Pallas kernels  7.42 us (25%)
    ppermute x3, starting transfers between devices, along_req(): return lax.ppermute(x, ('blk', 'req'), pairs)  6.46 us
    ppermute x4, starting transfers between devices, other_chip(): return lax.ppermute(x, 'blk', [(i, i ^ 2 * s) for i in range(devices)])  5.04 us
    ppermute x4, waiting for transfers between devices, other_chip(): return lax.ppermute(x, 'blk', [(i, i ^ 2 * s) for i in range(devices)])  4.71 us
    pallas_call x1, Pallas kernels, per_device(): call(functools.partial(own_kernel, chips, each, shifts, held), 'own', [sh...  2.24 us
    ppermute x3, waiting for transfers between devices, along_req(): return lax.ppermute(x, ('blk', 'req'), pairs)  1.77 us
    pallas_call x1, Pallas kernels, per_device(): call(functools.partial(pieces_kernel, chips, each), 'pieces', [shape((3,)...  1.55 us
    ppermute x1, starting transfers between devices, per_device(): lax.ppermute(chip_queries, 'blk', [(i, i ^ 2 * (across_cores(s, chips) if...  1.49 us
    ppermute x6, waiting for transfers between devices, other_core(): return lax.ppermute(x, 'blk', [(i, i ^ 1) for i in range(devices)])  1.48 us
  transfers between devices with their start and end apart: 14, of which 8 were waited for; matrix products, arithmetic and copies ran while one was open for 0% of the time, Pallas kernels for 14%

profile of v4, /device:TPU:0, one launch (start us, length us, event | category | flops | bytes accessed | tf_op | source)
XLA Modules:
  0.0 29.8 jit_solution(703166408080309881)
XLA Ops:
  0.0 1.0 %parcel.1 = (bf16[4,64,256]{2,1,0:T(8,128)(2,1)S(1)}, bf16[2,24,256]{2,1,0:T(8,128)(2,1)S(1)}) custom-call(s32[1,4]{1,0:T(1,128)} %bitcast.12, bf16[4,32,256]{2,1,0:T(8,128)(2,1)} %keys_hbm.1, bf16[4,32,256]{2,1,0:T(8,128)(2,1)} %values_hbm.1, bf16[1,5,2,1024]{3,2,1,0:T(2,128)(2,1)} %bitcast.7), custom_call_target="tpu_custom_call" | custom-call | tf_op jit(solution)/shard_map/parcel/pallas_call | solution.py:475
  1.0 0.5 %collective-permute-start = (bf16[4,64,256]{2,1,0:T(8,128)(2,1)S(1)}, bf16[4,64,256]{2,1,0:T(8,128)(2,1)S(1)}, u32[]{:S(2)}, u32[]{:S(2)}) collective-permute-start(bf16[4,64,256]{2,1,0:T(8,128)(2,1)S(1)} %get-tuple-element.39.refs_3_), channel_id=1, source_target_pairs={{0,4},{4,0},{8,12},{12,8},{16,20},{20,16},{24,28},{28,24},{1,5},{5... | collective-permute-start | bytes 393224 | tf_op jit(solution)/shard_map/ppermute | solution.py:453
  1.5 0.1 collective-permute-start.1
  1.6 4.0 %collective-permute-start.7 = (bf16[4,64,256]{2,1,0:T(8,128)(2,1)S(1)}, bf16[4,64,256]{2,1,0:T(8,128)(2,1)S(1)}, u32[]{:S(2)}, u32[]{:S(2)}) collective-permute-start(bf16[4,64,256]{2,1,0:T(8,128)(2,1)S(1)} %get-tuple-element.39.refs_3_), channel_id=1, source_target_pairs={{0,2},{1,3},{2,0},{3,1},{4,7},{5,6},{6,5},{7,4},{8,10},{9,11},{10,... | collective-permute-start | bytes 393224 | tf_op jit(solution)/shard_map/ppermute | solution.py:463
  5.6 0.0 collective-permute-done.1.sibling_ref
  5.6 0.0 collective-permute-done.refs_4_
  5.6 0.9 %collective-permute-start.8 = (bf16[4,64,256]{2,1,0:T(8,128)(2,1)S(1)}, bf16[4,64,256]{2,1,0:T(8,128)(2,1)S(1)}, u32[]{:S(2)}, u32[]{:S(2)}) collective-permute-start(bf16[4,64,256]{2,1,0:T(8,128)(2,1)S(1)} %collective-permute-done.refs_4_), channel_id=1, source_target_pairs={{0,2},{1,3},{2,0},{3,1},{4,7},{5,6},{6,5},{7,4},{8,10},{9,11},{10,... | collective-permute-start | bytes 393224 | tf_op jit(solution)/shard_map/ppermute | solution.py:463
  6.5 1.6 %collective-permute-start.9 = (bf16[4,64,256]{2,1,0:T(8,128)(2,1)S(1)}, bf16[4,64,256]{2,1,0:T(8,128)(2,1)S(1)}, u32[]{:S(2)}, u32[]{:S(2)}) collective-permute-start(bf16[4,64,256]{2,1,0:T(8,128)(2,1)S(1)} %get-tuple-element.39.refs_3_), channel_id=1, source_target_pairs={{0,1},{1,0},{2,3},{3,2},{4,5},{5,4},{6,7},{7,6},{8,9},{9,8},{10,11... | collective-permute-start | bytes 393224 | tf_op jit(solution)/shard_map/ppermute | solution.py:463
  8.1 1.5 %collective-permute-start.2 = (bf16[4,24,256]{2,1,0:T(8,128)(2,1)S(1)}, bf16[4,24,256]{2,1,0:T(8,128)(2,1)S(1)}, u32[]{:S(2)}, u32[]{:S(2)}) collective-permute-start(bf16[4,24,256]{2,1,0:T(8,128)(2,1)S(1)} %pair.1.refs_10_.refs_1_), channel_id=1, source_target_pairs={{0,8},{4,20},{8,0},{12,28},{16,24},{20,4},{24,16},{28,12},{1,9},{5... | collective-permute-start | bytes 147464 | tf_op jit(solution)/shard_map/ppermute | solution.py:540
  9.6 1.5 %collective-permute-start.4 = (bf16[4,24,256]{2,1,0:T(8,128)(2,1)S(1)}, bf16[4,24,256]{2,1,0:T(8,128)(2,1)S(1)}, u32[]{:S(2)}, u32[]{:S(2)}) collective-permute-start(bf16[4,24,256]{2,1,0:T(8,128)(2,1)S(1)} %pair.1.refs_10_.refs_1_), channel_id=1, source_target_pairs={{0,24},{4,28},{8,16},{12,20},{16,8},{20,12},{24,0},{28,4},{1,25},{... | collective-permute-start | bytes 147464 | tf_op jit(solution)/shard_map/ppermute | solution.py:456
  11.1 2.2 %own.1 = (f32[3,2,32,256]{3,2,1,0:T(8,128)S(1)}, s32[24,128]{1,0:T(8,128)S(1)}, bf16[8,256,256]{2,1,0:T(8,128)(2,1)S(1)}, bf16[8,256,256]{2,1,0:T(8,128)(2,1)S(1)}) custom-call(s32[1,64]{1,0:T(1,128)} %refs_0_.1, s32[1,16]{1,0:T(1,128)} %refs_1_.1, s32[1,2]{1,0:T(1,128)} %refs_2_.1, s32[1,16]{1,0:T(1,128)} %refs_3_.1, bf16[1,5,2,256]{3,2,1,0:T(2,128)(2,1)} %bitcast.8, ...), custom_call_target="tpu_custom_call" | custom-call | bytes 8388608 | tf_op jit(solution)/shard_map/own/pallas_call | solution.py:506
  13.3 0.0 collective-permute-done.2.refs_2_
  13.3 0.1 collective-permute-start.3
  13.4 1.2 %collective-permute-done.4.refs_4_ = bf16[4,24,256]{2,1,0:T(8,128)(2,1)S(1)} collective-permute-done((bf16[4,24,256]{2,1,0:T(8,128)(2,1)S(1)}, bf16[4,24,256]{2,1,0:T(8,128)(2,1)S(1)}, u32[]{:S(2)}, u32[]{:S(2)}) %collective-permute-start.4) | collective-permute-done | bytes 49184 | tf_op jit(solution)/shard_map/ppermute | solution.py:456
  14.6 0.1 collective-permute-done.3.refs_3_
  14.6 1.5 %pieces.1 = (f32[3,8,32,256]{3,2,1,0:T(8,128)S(1)}, f32[4,24,256]{2,1,0:T(8,128)S(1)}, f32[4,24,256]{2,1,0:T(8,128)S(1)}, bf16[8,32,256]{2,1,0:T(8,128)(2,1)S(1)}) custom-call(s32[24,128]{1,0:T(8,128)S(1)} %get-tuple-element.29.refs_0_, bf16[4,24,256]{2,1,0:T(8,128)(2,1)S(1)} %pair.1.refs_10_.refs_1_, ...), custom_call_target="tpu_custom_call" | custom-call | tf_op jit(solution)/shard_map/pieces/pallas_call | solution.py:551
  16.2 0.0 collective-permute-done.7.refs_0_
  16.2 1.8 %collective-permute-done.8.refs_1_ = bf16[4,64,256]{2,1,0:T(8,128)(2,1)S(1)} collective-permute-done((bf16[4,64,256]{2,1,0:T(8,128)(2,1)S(1)}, bf16[4,64,256]{2,1,0:T(8,128)(2,1)S(1)}, u32[]{:S(2)}, u32[]{:S(2)}) %collective-permute-start.8) | collective-permute-done | bytes 131104 | tf_op jit(solution)/shard_map/ppermute | solution.py:463
  18.0 0.1 collective-permute-start.10
  18.1 0.5 %collective-permute-start.5 = (f32[4,24,256]{2,1,0:T(8,128)S(1)}, f32[4,24,256]{2,1,0:T(8,128)S(1)}, u32[]{:S(2)}, u32[]{:S(2)}) collective-permute-start(f32[4,24,256]{2,1,0:T(8,128)S(1)} %get-tuple-element.36), channel_id=1, source_target_pairs={{0,4},{4,0},{8,12},{12,8},{16,20},{20,16},{24,28},{28,24},{1,5},{5... | collective-permute-start | bytes 294920 | tf_op jit(solution)/shard_map/ppermute | solution.py:453
  18.6 0.1 collective-permute-start.6
  18.7 1.3 %collective-permute-done.5.first_ref = f32[4,24,256]{2,1,0:T(8,128)S(1)} collective-permute-done((f32[4,24,256]{2,1,0:T(8,128)S(1)}, f32[4,24,256]{2,1,0:T(8,128)S(1)}, u32[]{:S(2)}, u32[]{:S(2)}) %collective-permute-start.5) | collective-permute-done | bytes 98336 | tf_op jit(solution)/shard_map/ppermute | solution.py:453
  19.9 0.1 collective-permute-done.6.second_ref
  20.1 0.3 %join.1.refs_2_ = f32[3,8,32,256]{3,2,1,0:T(8,128)S(1)} custom-call(f32[3,8,32,256]{3,2,1,0:T(8,128)S(1)} %get-tuple-element.34.mine_ref, f32[3,2,32,256]{3,2,1,0:T(8,128)S(1)} %get-tuple-element.35.own_ref, f32[4,24,256]{2,1,0:T(8,128)S(1)} %collective-permute-done.5.first_ref, f32[4,24,256]{2,1,0:T(8,128)S(1)} %collective-permute-done.6.second_ref), custom_call_target="tpu_custom_call" | custom-call | tf_op jit(solution)/shard_map/join/pallas_call | solution.py:564
  20.4 1.3 %prompts.1 = (f32[2,24,256]{2,1,0:T(8,128)S(1)}, f32[2,24,256]{2,1,0:T(8,128)S(1)}, f32[2,24,256]{2,1,0:T(8,128)S(1)}, f32[2,24,256]{2,1,0:T(8,128)S(1)}) custom-call(s32[24,128]{1,0:T(8,128)S(1)} %get-tuple-element.29.refs_0_, bf16[8,32,256]{2,1,0:T(8,128)(2,1)S(1)} %get-tuple-element.33.refs_1_, f32[3,8,32,256]{3,2,1,0:T(8,128)S(1)} %join.1.refs_2_, ...), custom_call_target="tpu_custom_call" | custom-call | tf_op jit(solution)/shard_map/prompts/pallas_call | solution.py:575
  21.7 2.5 %collective-permute-start.11 = (f32[2,24,256]{2,1,0:T(8,128)S(1)}, f32[2,24,256]{2,1,0:T(8,128)S(1)}, u32[]{:S(2)}, u32[]{:S(2)}) collective-permute-start(f32[2,24,256]{2,1,0:T(8,128)S(1)} %get-tuple-element.44), channel_id=1, source_target_pairs={{0,24},{4,28},{8,16},{12,20},{16,8},{20,12},{24,0},{28,4},{1,25},{... | collective-permute-start | bytes 147464 | tf_op jit(solution)/shard_map/ppermute | solution.py:456
  24.2 0.5 %collective-permute-start.12 = (f32[2,24,256]{2,1,0:T(8,128)S(1)}, f32[2,24,256]{2,1,0:T(8,128)S(1)}, u32[]{:S(2)}, u32[]{:S(2)}) collective-permute-start(f32[2,24,256]{2,1,0:T(8,128)S(1)} %get-tuple-element.45), channel_id=1, source_target_pairs={{0,16},{4,20},{8,24},{12,28},{16,0},{20,4},{24,8},{28,12},{1,17},{... | collective-permute-start | bytes 147464 | tf_op jit(solution)/shard_map/ppermute | solution.py:456
  24.7 0.5 %collective-permute-start.13 = (f32[2,24,256]{2,1,0:T(8,128)S(1)}, f32[2,24,256]{2,1,0:T(8,128)S(1)}, u32[]{:S(2)}, u32[]{:S(2)}) collective-permute-start(f32[2,24,256]{2,1,0:T(8,128)S(1)} %get-tuple-element.46), channel_id=1, source_target_pairs={{0,8},{4,12},{8,0},{12,4},{16,24},{20,28},{24,16},{28,20},{1,9},{5... | collective-permute-start | bytes 147464 | tf_op jit(solution)/shard_map/ppermute | solution.py:456
  25.2 1.5 %collective-permute-done.11.refs_1_ = f32[2,24,256]{2,1,0:T(8,128)S(1)} collective-permute-done((f32[2,24,256]{2,1,0:T(8,128)S(1)}, f32[2,24,256]{2,1,0:T(8,128)S(1)}, u32[]{:S(2)}, u32[]{:S(2)}) %collective-permute-start.11) | collective-permute-done | bytes 49184 | tf_op jit(solution)/shard_map/ppermute | solution.py:456
  26.7 1.5 %collective-permute-done.12.refs_2_ = f32[2,24,256]{2,1,0:T(8,128)S(1)} collective-permute-done((f32[2,24,256]{2,1,0:T(8,128)S(1)}, f32[2,24,256]{2,1,0:T(8,128)S(1)}, u32[]{:S(2)}, u32[]{:S(2)}) %collective-permute-start.12) | collective-permute-done | bytes 49184 | tf_op jit(solution)/shard_map/ppermute | solution.py:456
  28.3 0.5 %collective-permute-done.13.refs_3_ = f32[2,24,256]{2,1,0:T(8,128)S(1)} collective-permute-done((f32[2,24,256]{2,1,0:T(8,128)S(1)}, f32[2,24,256]{2,1,0:T(8,128)S(1)}, u32[]{:S(2)}, u32[]{:S(2)}) %collective-permute-start.13) | collective-permute-done | bytes 49184 | tf_op jit(solution)/shard_map/ppermute | solution.py:456
  28.8 1.0 %combine.1 = bf16[1,5,2,1024]{3,2,1,0:T(2,128)(2,1)} custom-call(f32[2,24,256]{2,1,0:T(8,128)S(1)} %get-tuple-element.43.refs_0_, f32[2,24,256]{2,1,0:T(8,128)S(1)} %collective-permute-done.11.refs_1_, f32[2,24,256]{2,1,0:T(8,128)S(1)} %collective-permute-done.12.refs_2_, f32[2,24,256]{2,1,0:T(8,128)S(1)} %collective-permute-done.13.refs_3_), custom_call_target="tpu_custom_call" | custom-call | tf_op jit(solution)/shard_map/combine/pallas_call | solution.py:583
  (4 shorter events, 0.0 us)
Async XLA Ops:
  1.0 4.6 %collective-permute-start = (bf16[4,64,256]{2,1,0:T(8,128)(2,1)S(1)}, bf16[4,64,256]{2,1,0:T(8,128)(2,1)S(1)}, u32[]{:S(2)}, u32[]{:S(2)}) collective-permute-start(bf16[4,64,256]{2,1,0:T(8,128)(2,1)S(1)} %get-tuple-element.39.refs_3_), channel_id=1, source_target_pairs={{0,4},{4,0},{8,12},{12,8},{16,20},{20,16},{24,28},{28,24},{1,5},{5... | collective-permute-start | bytes 393224 | tf_op jit(solution)/shard_map/ppermute | solution.py:453
  1.5 4.1 %collective-permute-start.1 = (bf16[2,24,256]{2,1,0:T(8,128)(2,1)S(1)}, bf16[2,24,256]{2,1,0:T(8,128)(2,1)S(1)}, u32[]{:S(2)}, u32[]{:S(2)}) collective-permute-start(bf16[2,24,256]{2,1,0:T(8,128)(2,1)S(1)} %get-tuple-element.26.own_ref), channel_id=1, source_target_pairs={{0,4},{4,0},{8,12},{12,8},{16,20},{20,16},{24,28},{28,24},{1,5},{5... | collective-permute-start | bytes 73736 | tf_op jit(solution)/shard_map/ppermute | solution.py:453
  1.6 14.6 %collective-permute-start.7 = (bf16[4,64,256]{2,1,0:T(8,128)(2,1)S(1)}, bf16[4,64,256]{2,1,0:T(8,128)(2,1)S(1)}, u32[]{:S(2)}, u32[]{:S(2)}) collective-permute-start(bf16[4,64,256]{2,1,0:T(8,128)(2,1)S(1)} %get-tuple-element.39.refs_3_), channel_id=1, source_target_pairs={{0,2},{1,3},{2,0},{3,1},{4,7},{5,6},{6,5},{7,4},{8,10},{9,11},{10,... | collective-permute-start | bytes 393224 | tf_op jit(solution)/shard_map/ppermute | solution.py:463
  5.6 12.3 %collective-permute-start.8 = (bf16[4,64,256]{2,1,0:T(8,128)(2,1)S(1)}, bf16[4,64,256]{2,1,0:T(8,128)(2,1)S(1)}, u32[]{:S(2)}, u32[]{:S(2)}) collective-permute-start(bf16[4,64,256]{2,1,0:T(8,128)(2,1)S(1)} %collective-permute-done.refs_4_), channel_id=1, source_target_pairs={{0,2},{1,3},{2,0},{3,1},{4,7},{5,6},{6,5},{7,4},{8,10},{9,11},{10,... | collective-permute-start | bytes 393224 | tf_op jit(solution)/shard_map/ppermute | solution.py:463
  6.5 11.5 %collective-permute-start.9 = (bf16[4,64,256]{2,1,0:T(8,128)(2,1)S(1)}, bf16[4,64,256]{2,1,0:T(8,128)(2,1)S(1)}, u32[]{:S(2)}, u32[]{:S(2)}) collective-permute-start(bf16[4,64,256]{2,1,0:T(8,128)(2,1)S(1)} %get-tuple-element.39.refs_3_), channel_id=1, source_target_pairs={{0,1},{1,0},{2,3},{3,2},{4,5},{5,4},{6,7},{7,6},{8,9},{9,8},{10,11... | collective-permute-start | bytes 393224 | tf_op jit(solution)/shard_map/ppermute | solution.py:463
  8.1 5.2 %collective-permute-start.2 = (bf16[4,24,256]{2,1,0:T(8,128)(2,1)S(1)}, bf16[4,24,256]{2,1,0:T(8,128)(2,1)S(1)}, u32[]{:S(2)}, u32[]{:S(2)}) collective-permute-start(bf16[4,24,256]{2,1,0:T(8,128)(2,1)S(1)} %pair.1.refs_10_.refs_1_), channel_id=1, source_target_pairs={{0,8},{4,20},{8,0},{12,28},{16,24},{20,4},{24,16},{28,12},{1,9},{5... | collective-permute-start | bytes 147464 | tf_op jit(solution)/shard_map/ppermute | solution.py:540
  9.6 5.0 %collective-permute-start.4 = (bf16[4,24,256]{2,1,0:T(8,128)(2,1)S(1)}, bf16[4,24,256]{2,1,0:T(8,128)(2,1)S(1)}, u32[]{:S(2)}, u32[]{:S(2)}) collective-permute-start(bf16[4,24,256]{2,1,0:T(8,128)(2,1)S(1)} %pair.1.refs_10_.refs_1_), channel_id=1, source_target_pairs={{0,24},{4,28},{8,16},{12,20},{16,8},{20,12},{24,0},{28,4},{1,25},{... | collective-permute-start | bytes 147464 | tf_op jit(solution)/shard_map/ppermute | solution.py:456
  13.3 1.3 %collective-permute-start.3 = (bf16[4,24,256]{2,1,0:T(8,128)(2,1)S(1)}, bf16[4,24,256]{2,1,0:T(8,128)(2,1)S(1)}, u32[]{:S(2)}, u32[]{:S(2)}) collective-permute-start(bf16[4,24,256]{2,1,0:T(8,128)(2,1)S(1)} %collective-permute-done.2.refs_2_), channel_id=1, source_target_pairs={{0,4},{4,0},{8,12},{12,8},{16,20},{20,16},{24,28},{28,24},{1,5},{5... | collective-permute-start | bytes 147464 | tf_op jit(solution)/shard_map/ppermute | solution.py:453
  18.0 2.4 %collective-permute-start.10 = (bf16[3,4,64,256]{3,2,1,0:T(8,128)(2,1)S(1)}, bf16[3,4,64,256]{3,2,1,0:T(8,128)(2,1)S(1)}, u32[]{:S(2)}, u32[]{:S(2)}) collective-permute-start(bf16[3,4,64,256]{3,2,1,0:T(8,128)(2,1)S(1)} %gather.1.refs_5_), channel_id=1, source_target_pairs={{0,4},{4,0},{8,12},{12,8},{16,20},{20,16},{24,28},{28,24},{1,5},{5... | collective-permute-start | bytes 1179656 | tf_op jit(solution)/shard_map/ppermute | solution.py:453
  18.1 1.9 %collective-permute-start.5 = (f32[4,24,256]{2,1,0:T(8,128)S(1)}, f32[4,24,256]{2,1,0:T(8,128)S(1)}, u32[]{:S(2)}, u32[]{:S(2)}) collective-permute-start(f32[4,24,256]{2,1,0:T(8,128)S(1)} %get-tuple-element.36), channel_id=1, source_target_pairs={{0,4},{4,0},{8,12},{12,8},{16,20},{20,16},{24,28},{28,24},{1,5},{5... | collective-permute-start | bytes 294920 | tf_op jit(solution)/shard_map/ppermute | solution.py:453
  18.6 1.5 %collective-permute-start.6 = (f32[4,24,256]{2,1,0:T(8,128)S(1)}, f32[4,24,256]{2,1,0:T(8,128)S(1)}, u32[]{:S(2)}, u32[]{:S(2)}) collective-permute-start(f32[4,24,256]{2,1,0:T(8,128)S(1)} %get-tuple-element.37), channel_id=1, source_target_pairs={{0,4},{4,0},{8,12},{12,8},{16,20},{20,16},{24,28},{28,24},{1,5},{5... | collective-permute-start | bytes 294920 | tf_op jit(solution)/shard_map/ppermute | solution.py:453
  21.7 5.1 %collective-permute-start.11 = (f32[2,24,256]{2,1,0:T(8,128)S(1)}, f32[2,24,256]{2,1,0:T(8,128)S(1)}, u32[]{:S(2)}, u32[]{:S(2)}) collective-permute-start(f32[2,24,256]{2,1,0:T(8,128)S(1)} %get-tuple-element.44), channel_id=1, source_target_pairs={{0,24},{4,28},{8,16},{12,20},{16,8},{20,12},{24,0},{28,4},{1,25},{... | collective-permute-start | bytes 147464 | tf_op jit(solution)/shard_map/ppermute | solution.py:456
  24.2 4.1 %collective-permute-start.12 = (f32[2,24,256]{2,1,0:T(8,128)S(1)}, f32[2,24,256]{2,1,0:T(8,128)S(1)}, u32[]{:S(2)}, u32[]{:S(2)}) collective-permute-start(f32[2,24,256]{2,1,0:T(8,128)S(1)} %get-tuple-element.45), channel_id=1, source_target_pairs={{0,16},{4,20},{8,24},{12,28},{16,0},{20,4},{24,8},{28,12},{1,17},{... | collective-permute-start | bytes 147464 | tf_op jit(solution)/shard_map/ppermute | solution.py:456
  24.7 4.1 %collective-permute-start.13 = (f32[2,24,256]{2,1,0:T(8,128)S(1)}, f32[2,24,256]{2,1,0:T(8,128)S(1)}, u32[]{:S(2)}, u32[]{:S(2)}) collective-permute-start(f32[2,24,256]{2,1,0:T(8,128)S(1)} %get-tuple-element.46), channel_id=1, source_target_pairs={{0,8},{4,12},{8,0},{12,4},{16,24},{20,28},{24,16},{28,20},{1,9},{5... | collective-permute-start | bytes 147464 | tf_op jit(solution)/shard_map/ppermute | solution.py:456

commit v5 on v4

--- a/solution.py
+++ b/solution.py
@@ -275,7 +275,7 @@
         request = ((chip ^ (i // each)) * 2 + core) * each + i % each
         group = group_ref[0, request]
         shift = z ^ lax.div(group, held)
-        array = jnp.where(shift < 2, shift, (shift & ~1) + ((shift ^ core) & 1))
+        array = jnp.where(shift < 2, shift, (shift & ~1) + ((shift ^ core ^ 1) & 1))
         to = 2 * pieces + i
         table_out[to : to + 1] = jnp.full((1, 128), array * held + lax.rem(group, held), jnp.int32)
     for copy in large:
@@ -497,7 +497,7 @@
     )
     fetched = []
     for s in range(2, shifts, 2):
-        fetched += [along_req(x, s, s + 1) for x in (own_blocks, sibling_blocks)]
+        fetched += [along_req(x, s + 1, s) for x in (own_blocks, sibling_blocks)]
     fetched.append(along_req(later_blocks, 1, 1))
     chip_queries = call(
         pair_kernel, "pair", shape((2 * each, MESSAGE, WIDTH), BF16), [VMEM] * 2

time: 30 us -> 28.3 us (0.943)
  waiting for transfers between devices: 7.97 us -> 6.01 us
    ppermute x3, waiting for transfers between devices: 1.77 us -> 0.01 us  [along_req(): return lax.ppermute(x, ('blk', 'req'), pairs)]
    ppermute x6, starting transfers between devices: 1.31 us -> 2.07 us  [other_core(): return lax.ppermute(x, 'blk', [(i, i ^ 1) for i in range(devices)])]
    ppermute x3, starting transfers between devices: 6.46 us -> 5.9 us  [along_req(): return lax.ppermute(x, ('blk', 'req'), pairs)]
  transfers between devices with their start and end apart: 14 -> 14, of which waited for: 8 -> 7; matrix products, arithmetic and copies ran while one was open for 0% -> 0% of each run, Pallas kernels for 14% -> 15%
where the time goes in v5:
time: 28.3 us; the launch traced here: 28.1 us
  starting transfers between devices  14.6 us (52%)
  Pallas kernels  7.43 us (26%)
  waiting for transfers between devices  6.01 us (21%)
    ppermute x3, starting transfers between devices, along_req(): return lax.ppermute(x, ('blk', 'req'), pairs)  5.9 us
    ppermute x4, starting transfers between devices, other_chip(): return lax.ppermute(x, 'blk', [(i, i ^ 2 * s) for i in range(devices)])  5.06 us
    ppermute x4, waiting for transfers between devices, other_chip(): return lax.ppermute(x, 'blk', [(i, i ^ 2 * s) for i in range(devices)])  4.82 us
    pallas_call x1, Pallas kernels, per_device(): call(functools.partial(own_kernel, chips, each, shifts, held), 'own', [sh...  2.24 us
    ppermute x6, starting transfers between devices, other_core(): return lax.ppermute(x, 'blk', [(i, i ^ 1) for i in range(devices)])  2.07 us
    ppermute x1, starting transfers between devices, per_device(): lax.ppermute(chip_queries, 'blk', [(i, i ^ 2 * (across_cores(s, chips) if...  1.55 us
    pallas_call x1, Pallas kernels, per_device(): call(functools.partial(pieces_kernel, chips, each), 'pieces', [shape((3,)...  1.55 us
    pallas_call x1, Pallas kernels, per_device(): call(functools.partial(prompts_kernel, chips, each, 2 * pieces), 'prompts...  1.27 us
  transfers between devices with their start and end apart: 14, of which 7 were waited for; matrix products, arithmetic and copies ran while one was open for 0% of the time, Pallas kernels for 15%

profile of v5, /device:TPU:0, one launch (start us, length us, event | category | flops | bytes accessed | tf_op | source)
XLA Modules:
  0.0 28.1 jit_solution(3201473531974068303)
XLA Ops:
  0.0 1.0 %parcel.1 = (bf16[4,64,256]{2,1,0:T(8,128)(2,1)S(1)}, bf16[2,24,256]{2,1,0:T(8,128)(2,1)S(1)}) custom-call(s32[1,4]{1,0:T(1,128)} %bitcast.12, bf16[4,32,256]{2,1,0:T(8,128)(2,1)} %keys_hbm.1, bf16[4,32,256]{2,1,0:T(8,128)(2,1)} %values_hbm.1, bf16[1,5,2,1024]{3,2,1,0:T(2,128)(2,1)} %bitcast.7), custom_call_target="tpu_custom_call" | custom-call | tf_op jit(solution)/shard_map/parcel/pallas_call | solution.py:475
  1.0 0.5 %collective-permute-start = (bf16[4,64,256]{2,1,0:T(8,128)(2,1)S(1)}, bf16[4,64,256]{2,1,0:T(8,128)(2,1)S(1)}, u32[]{:S(2)}, u32[]{:S(2)}) collective-permute-start(bf16[4,64,256]{2,1,0:T(8,128)(2,1)S(1)} %get-tuple-element.39.refs_3_), channel_id=1, source_target_pairs={{0,4},{4,0},{8,12},{12,8},{16,20},{20,16},{24,28},{28,24},{1,5},{5... | collective-permute-start | bytes 393224 | tf_op jit(solution)/shard_map/ppermute | solution.py:453
  1.5 0.1 collective-permute-start.1
  1.6 5.0 %collective-permute-start.7 = (bf16[4,64,256]{2,1,0:T(8,128)(2,1)S(1)}, bf16[4,64,256]{2,1,0:T(8,128)(2,1)S(1)}, u32[]{:S(2)}, u32[]{:S(2)}) collective-permute-start(bf16[4,64,256]{2,1,0:T(8,128)(2,1)S(1)} %get-tuple-element.39.refs_3_), channel_id=1, source_target_pairs={{0,3},{1,2},{2,1},{3,0},{4,6},{5,7},{6,4},{7,5},{8,11},{9,10},{10,... | collective-permute-start | bytes 393224 | tf_op jit(solution)/shard_map/ppermute | solution.py:463
  6.7 0.0 collective-permute-done.1.sibling_ref
  6.7 0.0 collective-permute-done.refs_4_
  6.7 0.9 %collective-permute-start.8 = (bf16[4,64,256]{2,1,0:T(8,128)(2,1)S(1)}, bf16[4,64,256]{2,1,0:T(8,128)(2,1)S(1)}, u32[]{:S(2)}, u32[]{:S(2)}) collective-permute-start(bf16[4,64,256]{2,1,0:T(8,128)(2,1)S(1)} %collective-permute-done.refs_4_), channel_id=1, source_target_pairs={{0,3},{1,2},{2,1},{3,0},{4,6},{5,7},{6,4},{7,5},{8,11},{9,10},{10,... | collective-permute-start | bytes 393224 | tf_op jit(solution)/shard_map/ppermute | solution.py:463
  7.5 0.0 collective-permute-start.9
  7.5 1.6 %collective-permute-start.2 = (bf16[4,24,256]{2,1,0:T(8,128)(2,1)S(1)}, bf16[4,24,256]{2,1,0:T(8,128)(2,1)S(1)}, u32[]{:S(2)}, u32[]{:S(2)}) collective-permute-start(bf16[4,24,256]{2,1,0:T(8,128)(2,1)S(1)} %pair.1.refs_10_.refs_1_), channel_id=1, source_target_pairs={{0,8},{4,20},{8,0},{12,28},{16,24},{20,4},{24,16},{28,12},{1,9},{5... | collective-permute-start | bytes 147464 | tf_op jit(solution)/shard_map/ppermute | solution.py:540
  9.1 1.5 %collective-permute-start.4 = (bf16[4,24,256]{2,1,0:T(8,128)(2,1)S(1)}, bf16[4,24,256]{2,1,0:T(8,128)(2,1)S(1)}, u32[]{:S(2)}, u32[]{:S(2)}) collective-permute-start(bf16[4,24,256]{2,1,0:T(8,128)(2,1)S(1)} %pair.1.refs_10_.refs_1_), channel_id=1, source_target_pairs={{0,24},{4,28},{8,16},{12,20},{16,8},{20,12},{24,0},{28,4},{1,25},{... | collective-permute-start | bytes 147464 | tf_op jit(solution)/shard_map/ppermute | solution.py:456
  10.6 2.2 %own.1 = (f32[3,2,32,256]{3,2,1,0:T(8,128)S(1)}, s32[24,128]{1,0:T(8,128)S(1)}, bf16[8,256,256]{2,1,0:T(8,128)(2,1)S(1)}, bf16[8,256,256]{2,1,0:T(8,128)(2,1)S(1)}) custom-call(s32[1,64]{1,0:T(1,128)} %refs_0_.1, s32[1,16]{1,0:T(1,128)} %refs_1_.1, s32[1,2]{1,0:T(1,128)} %refs_2_.1, s32[1,16]{1,0:T(1,128)} %refs_3_.1, bf16[1,5,2,256]{3,2,1,0:T(2,128)(2,1)} %bitcast.8, ...), custom_call_target="tpu_custom_call" | custom-call | bytes 8388608 | tf_op jit(solution)/shard_map/own/pallas_call | solution.py:506
  12.8 0.0 collective-permute-done.2.refs_2_
  12.8 0.1 collective-permute-start.3
  12.9 1.2 %collective-permute-done.4.refs_4_ = bf16[4,24,256]{2,1,0:T(8,128)(2,1)S(1)} collective-permute-done((bf16[4,24,256]{2,1,0:T(8,128)(2,1)S(1)}, bf16[4,24,256]{2,1,0:T(8,128)(2,1)S(1)}, u32[]{:S(2)}, u32[]{:S(2)}) %collective-permute-start.4) | collective-permute-done | bytes 49184 | tf_op jit(solution)/shard_map/ppermute | solution.py:456
  14.1 0.1 collective-permute-done.3.refs_3_
  14.1 1.6 %pieces.1 = (f32[3,8,32,256]{3,2,1,0:T(8,128)S(1)}, f32[4,24,256]{2,1,0:T(8,128)S(1)}, f32[4,24,256]{2,1,0:T(8,128)S(1)}, bf16[8,32,256]{2,1,0:T(8,128)(2,1)S(1)}) custom-call(s32[24,128]{1,0:T(8,128)S(1)} %get-tuple-element.29.refs_0_, bf16[4,24,256]{2,1,0:T(8,128)(2,1)S(1)} %pair.1.refs_10_.refs_1_, ...), custom_call_target="tpu_custom_call" | custom-call | tf_op jit(solution)/shard_map/pieces/pallas_call | solution.py:551
  15.7 0.0 collective-permute-done.9.refs_2_
  15.8 0.9 %collective-permute-start.10 = (bf16[3,4,64,256]{3,2,1,0:T(8,128)(2,1)S(1)}, bf16[3,4,64,256]{3,2,1,0:T(8,128)(2,1)S(1)}, u32[]{:S(2)}, u32[]{:S(2)}) collective-permute-start(bf16[3,4,64,256]{3,2,1,0:T(8,128)(2,1)S(1)} %gather.1.refs_5_), channel_id=1, source_target_pairs={{0,4},{4,0},{8,12},{12,8},{16,20},{20,16},{24,28},{28,24},{1,5},{5... | collective-permute-start | bytes 1179656 | tf_op jit(solution)/shard_map/ppermute | solution.py:453
  16.7 0.1 collective-permute-start.5
  16.7 0.4 %collective-permute-start.6 = (f32[4,24,256]{2,1,0:T(8,128)S(1)}, f32[4,24,256]{2,1,0:T(8,128)S(1)}, u32[]{:S(2)}, u32[]{:S(2)}) collective-permute-start(f32[4,24,256]{2,1,0:T(8,128)S(1)} %get-tuple-element.37), channel_id=1, source_target_pairs={{0,4},{4,0},{8,12},{12,8},{16,20},{20,16},{24,28},{28,24},{1,5},{5... | collective-permute-start | bytes 294920 | tf_op jit(solution)/shard_map/ppermute | solution.py:453
  17.2 1.0 %collective-permute-done.5.first_ref = f32[4,24,256]{2,1,0:T(8,128)S(1)} collective-permute-done((f32[4,24,256]{2,1,0:T(8,128)S(1)}, f32[4,24,256]{2,1,0:T(8,128)S(1)}, u32[]{:S(2)}, u32[]{:S(2)}) %collective-permute-start.5) | collective-permute-done | bytes 98336 | tf_op jit(solution)/shard_map/ppermute | solution.py:453
  18.2 0.1 collective-permute-done.6.second_ref
  18.3 0.3 %join.1.refs_2_ = f32[3,8,32,256]{3,2,1,0:T(8,128)S(1)} custom-call(f32[3,8,32,256]{3,2,1,0:T(8,128)S(1)} %get-tuple-element.34.mine_ref, f32[3,2,32,256]{3,2,1,0:T(8,128)S(1)} %get-tuple-element.35.own_ref, f32[4,24,256]{2,1,0:T(8,128)S(1)} %collective-permute-done.5.first_ref, f32[4,24,256]{2,1,0:T(8,128)S(1)} %collective-permute-done.6.second_ref), custom_call_target="tpu_custom_call" | custom-call | tf_op jit(solution)/shard_map/join/pallas_call | solution.py:564
  18.6 0.0 collective-permute-done.10.refs_6_
  18.6 1.3 %prompts.1 = (f32[2,24,256]{2,1,0:T(8,128)S(1)}, f32[2,24,256]{2,1,0:T(8,128)S(1)}, f32[2,24,256]{2,1,0:T(8,128)S(1)}, f32[2,24,256]{2,1,0:T(8,128)S(1)}) custom-call(s32[24,128]{1,0:T(8,128)S(1)} %get-tuple-element.29.refs_0_, bf16[8,32,256]{2,1,0:T(8,128)(2,1)S(1)} %get-tuple-element.33.refs_1_, f32[3,8,32,256]{3,2,1,0:T(8,128)S(1)} %join.1.refs_2_, ...), custom_call_target="tpu_custom_call" | custom-call | tf_op jit(solution)/shard_map/prompts/pallas_call | solution.py:575
  19.9 2.6 %collective-permute-start.11 = (f32[2,24,256]{2,1,0:T(8,128)S(1)}, f32[2,24,256]{2,1,0:T(8,128)S(1)}, u32[]{:S(2)}, u32[]{:S(2)}) collective-permute-start(f32[2,24,256]{2,1,0:T(8,128)S(1)} %get-tuple-element.44), channel_id=1, source_target_pairs={{0,24},{4,28},{8,16},{12,20},{16,8},{20,12},{24,0},{28,4},{1,25},{... | collective-permute-start | bytes 147464 | tf_op jit(solution)/shard_map/ppermute | solution.py:456
  22.5 0.5 %collective-permute-start.12 = (f32[2,24,256]{2,1,0:T(8,128)S(1)}, f32[2,24,256]{2,1,0:T(8,128)S(1)}, u32[]{:S(2)}, u32[]{:S(2)}) collective-permute-start(f32[2,24,256]{2,1,0:T(8,128)S(1)} %get-tuple-element.45), channel_id=1, source_target_pairs={{0,16},{4,20},{8,24},{12,28},{16,0},{20,4},{24,8},{28,12},{1,17},{... | collective-permute-start | bytes 147464 | tf_op jit(solution)/shard_map/ppermute | solution.py:456
  23.0 0.4 %collective-permute-start.13 = (f32[2,24,256]{2,1,0:T(8,128)S(1)}, f32[2,24,256]{2,1,0:T(8,128)S(1)}, u32[]{:S(2)}, u32[]{:S(2)}) collective-permute-start(f32[2,24,256]{2,1,0:T(8,128)S(1)} %get-tuple-element.46), channel_id=1, source_target_pairs={{0,8},{4,12},{8,0},{12,4},{16,24},{20,28},{24,16},{28,20},{1,9},{5... | collective-permute-start | bytes 147464 | tf_op jit(solution)/shard_map/ppermute | solution.py:456
  23.5 1.5 %collective-permute-done.11.refs_1_ = f32[2,24,256]{2,1,0:T(8,128)S(1)} collective-permute-done((f32[2,24,256]{2,1,0:T(8,128)S(1)}, f32[2,24,256]{2,1,0:T(8,128)S(1)}, u32[]{:S(2)}, u32[]{:S(2)}) %collective-permute-start.11) | collective-permute-done | bytes 49184 | tf_op jit(solution)/shard_map/ppermute | solution.py:456
  25.0 1.7 %collective-permute-done.12.refs_2_ = f32[2,24,256]{2,1,0:T(8,128)S(1)} collective-permute-done((f32[2,24,256]{2,1,0:T(8,128)S(1)}, f32[2,24,256]{2,1,0:T(8,128)S(1)}, u32[]{:S(2)}, u32[]{:S(2)}) %collective-permute-start.12) | collective-permute-done | bytes 49184 | tf_op jit(solution)/shard_map/ppermute | solution.py:456
  26.6 0.5 %collective-permute-done.13.refs_3_ = f32[2,24,256]{2,1,0:T(8,128)S(1)} collective-permute-done((f32[2,24,256]{2,1,0:T(8,128)S(1)}, f32[2,24,256]{2,1,0:T(8,128)S(1)}, u32[]{:S(2)}, u32[]{:S(2)}) %collective-permute-start.13) | collective-permute-done | bytes 49184 | tf_op jit(solution)/shard_map/ppermute | solution.py:456
  27.1 1.0 %combine.1 = bf16[1,5,2,1024]{3,2,1,0:T(2,128)(2,1)} custom-call(f32[2,24,256]{2,1,0:T(8,128)S(1)} %get-tuple-element.43.refs_0_, f32[2,24,256]{2,1,0:T(8,128)S(1)} %collective-permute-done.11.refs_1_, f32[2,24,256]{2,1,0:T(8,128)S(1)} %collective-permute-done.12.refs_2_, f32[2,24,256]{2,1,0:T(8,128)S(1)} %collective-permute-done.13.refs_3_), custom_call_target="tpu_custom_call" | custom-call | tf_op jit(solution)/shard_map/combine/pallas_call | solution.py:583
  (4 shorter events, 0.0 us)
Async XLA Ops:
  1.0 5.6 %collective-permute-start = (bf16[4,64,256]{2,1,0:T(8,128)(2,1)S(1)}, bf16[4,64,256]{2,1,0:T(8,128)(2,1)S(1)}, u32[]{:S(2)}, u32[]{:S(2)}) collective-permute-start(bf16[4,64,256]{2,1,0:T(8,128)(2,1)S(1)} %get-tuple-element.39.refs_3_), channel_id=1, source_target_pairs={{0,4},{4,0},{8,12},{12,8},{16,20},{20,16},{24,28},{28,24},{1,5},{5... | collective-permute-start | bytes 393224 | tf_op jit(solution)/shard_map/ppermute | solution.py:453
  1.5 5.1 %collective-permute-start.1 = (bf16[2,24,256]{2,1,0:T(8,128)(2,1)S(1)}, bf16[2,24,256]{2,1,0:T(8,128)(2,1)S(1)}, u32[]{:S(2)}, u32[]{:S(2)}) collective-permute-start(bf16[2,24,256]{2,1,0:T(8,128)(2,1)S(1)} %get-tuple-element.26.own_ref), channel_id=1, source_target_pairs={{0,4},{4,0},{8,12},{12,8},{16,20},{20,16},{24,28},{28,24},{1,5},{5... | collective-permute-start | bytes 73736 | tf_op jit(solution)/shard_map/ppermute | solution.py:453
  1.6 14.1 %collective-permute-start.7 = (bf16[4,64,256]{2,1,0:T(8,128)(2,1)S(1)}, bf16[4,64,256]{2,1,0:T(8,128)(2,1)S(1)}, u32[]{:S(2)}, u32[]{:S(2)}) collective-permute-start(bf16[4,64,256]{2,1,0:T(8,128)(2,1)S(1)} %get-tuple-element.39.refs_3_), channel_id=1, source_target_pairs={{0,3},{1,2},{2,1},{3,0},{4,6},{5,7},{6,4},{7,5},{8,11},{9,10},{10,... | collective-permute-start | bytes 393224 | tf_op jit(solution)/shard_map/ppermute | solution.py:463
  6.7 9.1 %collective-permute-start.8 = (bf16[4,64,256]{2,1,0:T(8,128)(2,1)S(1)}, bf16[4,64,256]{2,1,0:T(8,128)(2,1)S(1)}, u32[]{:S(2)}, u32[]{:S(2)}) collective-permute-start(bf16[4,64,256]{2,1,0:T(8,128)(2,1)S(1)} %collective-permute-done.refs_4_), channel_id=1, source_target_pairs={{0,3},{1,2},{2,1},{3,0},{4,6},{5,7},{6,4},{7,5},{8,11},{9,10},{10,... | collective-permute-start | bytes 393224 | tf_op jit(solution)/shard_map/ppermute | solution.py:463
  7.5 8.2 %collective-permute-start.9 = (bf16[4,64,256]{2,1,0:T(8,128)(2,1)S(1)}, bf16[4,64,256]{2,1,0:T(8,128)(2,1)S(1)}, u32[]{:S(2)}, u32[]{:S(2)}) collective-permute-start(bf16[4,64,256]{2,1,0:T(8,128)(2,1)S(1)} %get-tuple-element.39.refs_3_), channel_id=1, source_target_pairs={{0,1},{1,0},{2,3},{3,2},{4,5},{5,4},{6,7},{7,6},{8,9},{9,8},{10,11... | collective-permute-start | bytes 393224 | tf_op jit(solution)/shard_map/ppermute | solution.py:463
  7.5 5.3 %collective-permute-start.2 = (bf16[4,24,256]{2,1,0:T(8,128)(2,1)S(1)}, bf16[4,24,256]{2,1,0:T(8,128)(2,1)S(1)}, u32[]{:S(2)}, u32[]{:S(2)}) collective-permute-start(bf16[4,24,256]{2,1,0:T(8,128)(2,1)S(1)} %pair.1.refs_10_.refs_1_), channel_id=1, source_target_pairs={{0,8},{4,20},{8,0},{12,28},{16,24},{20,4},{24,16},{28,12},{1,9},{5... | collective-permute-start | bytes 147464 | tf_op jit(solution)/shard_map/ppermute | solution.py:540
  9.1 5.0 %collective-permute-start.4 = (bf16[4,24,256]{2,1,0:T(8,128)(2,1)S(1)}, bf16[4,24,256]{2,1,0:T(8,128)(2,1)S(1)}, u32[]{:S(2)}, u32[]{:S(2)}) collective-permute-start(bf16[4,24,256]{2,1,0:T(8,128)(2,1)S(1)} %pair.1.refs_10_.refs_1_), channel_id=1, source_target_pairs={{0,24},{4,28},{8,16},{12,20},{16,8},{20,12},{24,0},{28,4},{1,25},{... | collective-permute-start | bytes 147464 | tf_op jit(solution)/shard_map/ppermute | solution.py:456
  12.8 1.3 %collective-permute-start.3 = (bf16[4,24,256]{2,1,0:T(8,128)(2,1)S(1)}, bf16[4,24,256]{2,1,0:T(8,128)(2,1)S(1)}, u32[]{:S(2)}, u32[]{:S(2)}) collective-permute-start(bf16[4,24,256]{2,1,0:T(8,128)(2,1)S(1)} %collective-permute-done.2.refs_2_), channel_id=1, source_target_pairs={{0,4},{4,0},{8,12},{12,8},{16,20},{20,16},{24,28},{28,24},{1,5},{5... | collective-permute-start | bytes 147464 | tf_op jit(solution)/shard_map/ppermute | solution.py:453
  15.8 2.8 %collective-permute-start.10 = (bf16[3,4,64,256]{3,2,1,0:T(8,128)(2,1)S(1)}, bf16[3,4,64,256]{3,2,1,0:T(8,128)(2,1)S(1)}, u32[]{:S(2)}, u32[]{:S(2)}) collective-permute-start(bf16[3,4,64,256]{3,2,1,0:T(8,128)(2,1)S(1)} %gather.1.refs_5_), channel_id=1, source_target_pairs={{0,4},{4,0},{8,12},{12,8},{16,20},{20,16},{24,28},{28,24},{1,5},{5... | collective-permute-start | bytes 1179656 | tf_op jit(solution)/shard_map/ppermute | solution.py:453
  16.7 1.5 %collective-permute-start.5 = (f32[4,24,256]{2,1,0:T(8,128)S(1)}, f32[4,24,256]{2,1,0:T(8,128)S(1)}, u32[]{:S(2)}, u32[]{:S(2)}) collective-permute-start(f32[4,24,256]{2,1,0:T(8,128)S(1)} %get-tuple-element.36), channel_id=1, source_target_pairs={{0,4},{4,0},{8,12},{12,8},{16,20},{20,16},{24,28},{28,24},{1,5},{5... | collective-permute-start | bytes 294920 | tf_op jit(solution)/shard_map/ppermute | solution.py:453
  16.7 1.6 %collective-permute-start.6 = (f32[4,24,256]{2,1,0:T(8,128)S(1)}, f32[4,24,256]{2,1,0:T(8,128)S(1)}, u32[]{:S(2)}, u32[]{:S(2)}) collective-permute-start(f32[4,24,256]{2,1,0:T(8,128)S(1)} %get-tuple-element.37), channel_id=1, source_target_pairs={{0,4},{4,0},{8,12},{12,8},{16,20},{20,16},{24,28},{28,24},{1,5},{5... | collective-permute-start | bytes 294920 | tf_op jit(solution)/shard_map/ppermute | solution.py:453
  19.9 5.1 %collective-permute-start.11 = (f32[2,24,256]{2,1,0:T(8,128)S(1)}, f32[2,24,256]{2,1,0:T(8,128)S(1)}, u32[]{:S(2)}, u32[]{:S(2)}) collective-permute-start(f32[2,24,256]{2,1,0:T(8,128)S(1)} %get-tuple-element.44), channel_id=1, source_target_pairs={{0,24},{4,28},{8,16},{12,20},{16,8},{20,12},{24,0},{28,4},{1,25},{... | collective-permute-start | bytes 147464 | tf_op jit(solution)/shard_map/ppermute | solution.py:456
  22.5 4.1 %collective-permute-start.12 = (f32[2,24,256]{2,1,0:T(8,128)S(1)}, f32[2,24,256]{2,1,0:T(8,128)S(1)}, u32[]{:S(2)}, u32[]{:S(2)}) collective-permute-start(f32[2,24,256]{2,1,0:T(8,128)S(1)} %get-tuple-element.45), channel_id=1, source_target_pairs={{0,16},{4,20},{8,24},{12,28},{16,0},{20,4},{24,8},{28,12},{1,17},{... | collective-permute-start | bytes 147464 | tf_op jit(solution)/shard_map/ppermute | solution.py:456
  23.0 4.1 %collective-permute-start.13 = (f32[2,24,256]{2,1,0:T(8,128)S(1)}, f32[2,24,256]{2,1,0:T(8,128)S(1)}, u32[]{:S(2)}, u32[]{:S(2)}) collective-permute-start(f32[2,24,256]{2,1,0:T(8,128)S(1)} %get-tuple-element.46), channel_id=1, source_target_pairs={{0,8},{4,12},{8,0},{12,4},{16,24},{20,28},{24,16},{28,20},{1,9},{5... | collective-permute-start | bytes 147464 | tf_op jit(solution)/shard_map/ppermute | solution.py:456

commit v6 on v5

--- a/solution.py
+++ b/solution.py
@@ -255,7 +255,7 @@
             & (column - POSITIONS <= position)
         )
         query = unpack_rows(query_ref[k].astype(F32)).astype(BF16)
-        got = attend(query, rows_ref[0, k].astype(BF16), rows_ref[1, k].astype(BF16), live, False)
+        got = attend(query, rows_ref[0, k].astype(BF16), rows_ref[1, k].astype(BF16), live, True)
         for j in range(3):
             own_out[j, k] = got[j]
 

time: 28.3 us -> 28.3 us (level)
  transfers between devices with their start and end apart: 14 -> 14, of which waited for: 7 -> 6; matrix products, arithmetic and copies ran while one was open for 0% -> 0% of each run, Pallas kernels for 15% -> 14%
where the time goes in v6:
time: 28.3 us; the launch traced here: 28.1 us
  starting transfers between devices  14.6 us (52%)
  Pallas kernels  7.25 us (26%)
  waiting for transfers between devices  6.14 us (22%)
    ppermute x3, starting transfers between devices, along_req(): return lax.ppermute(x, ('blk', 'req'), pairs)  5.9 us
    ppermute x4, starting transfers between devices, other_chip(): return lax.ppermute(x, 'blk', [(i, i ^ 2 * s) for i in range(devices)])  5.06 us
    ppermute x4, waiting for transfers between devices, other_chip(): return lax.ppermute(x, 'blk', [(i, i ^ 2 * s) for i in range(devices)])  5 us
    ppermute x6, starting transfers between devices, other_core(): return lax.ppermute(x, 'blk', [(i, i ^ 1) for i in range(devices)])  2.13 us
    pallas_call x1, Pallas kernels, per_device(): call(functools.partial(own_kernel, chips, each, shifts, held), 'own', [sh...  2.06 us
    ppermute x1, starting transfers between devices, per_device(): lax.ppermute(chip_queries, 'blk', [(i, i ^ 2 * (across_cores(s, chips) if...  1.55 us
    pallas_call x1, Pallas kernels, per_device(): call(functools.partial(pieces_kernel, chips, each), 'pieces', [shape((3,)...  1.55 us
    pallas_call x1, Pallas kernels, per_device(): call(functools.partial(prompts_kernel, chips, each, 2 * pieces), 'prompts...  1.27 us
  transfers between devices with their start and end apart: 14, of which 6 were waited for; matrix products, arithmetic and copies ran while one was open for 0% of the time, Pallas kernels for 14%

profile of v6, /device:TPU:0, one launch (start us, length us, event | category | flops | bytes accessed | tf_op | source)
XLA Modules:
  0.0 28.1 jit_solution(9773933277776448475)
XLA Ops:
  0.0 1.0 %parcel.1 = (bf16[4,64,256]{2,1,0:T(8,128)(2,1)S(1)}, bf16[2,24,256]{2,1,0:T(8,128)(2,1)S(1)}) custom-call(s32[1,4]{1,0:T(1,128)} %bitcast.12, bf16[4,32,256]{2,1,0:T(8,128)(2,1)} %keys_hbm.1, bf16[4,32,256]{2,1,0:T(8,128)(2,1)} %values_hbm.1, bf16[1,5,2,1024]{3,2,1,0:T(2,128)(2,1)} %bitcast.7), custom_call_target="tpu_custom_call" | custom-call | tf_op jit(solution)/shard_map/parcel/pallas_call | solution.py:475
  1.0 0.5 %collective-permute-start = (bf16[4,64,256]{2,1,0:T(8,128)(2,1)S(1)}, bf16[4,64,256]{2,1,0:T(8,128)(2,1)S(1)}, u32[]{:S(2)}, u32[]{:S(2)}) collective-permute-start(bf16[4,64,256]{2,1,0:T(8,128)(2,1)S(1)} %get-tuple-element.39.refs_3_), channel_id=1, source_target_pairs={{0,4},{4,0},{8,12},{12,8},{16,20},{20,16},{24,28},{28,24},{1,5},{5... | collective-permute-start | bytes 393224 | tf_op jit(solution)/shard_map/ppermute | solution.py:453
  1.5 0.1 collective-permute-start.1
  1.6 5.0 %collective-permute-start.7 = (bf16[4,64,256]{2,1,0:T(8,128)(2,1)S(1)}, bf16[4,64,256]{2,1,0:T(8,128)(2,1)S(1)}, u32[]{:S(2)}, u32[]{:S(2)}) collective-permute-start(bf16[4,64,256]{2,1,0:T(8,128)(2,1)S(1)} %get-tuple-element.39.refs_3_), channel_id=1, source_target_pairs={{0,3},{1,2},{2,1},{3,0},{4,6},{5,7},{6,4},{7,5},{8,11},{9,10},{10,... | collective-permute-start | bytes 393224 | tf_op jit(solution)/shard_map/ppermute | solution.py:463
  6.7 0.0 collective-permute-done.1.sibling_ref
  6.7 0.0 collective-permute-done.refs_4_
  6.7 0.9 %collective-permute-start.8 = (bf16[4,64,256]{2,1,0:T(8,128)(2,1)S(1)}, bf16[4,64,256]{2,1,0:T(8,128)(2,1)S(1)}, u32[]{:S(2)}, u32[]{:S(2)}) collective-permute-start(bf16[4,64,256]{2,1,0:T(8,128)(2,1)S(1)} %collective-permute-done.refs_4_), channel_id=1, source_target_pairs={{0,3},{1,2},{2,1},{3,0},{4,6},{5,7},{6,4},{7,5},{8,11},{9,10},{10,... | collective-permute-start | bytes 393224 | tf_op jit(solution)/shard_map/ppermute | solution.py:463
  7.5 0.0 collective-permute-start.9
  7.5 1.6 %collective-permute-start.2 = (bf16[4,24,256]{2,1,0:T(8,128)(2,1)S(1)}, bf16[4,24,256]{2,1,0:T(8,128)(2,1)S(1)}, u32[]{:S(2)}, u32[]{:S(2)}) collective-permute-start(bf16[4,24,256]{2,1,0:T(8,128)(2,1)S(1)} %pair.1.refs_10_.refs_1_), channel_id=1, source_target_pairs={{0,8},{4,20},{8,0},{12,28},{16,24},{20,4},{24,16},{28,12},{1,9},{5... | collective-permute-start | bytes 147464 | tf_op jit(solution)/shard_map/ppermute | solution.py:540
  9.1 1.5 %collective-permute-start.4 = (bf16[4,24,256]{2,1,0:T(8,128)(2,1)S(1)}, bf16[4,24,256]{2,1,0:T(8,128)(2,1)S(1)}, u32[]{:S(2)}, u32[]{:S(2)}) collective-permute-start(bf16[4,24,256]{2,1,0:T(8,128)(2,1)S(1)} %pair.1.refs_10_.refs_1_), channel_id=1, source_target_pairs={{0,24},{4,28},{8,16},{12,20},{16,8},{20,12},{24,0},{28,4},{1,25},{... | collective-permute-start | bytes 147464 | tf_op jit(solution)/shard_map/ppermute | solution.py:456
  10.6 2.1 %own.1 = (f32[3,2,32,256]{3,2,1,0:T(8,128)S(1)}, s32[24,128]{1,0:T(8,128)S(1)}, bf16[8,256,256]{2,1,0:T(8,128)(2,1)S(1)}, bf16[8,256,256]{2,1,0:T(8,128)(2,1)S(1)}) custom-call(s32[1,64]{1,0:T(1,128)} %refs_0_.1, s32[1,16]{1,0:T(1,128)} %refs_1_.1, s32[1,2]{1,0:T(1,128)} %refs_2_.1, s32[1,16]{1,0:T(1,128)} %refs_3_.1, bf16[1,5,2,256]{3,2,1,0:T(2,128)(2,1)} %bitcast.8, ...), custom_call_target="tpu_custom_call" | custom-call | bytes 8388608 | tf_op jit(solution)/shard_map/own/pallas_call | solution.py:506
  12.6 0.0 collective-permute-done.2.refs_2_
  12.7 0.1 collective-permute-start.3
  12.7 1.3 %collective-permute-done.4.refs_4_ = bf16[4,24,256]{2,1,0:T(8,128)(2,1)S(1)} collective-permute-done((bf16[4,24,256]{2,1,0:T(8,128)(2,1)S(1)}, bf16[4,24,256]{2,1,0:T(8,128)(2,1)S(1)}, u32[]{:S(2)}, u32[]{:S(2)}) %collective-permute-start.4) | collective-permute-done | bytes 49184 | tf_op jit(solution)/shard_map/ppermute | solution.py:456
  14.1 1.6 %pieces.1 = (f32[3,8,32,256]{3,2,1,0:T(8,128)S(1)}, f32[4,24,256]{2,1,0:T(8,128)S(1)}, f32[4,24,256]{2,1,0:T(8,128)S(1)}, bf16[8,32,256]{2,1,0:T(8,128)(2,1)S(1)}) custom-call(s32[24,128]{1,0:T(8,128)S(1)} %get-tuple-element.29.refs_0_, bf16[4,24,256]{2,1,0:T(8,128)(2,1)S(1)} %pair.1.refs_10_.refs_1_, ...), custom_call_target="tpu_custom_call" | custom-call | tf_op jit(solution)/shard_map/pieces/pallas_call | solution.py:551
  15.6 0.0 collective-permute-done.7.refs_0_
  15.7 0.0 collective-permute-done.8.refs_1_
  15.7 1.0 %collective-permute-start.10 = (bf16[3,4,64,256]{3,2,1,0:T(8,128)(2,1)S(1)}, bf16[3,4,64,256]{3,2,1,0:T(8,128)(2,1)S(1)}, u32[]{:S(2)}, u32[]{:S(2)}) collective-permute-start(bf16[3,4,64,256]{3,2,1,0:T(8,128)(2,1)S(1)} %gather.1.refs_5_), channel_id=1, source_target_pairs={{0,4},{4,0},{8,12},{12,8},{16,20},{20,16},{24,28},{28,24},{1,5},{5... | collective-permute-start | bytes 1179656 | tf_op jit(solution)/shard_map/ppermute | solution.py:453
  16.7 0.1 collective-permute-start.5
  16.7 0.4 %collective-permute-start.6 = (f32[4,24,256]{2,1,0:T(8,128)S(1)}, f32[4,24,256]{2,1,0:T(8,128)S(1)}, u32[]{:S(2)}, u32[]{:S(2)}) collective-permute-start(f32[4,24,256]{2,1,0:T(8,128)S(1)} %get-tuple-element.37), channel_id=1, source_target_pairs={{0,4},{4,0},{8,12},{12,8},{16,20},{20,16},{24,28},{28,24},{1,5},{5... | collective-permute-start | bytes 294920 | tf_op jit(solution)/shard_map/ppermute | solution.py:453
  17.2 1.0 %collective-permute-done.5.first_ref = f32[4,24,256]{2,1,0:T(8,128)S(1)} collective-permute-done((f32[4,24,256]{2,1,0:T(8,128)S(1)}, f32[4,24,256]{2,1,0:T(8,128)S(1)}, u32[]{:S(2)}, u32[]{:S(2)}) %collective-permute-start.5) | collective-permute-done | bytes 98336 | tf_op jit(solution)/shard_map/ppermute | solution.py:453
  18.2 0.1 collective-permute-done.6.second_ref
  18.3 0.3 %join.1.refs_2_ = f32[3,8,32,256]{3,2,1,0:T(8,128)S(1)} custom-call(f32[3,8,32,256]{3,2,1,0:T(8,128)S(1)} %get-tuple-element.34.mine_ref, f32[3,2,32,256]{3,2,1,0:T(8,128)S(1)} %get-tuple-element.35.own_ref, f32[4,24,256]{2,1,0:T(8,128)S(1)} %collective-permute-done.5.first_ref, f32[4,24,256]{2,1,0:T(8,128)S(1)} %collective-permute-done.6.second_ref), custom_call_target="tpu_custom_call" | custom-call | tf_op jit(solution)/shard_map/join/pallas_call | solution.py:564
  18.6 0.0 collective-permute-done.10.refs_6_
  18.6 1.3 %prompts.1 = (f32[2,24,256]{2,1,0:T(8,128)S(1)}, f32[2,24,256]{2,1,0:T(8,128)S(1)}, f32[2,24,256]{2,1,0:T(8,128)S(1)}, f32[2,24,256]{2,1,0:T(8,128)S(1)}) custom-call(s32[24,128]{1,0:T(8,128)S(1)} %get-tuple-element.29.refs_0_, bf16[8,32,256]{2,1,0:T(8,128)(2,1)S(1)} %get-tuple-element.33.refs_1_, f32[3,8,32,256]{3,2,1,0:T(8,128)S(1)} %join.1.refs_2_, ...), custom_call_target="tpu_custom_call" | custom-call | tf_op jit(solution)/shard_map/prompts/pallas_call | solution.py:575
  19.9 2.6 %collective-permute-start.11 = (f32[2,24,256]{2,1,0:T(8,128)S(1)}, f32[2,24,256]{2,1,0:T(8,128)S(1)}, u32[]{:S(2)}, u32[]{:S(2)}) collective-permute-start(f32[2,24,256]{2,1,0:T(8,128)S(1)} %get-tuple-element.44), channel_id=1, source_target_pairs={{0,24},{4,28},{8,16},{12,20},{16,8},{20,12},{24,0},{28,4},{1,25},{... | collective-permute-start | bytes 147464 | tf_op jit(solution)/shard_map/ppermute | solution.py:456
  22.5 0.5 %collective-permute-start.12 = (f32[2,24,256]{2,1,0:T(8,128)S(1)}, f32[2,24,256]{2,1,0:T(8,128)S(1)}, u32[]{:S(2)}, u32[]{:S(2)}) collective-permute-start(f32[2,24,256]{2,1,0:T(8,128)S(1)} %get-tuple-element.45), channel_id=1, source_target_pairs={{0,16},{4,20},{8,24},{12,28},{16,0},{20,4},{24,8},{28,12},{1,17},{... | collective-permute-start | bytes 147464 | tf_op jit(solution)/shard_map/ppermute | solution.py:456
  23.0 0.4 %collective-permute-start.13 = (f32[2,24,256]{2,1,0:T(8,128)S(1)}, f32[2,24,256]{2,1,0:T(8,128)S(1)}, u32[]{:S(2)}, u32[]{:S(2)}) collective-permute-start(f32[2,24,256]{2,1,0:T(8,128)S(1)} %get-tuple-element.46), channel_id=1, source_target_pairs={{0,8},{4,12},{8,0},{12,4},{16,24},{20,28},{24,16},{28,20},{1,9},{5... | collective-permute-start | bytes 147464 | tf_op jit(solution)/shard_map/ppermute | solution.py:456
  23.5 1.5 %collective-permute-done.11.refs_1_ = f32[2,24,256]{2,1,0:T(8,128)S(1)} collective-permute-done((f32[2,24,256]{2,1,0:T(8,128)S(1)}, f32[2,24,256]{2,1,0:T(8,128)S(1)}, u32[]{:S(2)}, u32[]{:S(2)}) %collective-permute-start.11) | collective-permute-done | bytes 49184 | tf_op jit(solution)/shard_map/ppermute | solution.py:456
  25.0 1.7 %collective-permute-done.12.refs_2_ = f32[2,24,256]{2,1,0:T(8,128)S(1)} collective-permute-done((f32[2,24,256]{2,1,0:T(8,128)S(1)}, f32[2,24,256]{2,1,0:T(8,128)S(1)}, u32[]{:S(2)}, u32[]{:S(2)}) %collective-permute-start.12) | collective-permute-done | bytes 49184 | tf_op jit(solution)/shard_map/ppermute | solution.py:456
  26.6 0.5 %collective-permute-done.13.refs_3_ = f32[2,24,256]{2,1,0:T(8,128)S(1)} collective-permute-done((f32[2,24,256]{2,1,0:T(8,128)S(1)}, f32[2,24,256]{2,1,0:T(8,128)S(1)}, u32[]{:S(2)}, u32[]{:S(2)}) %collective-permute-start.13) | collective-permute-done | bytes 49184 | tf_op jit(solution)/shard_map/ppermute | solution.py:456
  27.1 1.0 %combine.1 = bf16[1,5,2,1024]{3,2,1,0:T(2,128)(2,1)} custom-call(f32[2,24,256]{2,1,0:T(8,128)S(1)} %get-tuple-element.43.refs_0_, f32[2,24,256]{2,1,0:T(8,128)S(1)} %collective-permute-done.11.refs_1_, f32[2,24,256]{2,1,0:T(8,128)S(1)} %collective-permute-done.12.refs_2_, f32[2,24,256]{2,1,0:T(8,128)S(1)} %collective-permute-done.13.refs_3_), custom_call_target="tpu_custom_call" | custom-call | tf_op jit(solution)/shard_map/combine/pallas_call | solution.py:583
  (4 shorter events, 0.0 us)
Async XLA Ops:
  1.0 5.6 %collective-permute-start = (bf16[4,64,256]{2,1,0:T(8,128)(2,1)S(1)}, bf16[4,64,256]{2,1,0:T(8,128)(2,1)S(1)}, u32[]{:S(2)}, u32[]{:S(2)}) collective-permute-start(bf16[4,64,256]{2,1,0:T(8,128)(2,1)S(1)} %get-tuple-element.39.refs_3_), channel_id=1, source_target_pairs={{0,4},{4,0},{8,12},{12,8},{16,20},{20,16},{24,28},{28,24},{1,5},{5... | collective-permute-start | bytes 393224 | tf_op jit(solution)/shard_map/ppermute | solution.py:453
  1.5 5.1 %collective-permute-start.1 = (bf16[2,24,256]{2,1,0:T(8,128)(2,1)S(1)}, bf16[2,24,256]{2,1,0:T(8,128)(2,1)S(1)}, u32[]{:S(2)}, u32[]{:S(2)}) collective-permute-start(bf16[2,24,256]{2,1,0:T(8,128)(2,1)S(1)} %get-tuple-element.26.own_ref), channel_id=1, source_target_pairs={{0,4},{4,0},{8,12},{12,8},{16,20},{20,16},{24,28},{28,24},{1,5},{5... | collective-permute-start | bytes 73736 | tf_op jit(solution)/shard_map/ppermute | solution.py:453
  1.6 14.0 %collective-permute-start.7 = (bf16[4,64,256]{2,1,0:T(8,128)(2,1)S(1)}, bf16[4,64,256]{2,1,0:T(8,128)(2,1)S(1)}, u32[]{:S(2)}, u32[]{:S(2)}) collective-permute-start(bf16[4,64,256]{2,1,0:T(8,128)(2,1)S(1)} %get-tuple-element.39.refs_3_), channel_id=1, source_target_pairs={{0,3},{1,2},{2,1},{3,0},{4,6},{5,7},{6,4},{7,5},{8,11},{9,10},{10,... | collective-permute-start | bytes 393224 | tf_op jit(solution)/shard_map/ppermute | solution.py:463
  6.7 9.0 %collective-permute-start.8 = (bf16[4,64,256]{2,1,0:T(8,128)(2,1)S(1)}, bf16[4,64,256]{2,1,0:T(8,128)(2,1)S(1)}, u32[]{:S(2)}, u32[]{:S(2)}) collective-permute-start(bf16[4,64,256]{2,1,0:T(8,128)(2,1)S(1)} %collective-permute-done.refs_4_), channel_id=1, source_target_pairs={{0,3},{1,2},{2,1},{3,0},{4,6},{5,7},{6,4},{7,5},{8,11},{9,10},{10,... | collective-permute-start | bytes 393224 | tf_op jit(solution)/shard_map/ppermute | solution.py:463
  7.5 8.1 %collective-permute-start.9 = (bf16[4,64,256]{2,1,0:T(8,128)(2,1)S(1)}, bf16[4,64,256]{2,1,0:T(8,128)(2,1)S(1)}, u32[]{:S(2)}, u32[]{:S(2)}) collective-permute-start(bf16[4,64,256]{2,1,0:T(8,128)(2,1)S(1)} %get-tuple-element.39.refs_3_), channel_id=1, source_target_pairs={{0,1},{1,0},{2,3},{3,2},{4,5},{5,4},{6,7},{7,6},{8,9},{9,8},{10,11... | collective-permute-start | bytes 393224 | tf_op jit(solution)/shard_map/ppermute | solution.py:463
  7.5 5.1 %collective-permute-start.2 = (bf16[4,24,256]{2,1,0:T(8,128)(2,1)S(1)}, bf16[4,24,256]{2,1,0:T(8,128)(2,1)S(1)}, u32[]{:S(2)}, u32[]{:S(2)}) collective-permute-start(bf16[4,24,256]{2,1,0:T(8,128)(2,1)S(1)} %pair.1.refs_10_.refs_1_), channel_id=1, source_target_pairs={{0,8},{4,20},{8,0},{12,28},{16,24},{20,4},{24,16},{28,12},{1,9},{5... | collective-permute-start | bytes 147464 | tf_op jit(solution)/shard_map/ppermute | solution.py:540
  9.1 5.0 %collective-permute-start.4 = (bf16[4,24,256]{2,1,0:T(8,128)(2,1)S(1)}, bf16[4,24,256]{2,1,0:T(8,128)(2,1)S(1)}, u32[]{:S(2)}, u32[]{:S(2)}) collective-permute-start(bf16[4,24,256]{2,1,0:T(8,128)(2,1)S(1)} %pair.1.refs_10_.refs_1_), channel_id=1, source_target_pairs={{0,24},{4,28},{8,16},{12,20},{16,8},{20,12},{24,0},{28,4},{1,25},{... | collective-permute-start | bytes 147464 | tf_op jit(solution)/shard_map/ppermute | solution.py:456
  12.7 1.4 %collective-permute-start.3 = (bf16[4,24,256]{2,1,0:T(8,128)(2,1)S(1)}, bf16[4,24,256]{2,1,0:T(8,128)(2,1)S(1)}, u32[]{:S(2)}, u32[]{:S(2)}) collective-permute-start(bf16[4,24,256]{2,1,0:T(8,128)(2,1)S(1)} %collective-permute-done.2.refs_2_), channel_id=1, source_target_pairs={{0,4},{4,0},{8,12},{12,8},{16,20},{20,16},{24,28},{28,24},{1,5},{5... | collective-permute-start | bytes 147464 | tf_op jit(solution)/shard_map/ppermute | solution.py:453
  15.7 2.9 %collective-permute-start.10 = (bf16[3,4,64,256]{3,2,1,0:T(8,128)(2,1)S(1)}, bf16[3,4,64,256]{3,2,1,0:T(8,128)(2,1)S(1)}, u32[]{:S(2)}, u32[]{:S(2)}) collective-permute-start(bf16[3,4,64,256]{3,2,1,0:T(8,128)(2,1)S(1)} %gather.1.refs_5_), channel_id=1, source_target_pairs={{0,4},{4,0},{8,12},{12,8},{16,20},{20,16},{24,28},{28,24},{1,5},{5... | collective-permute-start | bytes 1179656 | tf_op jit(solution)/shard_map/ppermute | solution.py:453
  16.7 1.5 %collective-permute-start.5 = (f32[4,24,256]{2,1,0:T(8,128)S(1)}, f32[4,24,256]{2,1,0:T(8,128)S(1)}, u32[]{:S(2)}, u32[]{:S(2)}) collective-permute-start(f32[4,24,256]{2,1,0:T(8,128)S(1)} %get-tuple-element.36), channel_id=1, source_target_pairs={{0,4},{4,0},{8,12},{12,8},{16,20},{20,16},{24,28},{28,24},{1,5},{5... | collective-permute-start | bytes 294920 | tf_op jit(solution)/shard_map/ppermute | solution.py:453
  16.7 1.6 %collective-permute-start.6 = (f32[4,24,256]{2,1,0:T(8,128)S(1)}, f32[4,24,256]{2,1,0:T(8,128)S(1)}, u32[]{:S(2)}, u32[]{:S(2)}) collective-permute-start(f32[4,24,256]{2,1,0:T(8,128)S(1)} %get-tuple-element.37), channel_id=1, source_target_pairs={{0,4},{4,0},{8,12},{12,8},{16,20},{20,16},{24,28},{28,24},{1,5},{5... | collective-permute-start | bytes 294920 | tf_op jit(solution)/shard_map/ppermute | solution.py:453
  19.9 5.1 %collective-permute-start.11 = (f32[2,24,256]{2,1,0:T(8,128)S(1)}, f32[2,24,256]{2,1,0:T(8,128)S(1)}, u32[]{:S(2)}, u32[]{:S(2)}) collective-permute-start(f32[2,24,256]{2,1,0:T(8,128)S(1)} %get-tuple-element.44), channel_id=1, source_target_pairs={{0,24},{4,28},{8,16},{12,20},{16,8},{20,12},{24,0},{28,4},{1,25},{... | collective-permute-start | bytes 147464 | tf_op jit(solution)/shard_map/ppermute | solution.py:456
  22.5 4.1 %collective-permute-start.12 = (f32[2,24,256]{2,1,0:T(8,128)S(1)}, f32[2,24,256]{2,1,0:T(8,128)S(1)}, u32[]{:S(2)}, u32[]{:S(2)}) collective-permute-start(f32[2,24,256]{2,1,0:T(8,128)S(1)} %get-tuple-element.45), channel_id=1, source_target_pairs={{0,16},{4,20},{8,24},{12,28},{16,0},{20,4},{24,8},{28,12},{1,17},{... | collective-permute-start | bytes 147464 | tf_op jit(solution)/shard_map/ppermute | solution.py:456
  23.0 4.1 %collective-permute-start.13 = (f32[2,24,256]{2,1,0:T(8,128)S(1)}, f32[2,24,256]{2,1,0:T(8,128)S(1)}, u32[]{:S(2)}, u32[]{:S(2)}) collective-permute-start(f32[2,24,256]{2,1,0:T(8,128)S(1)} %get-tuple-element.46), channel_id=1, source_target_pairs={{0,8},{4,12},{8,0},{12,4},{16,24},{20,28},{24,16},{28,20},{1,9},{5... | collective-permute-start | bytes 147464 | tf_op jit(solution)/shard_map/ppermute | solution.py:456

commit v7 on v6

--- a/solution.py
+++ b/solution.py
@@ -498,7 +498,7 @@
     fetched = []
     for s in range(2, shifts, 2):
         fetched += [along_req(x, s + 1, s) for x in (own_blocks, sibling_blocks)]
-    fetched.append(along_req(later_blocks, 1, 1))
+    fetched.append(along_req(own_blocks, 1, 1))
     chip_queries = call(
         pair_kernel, "pair", shape((2 * each, MESSAGE, WIDTH), BF16), [VMEM] * 2
     )(own_queries, sibling_queries)

time: 28.3 us -> 28.3 us (level)
  waiting for transfers between devices: 6.14 us -> 6.72 us
  starting transfers between devices: 14.6 us -> 14.1 us
    ppermute x3, waiting for transfers between devices: 0.01 us -> 0.58 us  [along_req(): return lax.ppermute(x, ('blk', 'req'), pairs)]
    ppermute x6, starting transfers between devices: 2.13 us -> 1.6 us  [other_core(): return lax.ppermute(x, 'blk', [(i, i ^ 1) for i in range(devices)])]
  transfers between devices with their start and end apart: 14 -> 14, of which waited for: 6 -> 7; matrix products, arithmetic and copies ran while one was open for 0% -> 0% of each run, Pallas kernels for 14% -> 14%
where the time goes in v7:
time: 28.3 us; the launch traced here: 28.1 us
  starting transfers between devices  14.1 us (50%)
  Pallas kernels  7.25 us (26%)
  waiting for transfers between devices  6.72 us (24%)
    ppermute x3, starting transfers between devices, along_req(): return lax.ppermute(x, ('blk', 'req'), pairs)  5.93 us
    ppermute x4, starting transfers between devices, other_chip(): return lax.ppermute(x, 'blk', [(i, i ^ 2 * s) for i in range(devices)])  5.06 us
    ppermute x4, waiting for transfers between devices, other_chip(): return lax.ppermute(x, 'blk', [(i, i ^ 2 * s) for i in range(devices)])  4.99 us
    pallas_call x1, Pallas kernels, per_device(): call(functools.partial(own_kernel, chips, each, shifts, held), 'own', [sh...  2.06 us
    ppermute x6, starting transfers between devices, other_core(): return lax.ppermute(x, 'blk', [(i, i ^ 1) for i in range(devices)])  1.6 us
    pallas_call x1, Pallas kernels, per_device(): call(functools.partial(pieces_kernel, chips, each), 'pieces', [shape((3,)...  1.55 us
    ppermute x1, starting transfers between devices, per_device(): lax.ppermute(chip_queries, 'blk', [(i, i ^ 2 * (across_cores(s, chips) if...  1.49 us
    pallas_call x1, Pallas kernels, per_device(): call(functools.partial(prompts_kernel, chips, each, 2 * pieces), 'prompts...  1.27 us
  transfers between devices with their start and end apart: 14, of which 7 were waited for; matrix products, arithmetic and copies ran while one was open for 0% of the time, Pallas kernels for 14%

profile of v7, /device:TPU:0, one launch (start us, length us, event | category | flops | bytes accessed | tf_op | source)
XLA Modules:
  0.0 28.1 jit_solution(13816774370219525676)
XLA Ops:
  0.0 1.0 %parcel.1 = (bf16[4,64,256]{2,1,0:T(8,128)(2,1)S(1)}, bf16[2,24,256]{2,1,0:T(8,128)(2,1)S(1)}) custom-call(s32[1,4]{1,0:T(1,128)} %bitcast.12, bf16[4,32,256]{2,1,0:T(8,128)(2,1)} %keys_hbm.1, bf16[4,32,256]{2,1,0:T(8,128)(2,1)} %values_hbm.1, bf16[1,5,2,1024]{3,2,1,0:T(2,128)(2,1)} %bitcast.7), custom_call_target="tpu_custom_call" | custom-call | tf_op jit(solution)/shard_map/parcel/pallas_call | solution.py:475
  1.0 0.5 %collective-permute-start = (bf16[4,64,256]{2,1,0:T(8,128)(2,1)S(1)}, bf16[4,64,256]{2,1,0:T(8,128)(2,1)S(1)}, u32[]{:S(2)}, u32[]{:S(2)}) collective-permute-start(bf16[4,64,256]{2,1,0:T(8,128)(2,1)S(1)} %get-tuple-element.26.refs_3_), channel_id=1, source_target_pairs={{0,4},{4,0},{8,12},{12,8},{16,20},{20,16},{24,28},{28,24},{1,5},{5... | collective-permute-start | bytes 393224 | tf_op jit(solution)/shard_map/ppermute | solution.py:453
  1.5 0.1 collective-permute-start.1
  1.6 5.0 %collective-permute-start.7 = (bf16[4,64,256]{2,1,0:T(8,128)(2,1)S(1)}, bf16[4,64,256]{2,1,0:T(8,128)(2,1)S(1)}, u32[]{:S(2)}, u32[]{:S(2)}) collective-permute-start(bf16[4,64,256]{2,1,0:T(8,128)(2,1)S(1)} %get-tuple-element.26.refs_3_), channel_id=1, source_target_pairs={{0,3},{1,2},{2,1},{3,0},{4,6},{5,7},{6,4},{7,5},{8,11},{9,10},{10,... | collective-permute-start | bytes 393224 | tf_op jit(solution)/shard_map/ppermute | solution.py:463
  6.7 0.0 collective-permute-start.9
  6.7 0.0 collective-permute-done.1.sibling_ref
  6.7 0.0 collective-permute-done.refs_4_
  6.7 0.9 %collective-permute-start.8 = (bf16[4,64,256]{2,1,0:T(8,128)(2,1)S(1)}, bf16[4,64,256]{2,1,0:T(8,128)(2,1)S(1)}, u32[]{:S(2)}, u32[]{:S(2)}) collective-permute-start(bf16[4,64,256]{2,1,0:T(8,128)(2,1)S(1)} %collective-permute-done.refs_4_), channel_id=1, source_target_pairs={{0,3},{1,2},{2,1},{3,0},{4,6},{5,7},{6,4},{7,5},{8,11},{9,10},{10,... | collective-permute-start | bytes 393224 | tf_op jit(solution)/shard_map/ppermute | solution.py:463
  7.6 1.5 %collective-permute-start.2 = (bf16[4,24,256]{2,1,0:T(8,128)(2,1)S(1)}, bf16[4,24,256]{2,1,0:T(8,128)(2,1)S(1)}, u32[]{:S(2)}, u32[]{:S(2)}) collective-permute-start(bf16[4,24,256]{2,1,0:T(8,128)(2,1)S(1)} %pair.1.refs_10_.refs_1_), channel_id=1, source_target_pairs={{0,8},{4,20},{8,0},{12,28},{16,24},{20,4},{24,16},{28,12},{1,9},{5... | collective-permute-start | bytes 147464 | tf_op jit(solution)/shard_map/ppermute | solution.py:540
  9.1 1.5 %collective-permute-start.4 = (bf16[4,24,256]{2,1,0:T(8,128)(2,1)S(1)}, bf16[4,24,256]{2,1,0:T(8,128)(2,1)S(1)}, u32[]{:S(2)}, u32[]{:S(2)}) collective-permute-start(bf16[4,24,256]{2,1,0:T(8,128)(2,1)S(1)} %pair.1.refs_10_.refs_1_), channel_id=1, source_target_pairs={{0,24},{4,28},{8,16},{12,20},{16,8},{20,12},{24,0},{28,4},{1,25},{... | collective-permute-start | bytes 147464 | tf_op jit(solution)/shard_map/ppermute | solution.py:456
  10.5 2.1 %own.1 = (f32[3,2,32,256]{3,2,1,0:T(8,128)S(1)}, s32[24,128]{1,0:T(8,128)S(1)}, bf16[8,256,256]{2,1,0:T(8,128)(2,1)S(1)}, bf16[8,256,256]{2,1,0:T(8,128)(2,1)S(1)}) custom-call(s32[1,64]{1,0:T(1,128)} %refs_0_.1, s32[1,16]{1,0:T(1,128)} %refs_1_.1, s32[1,2]{1,0:T(1,128)} %refs_2_.1, s32[1,16]{1,0:T(1,128)} %refs_3_.1, bf16[1,5,2,256]{3,2,1,0:T(2,128)(2,1)} %bitcast.8, ...), custom_call_target="tpu_custom_call" | custom-call | bytes 8388608 | tf_op jit(solution)/shard_map/own/pallas_call | solution.py:506
  12.6 0.0 collective-permute-done.2.refs_2_
  12.6 0.1 collective-permute-start.3
  12.7 1.3 %collective-permute-done.4.refs_4_ = bf16[4,24,256]{2,1,0:T(8,128)(2,1)S(1)} collective-permute-done((bf16[4,24,256]{2,1,0:T(8,128)(2,1)S(1)}, bf16[4,24,256]{2,1,0:T(8,128)(2,1)S(1)}, u32[]{:S(2)}, u32[]{:S(2)}) %collective-permute-start.4) | collective-permute-done | bytes 49184 | tf_op jit(solution)/shard_map/ppermute | solution.py:456
  14.1 1.6 %pieces.1 = (f32[3,8,32,256]{3,2,1,0:T(8,128)S(1)}, f32[4,24,256]{2,1,0:T(8,128)S(1)}, f32[4,24,256]{2,1,0:T(8,128)S(1)}, bf16[8,32,256]{2,1,0:T(8,128)(2,1)S(1)}) custom-call(s32[24,128]{1,0:T(8,128)S(1)} %get-tuple-element.28.refs_0_, bf16[4,24,256]{2,1,0:T(8,128)(2,1)S(1)} %pair.1.refs_10_.refs_1_, ...), custom_call_target="tpu_custom_call" | custom-call | tf_op jit(solution)/shard_map/pieces/pallas_call | solution.py:551
  15.6 0.0 collective-permute-done.7.refs_0_
  15.6 0.6 %collective-permute-done.8.refs_1_ = bf16[4,64,256]{2,1,0:T(8,128)(2,1)S(1)} collective-permute-done((bf16[4,64,256]{2,1,0:T(8,128)(2,1)S(1)}, bf16[4,64,256]{2,1,0:T(8,128)(2,1)S(1)}, u32[]{:S(2)}, u32[]{:S(2)}) %collective-permute-start.8) | collective-permute-done | bytes 131104 | tf_op jit(solution)/shard_map/ppermute | solution.py:463
  16.2 0.4 %collective-permute-start.10 = (bf16[3,4,64,256]{3,2,1,0:T(8,128)(2,1)S(1)}, bf16[3,4,64,256]{3,2,1,0:T(8,128)(2,1)S(1)}, u32[]{:S(2)}, u32[]{:S(2)}) collective-permute-start(bf16[3,4,64,256]{3,2,1,0:T(8,128)(2,1)S(1)} %gather.1.refs_5_), channel_id=1, source_target_pairs={{0,4},{4,0},{8,12},{12,8},{16,20},{20,16},{24,28},{28,24},{1,5},{5... | collective-permute-start | bytes 1179656 | tf_op jit(solution)/shard_map/ppermute | solution.py:453
  16.7 0.2 collective-permute-start.5
  16.8 0.4 %collective-permute-start.6 = (f32[4,24,256]{2,1,0:T(8,128)S(1)}, f32[4,24,256]{2,1,0:T(8,128)S(1)}, u32[]{:S(2)}, u32[]{:S(2)}) collective-permute-start(f32[4,24,256]{2,1,0:T(8,128)S(1)} %get-tuple-element.36), channel_id=1, source_target_pairs={{0,4},{4,0},{8,12},{12,8},{16,20},{20,16},{24,28},{28,24},{1,5},{5... | collective-permute-start | bytes 294920 | tf_op jit(solution)/shard_map/ppermute | solution.py:453
  17.2 1.0 %collective-permute-done.5.first_ref = f32[4,24,256]{2,1,0:T(8,128)S(1)} collective-permute-done((f32[4,24,256]{2,1,0:T(8,128)S(1)}, f32[4,24,256]{2,1,0:T(8,128)S(1)}, u32[]{:S(2)}, u32[]{:S(2)}) %collective-permute-start.5) | collective-permute-done | bytes 98336 | tf_op jit(solution)/shard_map/ppermute | solution.py:453
  18.2 0.1 collective-permute-done.6.second_ref
  18.3 0.3 %join.1.refs_2_ = f32[3,8,32,256]{3,2,1,0:T(8,128)S(1)} custom-call(f32[3,8,32,256]{3,2,1,0:T(8,128)S(1)} %get-tuple-element.33.mine_ref, f32[3,2,32,256]{3,2,1,0:T(8,128)S(1)} %get-tuple-element.34.own_ref, f32[4,24,256]{2,1,0:T(8,128)S(1)} %collective-permute-done.5.first_ref, f32[4,24,256]{2,1,0:T(8,128)S(1)} %collective-permute-done.6.second_ref), custom_call_target="tpu_custom_call" | custom-call | tf_op jit(solution)/shard_map/join/pallas_call | solution.py:564
  18.6 0.0 collective-permute-done.10.refs_6_
  18.6 1.3 %prompts.1 = (f32[2,24,256]{2,1,0:T(8,128)S(1)}, f32[2,24,256]{2,1,0:T(8,128)S(1)}, f32[2,24,256]{2,1,0:T(8,128)S(1)}, f32[2,24,256]{2,1,0:T(8,128)S(1)}) custom-call(s32[24,128]{1,0:T(8,128)S(1)} %get-tuple-element.28.refs_0_, bf16[8,32,256]{2,1,0:T(8,128)(2,1)S(1)} %get-tuple-element.32.refs_1_, f32[3,8,32,256]{3,2,1,0:T(8,128)S(1)} %join.1.refs_2_, ...), custom_call_target="tpu_custom_call" | custom-call | tf_op jit(solution)/shard_map/prompts/pallas_call | solution.py:575
  19.9 2.6 %collective-permute-start.11 = (f32[2,24,256]{2,1,0:T(8,128)S(1)}, f32[2,24,256]{2,1,0:T(8,128)S(1)}, u32[]{:S(2)}, u32[]{:S(2)}) collective-permute-start(f32[2,24,256]{2,1,0:T(8,128)S(1)} %get-tuple-element.42), channel_id=1, source_target_pairs={{0,24},{4,28},{8,16},{12,20},{16,8},{20,12},{24,0},{28,4},{1,25},{... | collective-permute-start | bytes 147464 | tf_op jit(solution)/shard_map/ppermute | solution.py:456
  22.5 0.5 %collective-permute-start.12 = (f32[2,24,256]{2,1,0:T(8,128)S(1)}, f32[2,24,256]{2,1,0:T(8,128)S(1)}, u32[]{:S(2)}, u32[]{:S(2)}) collective-permute-start(f32[2,24,256]{2,1,0:T(8,128)S(1)} %get-tuple-element.43), channel_id=1, source_target_pairs={{0,16},{4,20},{8,24},{12,28},{16,0},{20,4},{24,8},{28,12},{1,17},{... | collective-permute-start | bytes 147464 | tf_op jit(solution)/shard_map/ppermute | solution.py:456
  23.0 0.4 %collective-permute-start.13 = (f32[2,24,256]{2,1,0:T(8,128)S(1)}, f32[2,24,256]{2,1,0:T(8,128)S(1)}, u32[]{:S(2)}, u32[]{:S(2)}) collective-permute-start(f32[2,24,256]{2,1,0:T(8,128)S(1)} %get-tuple-element.44), channel_id=1, source_target_pairs={{0,8},{4,12},{8,0},{12,4},{16,24},{20,28},{24,16},{28,20},{1,9},{5... | collective-permute-start | bytes 147464 | tf_op jit(solution)/shard_map/ppermute | solution.py:456
  23.5 1.5 %collective-permute-done.11.refs_1_ = f32[2,24,256]{2,1,0:T(8,128)S(1)} collective-permute-done((f32[2,24,256]{2,1,0:T(8,128)S(1)}, f32[2,24,256]{2,1,0:T(8,128)S(1)}, u32[]{:S(2)}, u32[]{:S(2)}) %collective-permute-start.11) | collective-permute-done | bytes 49184 | tf_op jit(solution)/shard_map/ppermute | solution.py:456
  25.0 1.6 %collective-permute-done.12.refs_2_ = f32[2,24,256]{2,1,0:T(8,128)S(1)} collective-permute-done((f32[2,24,256]{2,1,0:T(8,128)S(1)}, f32[2,24,256]{2,1,0:T(8,128)S(1)}, u32[]{:S(2)}, u32[]{:S(2)}) %collective-permute-start.12) | collective-permute-done | bytes 49184 | tf_op jit(solution)/shard_map/ppermute | solution.py:456
  26.6 0.5 %collective-permute-done.13.refs_3_ = f32[2,24,256]{2,1,0:T(8,128)S(1)} collective-permute-done((f32[2,24,256]{2,1,0:T(8,128)S(1)}, f32[2,24,256]{2,1,0:T(8,128)S(1)}, u32[]{:S(2)}, u32[]{:S(2)}) %collective-permute-start.13) | collective-permute-done | bytes 49184 | tf_op jit(solution)/shard_map/ppermute | solution.py:456
  27.1 1.0 %combine.1 = bf16[1,5,2,1024]{3,2,1,0:T(2,128)(2,1)} custom-call(f32[2,24,256]{2,1,0:T(8,128)S(1)} %get-tuple-element.41.refs_0_, f32[2,24,256]{2,1,0:T(8,128)S(1)} %collective-permute-done.11.refs_1_, f32[2,24,256]{2,1,0:T(8,128)S(1)} %collective-permute-done.12.refs_2_, f32[2,24,256]{2,1,0:T(8,128)S(1)} %collective-permute-done.13.refs_3_), custom_call_target="tpu_custom_call" | custom-call | tf_op jit(solution)/shard_map/combine/pallas_call | solution.py:583
  (4 shorter events, 0.0 us)
Async XLA Ops:
  1.0 5.6 %collective-permute-start = (bf16[4,64,256]{2,1,0:T(8,128)(2,1)S(1)}, bf16[4,64,256]{2,1,0:T(8,128)(2,1)S(1)}, u32[]{:S(2)}, u32[]{:S(2)}) collective-permute-start(bf16[4,64,256]{2,1,0:T(8,128)(2,1)S(1)} %get-tuple-element.26.refs_3_), channel_id=1, source_target_pairs={{0,4},{4,0},{8,12},{12,8},{16,20},{20,16},{24,28},{28,24},{1,5},{5... | collective-permute-start | bytes 393224 | tf_op jit(solution)/shard_map/ppermute | solution.py:453
  1.5 5.1 %collective-permute-start.1 = (bf16[2,24,256]{2,1,0:T(8,128)(2,1)S(1)}, bf16[2,24,256]{2,1,0:T(8,128)(2,1)S(1)}, u32[]{:S(2)}, u32[]{:S(2)}) collective-permute-start(bf16[2,24,256]{2,1,0:T(8,128)(2,1)S(1)} %get-tuple-element.25.own_ref), channel_id=1, source_target_pairs={{0,4},{4,0},{8,12},{12,8},{16,20},{20,16},{24,28},{28,24},{1,5},{5... | collective-permute-start | bytes 73736 | tf_op jit(solution)/shard_map/ppermute | solution.py:453
  1.6 14.0 %collective-permute-start.7 = (bf16[4,64,256]{2,1,0:T(8,128)(2,1)S(1)}, bf16[4,64,256]{2,1,0:T(8,128)(2,1)S(1)}, u32[]{:S(2)}, u32[]{:S(2)}) collective-permute-start(bf16[4,64,256]{2,1,0:T(8,128)(2,1)S(1)} %get-tuple-element.26.refs_3_), channel_id=1, source_target_pairs={{0,3},{1,2},{2,1},{3,0},{4,6},{5,7},{6,4},{7,5},{8,11},{9,10},{10,... | collective-permute-start | bytes 393224 | tf_op jit(solution)/shard_map/ppermute | solution.py:463
  6.7 9.0 %collective-permute-start.9 = (bf16[4,64,256]{2,1,0:T(8,128)(2,1)S(1)}, bf16[4,64,256]{2,1,0:T(8,128)(2,1)S(1)}, u32[]{:S(2)}, u32[]{:S(2)}) collective-permute-start(bf16[4,64,256]{2,1,0:T(8,128)(2,1)S(1)} %get-tuple-element.26.refs_3_), channel_id=1, source_target_pairs={{0,1},{1,0},{2,3},{3,2},{4,5},{5,4},{6,7},{7,6},{8,9},{9,8},{10,11... | collective-permute-start | bytes 393224 | tf_op jit(solution)/shard_map/ppermute | solution.py:463
  6.7 9.5 %collective-permute-start.8 = (bf16[4,64,256]{2,1,0:T(8,128)(2,1)S(1)}, bf16[4,64,256]{2,1,0:T(8,128)(2,1)S(1)}, u32[]{:S(2)}, u32[]{:S(2)}) collective-permute-start(bf16[4,64,256]{2,1,0:T(8,128)(2,1)S(1)} %collective-permute-done.refs_4_), channel_id=1, source_target_pairs={{0,3},{1,2},{2,1},{3,0},{4,6},{5,7},{6,4},{7,5},{8,11},{9,10},{10,... | collective-permute-start | bytes 393224 | tf_op jit(solution)/shard_map/ppermute | solution.py:463
  7.6 5.1 %collective-permute-start.2 = (bf16[4,24,256]{2,1,0:T(8,128)(2,1)S(1)}, bf16[4,24,256]{2,1,0:T(8,128)(2,1)S(1)}, u32[]{:S(2)}, u32[]{:S(2)}) collective-permute-start(bf16[4,24,256]{2,1,0:T(8,128)(2,1)S(1)} %pair.1.refs_10_.refs_1_), channel_id=1, source_target_pairs={{0,8},{4,20},{8,0},{12,28},{16,24},{20,4},{24,16},{28,12},{1,9},{5... | collective-permute-start | bytes 147464 | tf_op jit(solution)/shard_map/ppermute | solution.py:540
  9.1 5.0 %collective-permute-start.4 = (bf16[4,24,256]{2,1,0:T(8,128)(2,1)S(1)}, bf16[4,24,256]{2,1,0:T(8,128)(2,1)S(1)}, u32[]{:S(2)}, u32[]{:S(2)}) collective-permute-start(bf16[4,24,256]{2,1,0:T(8,128)(2,1)S(1)} %pair.1.refs_10_.refs_1_), channel_id=1, source_target_pairs={{0,24},{4,28},{8,16},{12,20},{16,8},{20,12},{24,0},{28,4},{1,25},{... | collective-permute-start | bytes 147464 | tf_op jit(solution)/shard_map/ppermute | solution.py:456
  12.6 1.4 %collective-permute-start.3 = (bf16[4,24,256]{2,1,0:T(8,128)(2,1)S(1)}, bf16[4,24,256]{2,1,0:T(8,128)(2,1)S(1)}, u32[]{:S(2)}, u32[]{:S(2)}) collective-permute-start(bf16[4,24,256]{2,1,0:T(8,128)(2,1)S(1)} %collective-permute-done.2.refs_2_), channel_id=1, source_target_pairs={{0,4},{4,0},{8,12},{12,8},{16,20},{20,16},{24,28},{28,24},{1,5},{5... | collective-permute-start | bytes 147464 | tf_op jit(solution)/shard_map/ppermute | solution.py:453
  16.2 2.4 %collective-permute-start.10 = (bf16[3,4,64,256]{3,2,1,0:T(8,128)(2,1)S(1)}, bf16[3,4,64,256]{3,2,1,0:T(8,128)(2,1)S(1)}, u32[]{:S(2)}, u32[]{:S(2)}) collective-permute-start(bf16[3,4,64,256]{3,2,1,0:T(8,128)(2,1)S(1)} %gather.1.refs_5_), channel_id=1, source_target_pairs={{0,4},{4,0},{8,12},{12,8},{16,20},{20,16},{24,28},{28,24},{1,5},{5... | collective-permute-start | bytes 1179656 | tf_op jit(solution)/shard_map/ppermute | solution.py:453
  16.7 1.5 %collective-permute-start.5 = (f32[4,24,256]{2,1,0:T(8,128)S(1)}, f32[4,24,256]{2,1,0:T(8,128)S(1)}, u32[]{:S(2)}, u32[]{:S(2)}) collective-permute-start(f32[4,24,256]{2,1,0:T(8,128)S(1)} %get-tuple-element.35), channel_id=1, source_target_pairs={{0,4},{4,0},{8,12},{12,8},{16,20},{20,16},{24,28},{28,24},{1,5},{5... | collective-permute-start | bytes 294920 | tf_op jit(solution)/shard_map/ppermute | solution.py:453
  16.8 1.5 %collective-permute-start.6 = (f32[4,24,256]{2,1,0:T(8,128)S(1)}, f32[4,24,256]{2,1,0:T(8,128)S(1)}, u32[]{:S(2)}, u32[]{:S(2)}) collective-permute-start(f32[4,24,256]{2,1,0:T(8,128)S(1)} %get-tuple-element.36), channel_id=1, source_target_pairs={{0,4},{4,0},{8,12},{12,8},{16,20},{20,16},{24,28},{28,24},{1,5},{5... | collective-permute-start | bytes 294920 | tf_op jit(solution)/shard_map/ppermute | solution.py:453
  19.9 5.1 %collective-permute-start.11 = (f32[2,24,256]{2,1,0:T(8,128)S(1)}, f32[2,24,256]{2,1,0:T(8,128)S(1)}, u32[]{:S(2)}, u32[]{:S(2)}) collective-permute-start(f32[2,24,256]{2,1,0:T(8,128)S(1)} %get-tuple-element.42), channel_id=1, source_target_pairs={{0,24},{4,28},{8,16},{12,20},{16,8},{20,12},{24,0},{28,4},{1,25},{... | collective-permute-start | bytes 147464 | tf_op jit(solution)/shard_map/ppermute | solution.py:456
  22.5 4.1 %collective-permute-start.12 = (f32[2,24,256]{2,1,0:T(8,128)S(1)}, f32[2,24,256]{2,1,0:T(8,128)S(1)}, u32[]{:S(2)}, u32[]{:S(2)}) collective-permute-start(f32[2,24,256]{2,1,0:T(8,128)S(1)} %get-tuple-element.43), channel_id=1, source_target_pairs={{0,16},{4,20},{8,24},{12,28},{16,0},{20,4},{24,8},{28,12},{1,17},{... | collective-permute-start | bytes 147464 | tf_op jit(solution)/shard_map/ppermute | solution.py:456
  23.0 4.1 %collective-permute-start.13 = (f32[2,24,256]{2,1,0:T(8,128)S(1)}, f32[2,24,256]{2,1,0:T(8,128)S(1)}, u32[]{:S(2)}, u32[]{:S(2)}) collective-permute-start(f32[2,24,256]{2,1,0:T(8,128)S(1)} %get-tuple-element.44), channel_id=1, source_target_pairs={{0,8},{4,12},{8,0},{12,4},{16,24},{20,28},{24,16},{28,20},{1,9},{5... | collective-permute-start | bytes 147464 | tf_op jit(solution)/shard_map/ppermute | solution.py:456
